TPU v7x, 32 devices: a whole 2x2x4 slice. The times are simulated.
32 devices in a mesh: req: 4 (over y, x), hid: 8 (over z, core).
Axes of the slice: x: 2, y: 2, z: 4, core: 2. Of those that a mesh axis runs over, the one named last changes fastest.
Arguments:
- patches: bfloat16 [4096, 1408], P('req'), may hold values from -6 to 6
- segments: int32 [4096], P('req'), may hold values from 0 to 31, as said below
- grid_sizes: int32 [32, 2], replicated, may hold values from 0 to 32, as said below
- owners: int32 [32], replicated, may hold values from 0 to 3, as said below
- row_table: bfloat16 [32, 1408], replicated, may hold values from -3 to 3
- col_table: bfloat16 [32, 1408], replicated, may hold values from -3 to 3
- gain_attn: float32 [1408], replicated, may hold values from 0.1 to 1.9
- qkv_weight: bfloat16 [3, 1408, 1408], P(None, None, 'hid')
- out_weight: bfloat16 [1408, 1408], replicated, may hold values from -0.15625 to 0.15625
- gain_mlp: float32 [1408], replicated, may hold values from 0.1 to 1.9
- up_weight: bfloat16 [1408, 6144], P(None, 'hid'), may hold values from -0.15625 to 0.15625
- down_weight: bfloat16 [6144, 1408], P('hid'), may hold values from -0.078125 to 0.078125
- merge_weight: bfloat16 [5632, 4096], P(None, 'hid'), may hold values from -0.078125 to 0.078125
Outputs:
- returned: bfloat16 [4, 256, 4096], P('req', None, 'hid')
Inputs may be any that keep to these rules, and one draw needn't show every extreme that they name: `grid_sizes`: row r holds request r's patch grid as (height, width); both are even; a request of height 0 holds no patches, and the first and the last request are never of height 0; every width is 32, 16 or 8. `owners`: every owner appears in exactly 8 entries, and its requests hold exactly 256 2x2 cells together. segments[p] is the request holding patch p: the requests' patches lie end to end in table order, each image as 2x2 cells of four consecutive patches (top left, top right, bottom left, bottom right), cells in row-major order.
All inputs are finite; a program needn't handle non-finite values.
Results may differ from a plain program's by a relative error of at most 0.018.
Values may be sent and summed in bfloat16 or wider, within the bound.
No kernel may reach another device: no remote copies, remote signals or barrier semaphores. Data moves between devices by JAX's collectives and lax.ppermute only.
A program may use at most 128 MiB of HBM per device.

v0:
```python
import math

import jax
import jax.numpy as jnp
from jax import lax
from jax.sharding import PartitionSpec as P

HEAD_DIM = 88


def from_behind(value, axis, steps):
    count = lax.axis_size(axis)
    first, last = (max(0, -steps), min(count, count - steps))
    return lax.ppermute(value, axis, [(source, source + steps) for source in range(first, last)])


def layer_norm(values, gain_row):
    widened = values.astype(jnp.float32)
    centered = widened - jnp.mean(widened, axis=-1, keepdims=True)
    variance = jnp.mean(centered * centered, axis=-1, keepdims=True)
    return centered * lax.rsqrt(variance + 1e-06) * gain_row


def request_tables(grid_sizes, owners):
    cell_count = grid_sizes[:, 0] // 2 * (grid_sizes[:, 1] // 2)
    cell_end = jnp.cumsum(cell_count)
    cell_start = cell_end - cell_count
    ordinal = jnp.arange(cell_count.shape[0], dtype=jnp.int32)
    earlier = (owners[:, None] == owners[None, :]) & (ordinal[None, :] < ordinal[:, None])
    preceding = jnp.sum(jnp.where(earlier, cell_count[None, :], 0), axis=1)
    return (cell_start, cell_end, preceding)


def lookup(indices, small_table):
    columns = jnp.arange(small_table.shape[0], dtype=jnp.int32)
    matches = indices[:, None] == columns[None, :]
    return jnp.sum(jnp.where(matches, small_table[None, :], 0), axis=1)


def attend_block(queries, key_rows, value_rows, query_marks, key_marks):
    scores = jnp.einsum("qhe,khe->hqk", queries, key_rows, preferred_element_type=jnp.float32) * (
        1.0 / math.sqrt(HEAD_DIM)
    )
    allowed = (query_marks[:, None] == key_marks[None, :])[None, :, :]
    scores = jnp.where(allowed, scores, -jnp.inf)
    highest = jnp.max(scores, axis=2, keepdims=True)
    weights = jnp.exp(scores - highest)
    totals = jnp.sum(weights, axis=2, keepdims=True)
    blended = jnp.einsum(
        "hqk,khe->qhe", weights.astype(jnp.bfloat16), value_rows, preferred_element_type=jnp.float32
    )
    return (blended / jnp.transpose(totals, (1, 0, 2))).astype(jnp.bfloat16)


def on_device(
    patches,
    segments,
    grid_sizes,
    owners,
    row_table,
    col_table,
    gain_attn,
    qkv_weight,
    out_weight,
    gain_mlp,
    up_weight,
    down_weight,
    merge_weight,
):
    group_rows = patches.shape[0]
    model_width = patches.shape[1]
    head_cols = qkv_weight.shape[2]
    heads_here = head_cols // HEAD_DIM
    request_band = lax.axis_index("req")
    cell_start, cell_end, preceding = request_tables(grid_sizes, owners)
    patch_index = request_band * group_rows + jnp.arange(group_rows, dtype=jnp.int32)
    offset_in = patch_index - 4 * lookup(segments, cell_start)
    grid_cells = lookup(segments, grid_sizes[:, 1] // 2)
    block_index = offset_in // 4
    corner = offset_in % 4
    row_place = 2 * (block_index // grid_cells) + corner // 2
    col_place = 2 * (block_index % grid_cells) + corner % 2
    places = jnp.arange(row_table.shape[0], dtype=jnp.int32)
    pick_row = (row_place[:, None] == places[None, :]).astype(jnp.bfloat16)
    pick_col = (col_place[:, None] == places[None, :]).astype(jnp.bfloat16)
    embedded = (
        patches.astype(jnp.float32)
        + jnp.dot(pick_row, row_table, preferred_element_type=jnp.float32)
        + jnp.dot(pick_col, col_table, preferred_element_type=jnp.float32)
    ).astype(jnp.bfloat16)
    normed = layer_norm(embedded, gain_attn).astype(jnp.bfloat16)
    queries = jnp.dot(normed, qkv_weight[0], preferred_element_type=jnp.float32).astype(
        jnp.bfloat16
    )
    key_rows = jnp.dot(normed, qkv_weight[1], preferred_element_type=jnp.float32).astype(
        jnp.bfloat16
    )
    value_rows = jnp.dot(normed, qkv_weight[2], preferred_element_type=jnp.float32).astype(
        jnp.bfloat16
    )
    request_marks = segments + 1
    beside = []
    for direction in (1, -1):
        moved_keys, moved_values, moved_marks = from_behind(
            (key_rows, value_rows, request_marks), "req", direction
        )
        beside.append((moved_keys, moved_values, moved_marks - 1))
    window_keys = jnp.concatenate([beside[0][0], key_rows, beside[1][0]], axis=0).reshape(
        3 * group_rows, heads_here, HEAD_DIM
    )
    window_values = jnp.concatenate([beside[0][1], value_rows, beside[1][1]], axis=0).reshape(
        3 * group_rows, heads_here, HEAD_DIM
    )
    window_marks = jnp.concatenate([beside[0][2], segments, beside[1][2]], axis=0)
    block_rows = 512
    block_count = group_rows // block_rows
    query_blocks = queries.reshape(block_count, block_rows, heads_here, HEAD_DIM)
    mark_blocks = segments.reshape(block_count, block_rows)

    def one_block(pieces):
        return attend_block(pieces[0], window_keys, window_values, pieces[1], window_marks)

    blended = lax.map(one_block, (query_blocks, mark_blocks)).reshape(group_rows, head_cols)
    rows_from = lax.axis_index("hid") * head_cols
    weight_rows = lax.dynamic_slice_in_dim(out_weight, rows_from, head_cols, 0)
    attended = lax.psum(
        jnp.dot(blended, weight_rows, preferred_element_type=jnp.float32).astype(jnp.bfloat16),
        "hid",
    ).astype(jnp.float32)
    residual = (embedded.astype(jnp.float32) + attended).astype(jnp.bfloat16)
    normed_mlp = layer_norm(residual, gain_mlp).astype(jnp.bfloat16)
    lifted = jnp.dot(normed_mlp, up_weight, preferred_element_type=jnp.float32)
    activated = jax.nn.gelu(lifted, approximate=False).astype(jnp.bfloat16)
    partial_sum = jnp.dot(activated, down_weight, preferred_element_type=jnp.float32)
    mlp_total = lax.psum(partial_sum.astype(jnp.bfloat16), "hid").astype(jnp.float32)
    output_rows = (residual.astype(jnp.float32) + mlp_total).astype(jnp.bfloat16)
    merged = output_rows.reshape(group_rows // 4, 4 * model_width)
    projected = jnp.dot(merged, merge_weight, preferred_element_type=jnp.float32).astype(
        jnp.bfloat16
    )
    own_slots = jnp.arange(projected.shape[0], dtype=jnp.int32)
    shard_piece = lax.all_gather(projected, "req", axis=0, tiled=True)
    merged_index = jnp.arange(shard_piece.shape[0], dtype=jnp.int32)
    holder = jnp.sum((cell_end[None, :] <= merged_index[:, None]).astype(jnp.int32), axis=1)
    owner_of = lookup(holder, owners)
    target_slot = merged_index - lookup(holder, cell_start) + lookup(holder, preceding)
    chosen = (target_slot[None, :] == own_slots[:, None]) & (owner_of == request_band)[None, :]
    returned = jnp.dot(chosen.astype(jnp.bfloat16), shard_piece, preferred_element_type=jnp.float32)
    return returned.astype(jnp.bfloat16)[None]


def solution(mesh):
    return jax.shard_map(
        on_device,
        mesh=mesh,
        in_specs=(
            P("req", None),
            P("req"),
            P(),
            P(),
            P(),
            P(),
            P(),
            P(None, None, "hid"),
            P(),
            P(),
            P(None, "hid"),
            P("hid", None),
            P(None, "hid"),
        ),
        out_specs=P("req", None, "hid"),
        check_vma=False,
    )
```

profile of v0, /device:TPU:0, one launch (start us, length us, event | category | flops | bytes accessed | tf_op | source)
XLA Modules:
  0.0 322.5 jit_solution(16551035434421268197)
XLA Ops:
  6.5 0.9 broadcast_add_fusion.2
  7.4 1.3 collective-permute-start.1
  8.7 5.5 %collective-permute-start = (s32[1024]{0:T(1024)S(1)}, s32[1024]{0:T(1024)S(1)}, u32[]{:S(2)}, u32[]{:S(2)}) collective-permute-start(s32[1024]{0:T(1024)S(1)} %broadcast_add_fusion.2), channel_id=1, source_target_pairs={{0,8},{8,16},{16,24},{1,9},{9,17},{17,25},{2,10},{10,18},{18,26},{... | collective-permute-start | bytes 12296 | tf_op jit(solution)/shard_map/ppermute | solution.py:14
  14.2 0.8 fusion.83
  15.2 0.8 fusion.116
  16.1 1.0 select_reduce_fusion.5
  17.1 0.9 select_reduce_fusion.2
  18.1 1.9 fusion.62
  20.0 1.7 convert_reduce_fusion.1
  21.7 0.9 fusion.34
  22.7 0.9 fusion.36
  24.1 1.1 convolution_convert_fusion.3
  25.2 1.3 collective-permute-start.3
  26.5 6.2 %collective-permute-start.2 = (bf16[1024,176]{0,1:T(8,128)(2,1)S(1)}, bf16[1024,176]{0,1:T(8,128)(2,1)}, u32[]{:S(2)}, u32[]{:S(2)}) collective-permute-start(bf16[1024,176]{0,1:T(8,128)(2,1)S(1)} %convolution_convert_fusion.3), channel_id=1, source_target_pairs={{0,8},{8,16},{16,24},{1,9},{9,17},{17,25},{2,10},{10,18},{18,26},{... | collective-permute-start | bytes 1081352 | tf_op jit(solution)/shard_map/ppermute | solution.py:14
  32.7 1.8 convolution_convert_fusion.2
  34.6 1.4 collective-permute-start.5
  36.0 1.1 convolution_convert_fusion.4
  37.4 0.8 copy.20
  38.2 4.9 %collective-permute-start.4 = (bf16[1024,176]{0,1:T(8,128)(2,1)}, bf16[1024,176]{0,1:T(8,128)(2,1)S(1)}, u32[]{:S(2)}, u32[]{:S(2)}) collective-permute-start(bf16[1024,176]{0,1:T(8,128)(2,1)} %convolution_convert_fusion.2), channel_id=1, source_target_pairs={{0,8},{8,16},{16,24},{1,9},{9,17},{17,25},{2,10},{10,18},{18,26},{... | collective-permute-start | bytes 1081352 | tf_op jit(solution)/shard_map/ppermute | solution.py:14
  43.1 1.3 pad_maximum_fusion
  44.4 10.5 %collective-permute-done.5 = bf16[1024,176]{0,1:T(8,128)(2,1)} collective-permute-done((bf16[1024,176]{0,1:T(8,128)(2,1)}, bf16[1024,176]{0,1:T(8,128)(2,1)}, u32[]{:S(2)}, u32[]{:S(2)}) %collective-permute-start.5) | collective-permute-done | bytes 360480 | tf_op jit(solution)/shard_map/ppermute | solution.py:14
  54.9 2.2 pad_maximum_fusion.1
  57.1 34.3 %while.10 = (s32[]{:T(128)}, bf16[2,512,2,88]{1,3,2,0:T(8,128)(2,1)}, s32[2,512]{1,0:T(2,128)S(1)}, s32[3072]{0:T(1024)S(1)}, bf16[2,512,2,88]{1,3,2,0:T(8,128)(...) while((s32[]{:T(128)}, bf16[2,512,2,88]{1,3,2,0:T(8,128)(2,1)}, ...), condition=%wide.region_13.14_spmd, body=%wide.region_10.13_spmd.sunk | while | flops 1143650304 | bytes 104143056 | solution.py:123
  57.1 0.9 broadcast_compare_fusion.3
  58.0 4.2 %fusion.140 = (f32[2,512]{1,0:T(2,128)S(1)}, f32[2,512,3072]{2,1,0:T(8,128)S(1)}) fusion(pred[512,3072]{1,0:T(8,128)(4,1)S(1)} %broadcast_compare_fusion.3, bf16[3072,2,88]{0,2,1:T(8,128)(2,1)S(1)} %get-tuple-element.164, bf16[2,512,2,88]{1,3,2,0:T(8,128)(2,1)} %get-tuple-element.163, s32[]{:T(128)S(6)} %copy.26), kind=kOutput, calls=%fused_computation.2.clone.1 | convolution fusion | flops 563084288 | bytes 15421444 | tf_op jit(solution)/shard_map/while/body/eval_jaxpr/qhe,khe->hqk/dot_general | solution.py:41
  62.2 3.7 %fusion.141 = f32[2,512]{1,0:T(2,128)S(1)} fusion(f32[2,512,3072]{2,1,0:T(8,128)S(1)} %get-tuple-element.141, f32[2,512]{1,0:T(2,128)S(1)} %get-tuple-element.142, pred[512,3072]{1,0:T(8,128)(4,1)S(1)} %broadcast_compare_fusion.3), kind=kLoop, calls=%fused_computation.3.clone.1 | loop fusion | flops 12581888 | bytes 14163968 | tf_op jit(solution)/shard_map/while/body/eval_jaxpr/reduce_sum | solution.py:48
  65.9 1.0 copy-done.1
  66.9 6.6 %fusion.142 = bf16[2,512,2,88]{1,3,2,0:T(8,128)(2,1)S(1)} fusion(bf16[2,512,2,88]{1,3,2,0:T(8,128)(2,1)S(1)} %copy-done.6, s32[]{:T(128)S(6)} %copy.26, bf16[3072,2,88]{0,2,1:T(8,128)(2,1)S(1)} %copy-done.5, f32[2,512,3072]{2,1,0:T(8,128)} %copy-done.1, f32[2,512]{1,0:T(2,128)S(1)} %get-tuple-element.142, ...), kind=kOutput, calls=%fused_computation.12.clone.1 | convolution fusion | flops 566411264 | bytes 15425540 | tf_op jit(solution)/shard_map/while/body/eval_jaxpr/hqk,khe->qhe/dot_general | solution.py:49
  73.5 0.7 copy-done.7
  74.2 0.9 broadcast_compare_fusion.3
  75.1 4.2 %fusion.140 = (f32[2,512]{1,0:T(2,128)S(1)}, f32[2,512,3072]{2,1,0:T(8,128)S(1)}) fusion(pred[512,3072]{1,0:T(8,128)(4,1)S(1)} %broadcast_compare_fusion.3, bf16[3072,2,88]{0,2,1:T(8,128)(2,1)S(1)} %get-tuple-element.164, bf16[2,512,2,88]{1,3,2,0:T(8,128)(2,1)} %get-tuple-element.163, s32[]{:T(128)S(6)} %copy.26), kind=kOutput, calls=%fused_computation.2.clone.1 | convolution fusion | flops 563084288 | bytes 15421444 | tf_op jit(solution)/shard_map/while/body/eval_jaxpr/qhe,khe->hqk/dot_general | solution.py:41
  79.3 3.7 %fusion.141 = f32[2,512]{1,0:T(2,128)S(1)} fusion(f32[2,512,3072]{2,1,0:T(8,128)S(1)} %get-tuple-element.141, f32[2,512]{1,0:T(2,128)S(1)} %get-tuple-element.142, pred[512,3072]{1,0:T(8,128)(4,1)S(1)} %broadcast_compare_fusion.3), kind=kLoop, calls=%fused_computation.3.clone.1 | loop fusion | flops 12581888 | bytes 14163968 | tf_op jit(solution)/shard_map/while/body/eval_jaxpr/reduce_sum | solution.py:48
  83.0 1.0 copy-done.1
  84.0 6.6 %fusion.142 = bf16[2,512,2,88]{1,3,2,0:T(8,128)(2,1)S(1)} fusion(bf16[2,512,2,88]{1,3,2,0:T(8,128)(2,1)S(1)} %copy-done.6, s32[]{:T(128)S(6)} %copy.26, bf16[3072,2,88]{0,2,1:T(8,128)(2,1)S(1)} %copy-done.5, f32[2,512,3072]{2,1,0:T(8,128)} %copy-done.1, f32[2,512]{1,0:T(2,128)S(1)} %get-tuple-element.142, ...), kind=kOutput, calls=%fused_computation.12.clone.1 | convolution fusion | flops 566411264 | bytes 15425540 | tf_op jit(solution)/shard_map/while/body/eval_jaxpr/hqk,khe->qhe/dot_general | solution.py:49
  90.6 0.7 copy-done.7
  91.4 1.4 copy.21
  92.8 3.7 %convolution_convert_fusion.1 = bf16[1024,1408]{1,0:T(8,128)(2,1)} fusion(bf16[1024,176]{0,1:T(8,128)(2,1)S(1)} %bitcast.92, bf16[1408,1408]{1,0:T(8,128)(2,1)} %param.23, s32[]{:T(128)S(6)} %select_n.141), kind=kOutput, calls=%fused_computation.41 | convolution fusion | flops 508952576 | bytes 3739652 | tf_op jit(solution)/shard_map/dot_general | solution.py:127
  96.8 80.0 %all-reduce.3.cloned.1.call-done = bf16[1024,1408]{1,0:T(8,128)(2,1)} async-done(((bf16[1024,1408]{1,0:T(8,128)(2,1)}), bf16[1024,1408]{1,0:T(8,128)(2,1)}) %all-reduce.3.cloned.1.call-update) | async-done | bytes 2883600 | tf_op jit(solution)/shard_map/psum | solution.py:126
  176.7 3.6 %convert_reduce_fusion = (f32[1024]{0:T(1024)S(1)}, bf16[1024,1408]{1,0:T(8,128)(2,1)S(1)}) fusion(bf16[1024,1408]{1,0:T(8,128)(2,1)} %all-reduce.3.cloned.1.call-done, bf16[1024,1408]{1,0:T(8,128)(2,1)} %copy-done.2), kind=kLoop, calls=%fused_computation.22 | loop fusion | flops 8649728 | bytes 8654848 | tf_op jit(solution)/shard_map/reduce_sum | solution.py:19
  180.3 1.6 copy-done.3
  181.9 0.9 fusion.31
  182.8 16.1 %convolution_convert_fusion = bf16[1024,1408]{1,0:T(8,128)(2,1)} fusion(bf16[768,1408]{1,0:T(8,128)(2,1)S(1)} %copy-done, bf16[1408,768]{1,0:T(8,128)(2,1)} %param.25, bf16[1024,1408]{1,0:T(8,128)(2,1)} %copy-done.3, f32[1408]{0:T(1024)S(1)} %copy-done.13, f32[1024]{0:T(1024)S(1)} %add_rsqrt_fusion, f32[1024]{0:T(1024)S(1)} %broadcast_multiply_fusion), kind=kOutput, calls=%fused_computation.40 | convolution fusion | flops 4488953856 | bytes 10106368 | tf_op jit(solution)/shard_map/dot_general | solution.py:134
  199.0 72.0 %all-reduce.5.cloned.1.call-done = bf16[1024,1408]{1,0:T(8,128)(2,1)} async-done(((bf16[1024,1408]{1,0:T(8,128)(2,1)}), bf16[1024,1408]{1,0:T(8,128)(2,1)}) %all-reduce.5.cloned.1.call-update) | async-done | bytes 2883600 | tf_op jit(solution)/shard_map/psum | solution.py:135
  271.0 5.0 %fusion.38 = bf16[1024,1408]{1,0:T(8,128)(2,1)} fusion(bf16[1024,1408]{1,0:T(8,128)(2,1)} %copy-done.3, bf16[1024,1408]{1,0:T(8,128)(2,1)} %all-reduce.5.cloned.1.call-done), kind=kLoop, calls=%fused_computation.37 | loop fusion | flops 5767168 | bytes 8650752 | tf_op jit(solution)/shard_map/convert_element_type | solution.py:136
  275.9 5.6 %reshape.292 = bf16[256,5632]{1,0:T(8,128)(2,1)} reshape(bf16[1024,1408]{1,0:T(8,128)(2,1)} %fusion.38) | data formatting | bytes 5767168 | tf_op jit(solution)/shard_map/reshape | solution.py:137
  281.6 5.9 %convolution_convert_fusion.6 = bf16[256,512]{1,0:T(8,128)(2,1)} fusion(bf16[256,5632]{1,0:T(8,128)(2,1)} %reshape.292, bf16[5632,512]{1,0:T(8,128)(2,1)} %param.27), kind=kOutput, calls=%fused_computation.68 | convolution fusion | flops 1476526080 | bytes 8912896 | tf_op jit(solution)/shard_map/dot_general | solution.py:138
  287.5 26.1 %all-gather.2.cloned.1.call-done = bf16[1024,512]{1,0:T(8,128)(2,1)} async-done(((bf16[256,512]{1,0:T(8,128)(2,1)}), bf16[1024,512]{1,0:T(8,128)(2,1)}) %all-gather.2.cloned.1.call-update) | async-done | bytes 1048592 | tf_op jit(solution)/shard_map/all_gather | solution.py:142
  313.6 2.4 fusion.58
  (62 shorter events, 1.7 us)
Async XLA Ops:
  6.5 176.3 %copy-start = (bf16[768,1408]{1,0:T(8,128)(2,1)S(1)}, bf16[768,1408]{1,0:T(8,128)(2,1)}, u32[]{:S(2)}) copy-start(bf16[768,1408]{1,0:T(8,128)(2,1)} %param.26) | copy-start | bytes 6488068
  6.5 13.4 %copy-start.9 = (bf16[32,1408]{1,0:T(8,128)(2,1)S(1)}, bf16[32,1408]{1,0:T(8,128)(2,1)}, u32[]{:S(2)}) copy-start(bf16[32,1408]{1,0:T(8,128)(2,1)} %param.20) | copy-start | bytes 270340
  6.5 170.2 %all-reduce.3.cloned.1.call-start = ((), (), s32[]{:S(2)}) async-start(), calls=%async_computation | async-start | bytes 5767168 | tf_op jit(solution)/shard_map/psum | solution.py:126
  7.4 30.8 %collective-permute-start.1 = (s32[1024]{0:T(1024)S(1)}, s32[1024]{0:T(1024)S(1)}, u32[]{:S(2)}, u32[]{:S(2)}) collective-permute-start(s32[1024]{0:T(1024)S(1)} %broadcast_add_fusion.2), channel_id=1, source_target_pairs={{8,0},{16,8},{24,16},{9,1},{17,9},{25,17},{10,2},{18,10},{26,18},{... | collective-permute-start | bytes 12296 | tf_op jit(solution)/shard_map/ppermute | solution.py:14
  8.7 34.4 %collective-permute-start = (s32[1024]{0:T(1024)S(1)}, s32[1024]{0:T(1024)S(1)}, u32[]{:S(2)}, u32[]{:S(2)}) collective-permute-start(s32[1024]{0:T(1024)S(1)} %broadcast_add_fusion.2), channel_id=1, source_target_pairs={{0,8},{8,16},{16,24},{1,9},{9,17},{17,25},{2,10},{10,18},{18,26},{... | collective-permute-start | bytes 12296 | tf_op jit(solution)/shard_map/ppermute | solution.py:14
  16.1 3.9 %copy-start.4 = (bf16[1024,1408]{1,0:T(8,128)(2,1)S(1)}, bf16[1024,1408]{1,0:T(8,128)(2,1)}, u32[]{:S(2)}) copy-start(bf16[1024,1408]{1,0:T(8,128)(2,1)} %param.15) | copy-start | bytes 8650756
  20.0 2.7 copy-start.11
  21.7 1.9 copy-start.2
  22.6 1.4 copy-start.12
  25.2 11.9 %copy-start.8 = (bf16[1024,176]{0,1:T(8,128)(2,1)}, bf16[1024,176]{0,1:T(8,128)(2,1)S(1)}, u32[]{:S(2)}) copy-start(bf16[1024,176]{0,1:T(8,128)(2,1)S(1)} %convolution_convert_fusion.3) | copy-start | bytes 1081348
  25.2 17.9 %collective-permute-start.3 = (bf16[1024,176]{0,1:T(8,128)(2,1)S(1)}, bf16[1024,176]{0,1:T(8,128)(2,1)}, u32[]{:S(2)}, u32[]{:S(2)}) collective-permute-start(bf16[1024,176]{0,1:T(8,128)(2,1)S(1)} %convolution_convert_fusion.3), channel_id=1, source_target_pairs={{8,0},{16,8},{24,16},{9,1},{17,9},{25,17},{10,2},{18,10},{26,18},{... | collective-permute-start | bytes 1081352 | tf_op jit(solution)/shard_map/ppermute | solution.py:14
  26.5 16.6 %collective-permute-start.2 = (bf16[1024,176]{0,1:T(8,128)(2,1)S(1)}, bf16[1024,176]{0,1:T(8,128)(2,1)}, u32[]{:S(2)}, u32[]{:S(2)}) collective-permute-start(bf16[1024,176]{0,1:T(8,128)(2,1)S(1)} %convolution_convert_fusion.3), channel_id=1, source_target_pairs={{0,8},{8,16},{16,24},{1,9},{9,17},{17,25},{2,10},{10,18},{18,26},{... | collective-permute-start | bytes 1081352 | tf_op jit(solution)/shard_map/ppermute | solution.py:14
  34.6 2.5 copy-start.10
  34.6 20.3 %collective-permute-start.5 = (bf16[1024,176]{0,1:T(8,128)(2,1)}, bf16[1024,176]{0,1:T(8,128)(2,1)}, u32[]{:S(2)}, u32[]{:S(2)}) collective-permute-start(bf16[1024,176]{0,1:T(8,128)(2,1)} %convolution_convert_fusion.2), channel_id=1, source_target_pairs={{8,0},{16,8},{24,16},{9,1},{17,9},{25,17},{10,2},{18,10},{26,18},{... | collective-permute-start | bytes 1081352 | tf_op jit(solution)/shard_map/ppermute | solution.py:14
  38.2 16.7 %collective-permute-start.4 = (bf16[1024,176]{0,1:T(8,128)(2,1)}, bf16[1024,176]{0,1:T(8,128)(2,1)S(1)}, u32[]{:S(2)}, u32[]{:S(2)}) collective-permute-start(bf16[1024,176]{0,1:T(8,128)(2,1)} %convolution_convert_fusion.2), channel_id=1, source_target_pairs={{0,8},{8,16},{16,24},{1,9},{9,17},{17,25},{2,10},{10,18},{18,26},{... | collective-permute-start | bytes 1081352 | tf_op jit(solution)/shard_map/ppermute | solution.py:14
  62.2 4.7 %copy-start.1 = (f32[2,512,3072]{2,1,0:T(8,128)}, f32[2,512,3072]{2,1,0:T(8,128)S(1)}, u32[]{:S(2)}) copy-start(f32[2,512,3072]{2,1,0:T(8,128)S(1)} %get-tuple-element.141) | copy-start | bytes 37748740 | tf_op jit(solution)/shard_map/while
  62.2 4.7 %copy-start.5 = (bf16[3072,2,88]{0,2,1:T(8,128)(2,1)S(1)}, bf16[3072,2,88]{0,2,1:T(8,128)(2,1)}, u32[]{:S(2)}) copy-start(bf16[3072,2,88]{0,2,1:T(8,128)(2,1)} %get-tuple-element.165) | copy-start | bytes 3244036 | tf_op jit(solution)/shard_map/while
  62.2 4.7 %copy-start.6 = (bf16[2,512,2,88]{1,3,2,0:T(8,128)(2,1)S(1)}, bf16[2,512,2,88]{1,3,2,0:T(8,128)(2,1)}, u32[]{:S(2)}) copy-start(bf16[2,512,2,88]{1,3,2,0:T(8,128)(2,1)} %get-tuple-element.152) | copy-start | bytes 1081348 | tf_op jit(solution)/shard_map/while
  73.5 0.7 copy-start.7
  79.3 4.7 %copy-start.1 = (f32[2,512,3072]{2,1,0:T(8,128)}, f32[2,512,3072]{2,1,0:T(8,128)S(1)}, u32[]{:S(2)}) copy-start(f32[2,512,3072]{2,1,0:T(8,128)S(1)} %get-tuple-element.141) | copy-start | bytes 37748740 | tf_op jit(solution)/shard_map/while
  79.3 4.7 %copy-start.5 = (bf16[3072,2,88]{0,2,1:T(8,128)(2,1)S(1)}, bf16[3072,2,88]{0,2,1:T(8,128)(2,1)}, u32[]{:S(2)}) copy-start(bf16[3072,2,88]{0,2,1:T(8,128)(2,1)} %get-tuple-element.165) | copy-start | bytes 3244036 | tf_op jit(solution)/shard_map/while
  79.3 4.7 %copy-start.6 = (bf16[2,512,2,88]{1,3,2,0:T(8,128)(2,1)S(1)}, bf16[2,512,2,88]{1,3,2,0:T(8,128)(2,1)}, u32[]{:S(2)}) copy-start(bf16[2,512,2,88]{1,3,2,0:T(8,128)(2,1)} %get-tuple-element.152) | copy-start | bytes 1081348 | tf_op jit(solution)/shard_map/while
  90.6 0.7 copy-start.7
  96.5 86.3 %copy-start.13 = (f32[1408]{0:T(1024)S(1)}, f32[1408]{0:T(1024)}, u32[]{:S(2)}) copy-start(f32[1408]{0:T(1024)} %param.24) | copy-start | bytes 16900
  96.5 174.5 %all-reduce.5.cloned.1.call-start = ((), (), s32[]{:S(2)}) async-start(), calls=%async_computation.1 | async-start | bytes 5767168 | tf_op jit(solution)/shard_map/psum | solution.py:135
  180.3 1.6 copy-start.3
  198.9 114.7 %all-gather.2.cloned.1.call-start = ((), (), s32[]{:S(2)}) async-start(), calls=%async_computation.2 | async-start | bytes 1310720 | tf_op jit(solution)/shard_map/all_gather | solution.py:142
Sparse Core Ops, SparseCore 0:
  96.6 80.0 all-reduce.2
  199.1 71.8 all-reduce.4
  287.6 25.9 all-gather.1
where the time goes:
time: 323 us
  waiting for transfers between devices  189 us (59%)
  matrix products  57.2 us (18%)
  other arithmetic  28.7 us (9%)
  starting transfers between devices  20.9 us (6%)
  local copies, waits for them, and re-layouts  13.6 us (4%)
  between operations  13.5 us (4%)
    psum x1, waiting for transfers between devices, on_device(): lax.psum(jnp.dot(blended, weight_rows, preferred_element_type=jnp.float32...  80 us
    psum x1, waiting for transfers between devices, on_device(): lax.psum(partial_sum.astype(jnp.bfloat16), 'hid').astype(jnp.float32)  72 us
    all_gather x1, waiting for transfers between devices, on_device(): shard_piece = lax.all_gather(projected, 'req', axis=0, tiled=True)  26.1 us
    ppermute x6, starting transfers between devices, from_behind(): lax.ppermute(value, axis, [(source, source + steps) for source in range(f...  20.6 us
    dot_general x1, matrix products, on_device(): jnp.dot(activated, down_weight, preferred_element_type=jnp.float32)  16.1 us
    dot_general x2, matrix products, attend_block(): jnp.einsum('hqk,khe->qhe', weights.astype(jnp.bfloat16), value_rows, pref...  13.2 us
    ppermute x6, waiting for transfers between devices, from_behind(): lax.ppermute(value, axis, [(source, source + steps) for source in range(f...  10.5 us
    dot_general x2, matrix products, attend_block(): jnp.einsum('qhe,khe->hqk', queries, key_rows, preferred_element_type=jnp....  8.31 us
  transfers between devices with their start and end apart: 9, of which 4 were waited for; matrix products, arithmetic and copies ran while one was open for 5% of the time, Pallas kernels for 0%

commit v1 on v0

v1 whole, which is shorter than its diff:
```python
import functools
import math

import jax
import jax.numpy as jnp
from jax import lax
from jax.experimental import pallas as pl
from jax.experimental.pallas import tpu as pltpu
from jax.sharding import PartitionSpec as P

HEAD_DIM = 88
TILE = 256
LANES = 128
LOW = -1e30
VMEM_LIMIT = 56 * 1024 * 1024

NT = (((1,), (1,)), ((), ()))
TN = (((0,), (0,)), ((), ()))
TT = (((0,), (1,)), ((), ()))


def dot(left, right, dims=(((1,), (0,)), ((), ()))):
    return lax.dot_general(left, right, dims, preferred_element_type=jnp.float32)


def norm_rows(widened, gain_row):
    centered = widened - jnp.mean(widened, axis=-1, keepdims=True)
    variance = jnp.mean(centered * centered, axis=-1, keepdims=True)
    return centered * lax.rsqrt(variance + 1e-06) * gain_row


def whole(shape):
    return pl.BlockSpec(shape, lambda *_: (0,) * len(shape))


def project_kernel(
    base_ref, table_ref, patches_ref, places_ref, gain_ref, weight_ref, embedded_ref, q_ref, kv_ref
):
    rows = patches_ref.shape[0]
    width = weight_ref.shape[2]
    first = base_ref[0] + pl.program_id(0) * rows
    index = first + lax.broadcasted_iota(jnp.int32, (rows, LANES), 0)
    starts = table_ref[0:1, :]
    inside = (index >= starts) & (index < table_ref[1:2, :])
    offset = jnp.sum(jnp.where(inside, index - starts, 0), axis=1, keepdims=True)
    cells_across = jnp.sum(jnp.where(inside, table_ref[2:3, :], 0), axis=1, keepdims=True)
    shift = jnp.where(cells_across == 16, 4, jnp.where(cells_across == 8, 3, 2))
    block = offset >> 2
    corner = offset & 3
    row_place = 2 * (block >> shift) + (corner >> 1)
    col_place = 2 * (block & (cells_across - 1)) + (corner & 1)
    place_count = places_ref.shape[0]
    lane = lax.broadcasted_iota(jnp.int32, (rows, place_count), 1)
    picked = (lane == row_place) | (lane == col_place + place_count // 2)
    picked = jnp.where(picked, 1.0, 0.0).astype(jnp.bfloat16)
    embedded = (patches_ref[...].astype(jnp.float32) + dot(picked, places_ref[...])).astype(
        jnp.bfloat16
    )
    embedded_ref[...] = embedded
    normed = norm_rows(embedded.astype(jnp.float32), gain_ref[...]).astype(jnp.bfloat16)
    q_ref[...] = dot(weight_ref[0], normed, TT).astype(jnp.bfloat16)
    kv_ref[0:width, :] = dot(weight_ref[1], normed, TT).astype(jnp.bfloat16)
    kv_ref[width : 2 * width, :] = dot(weight_ref[2], normed, TT).astype(jnp.bfloat16)


def project(base, table, patches, places, gain, weight):
    rows, model = patches.shape
    width = weight.shape[2]
    return pl.pallas_call(
        project_kernel,
        grid_spec=pltpu.PrefetchScalarGridSpec(
            num_scalar_prefetch=1,
            grid=(rows // TILE,),
            in_specs=[
                whole(table.shape),
                pl.BlockSpec((TILE, model), lambda i, _: (i, 0)),
                whole(places.shape),
                whole(gain.shape),
                whole(weight.shape),
            ],
            out_specs=[
                pl.BlockSpec((TILE, model), lambda i, _: (i, 0)),
                pl.BlockSpec((width, TILE), lambda i, _: (0, i)),
                pl.BlockSpec((2 * width, TILE), lambda i, _: (0, i)),
            ],
        ),
        out_shape=[
            jax.ShapeDtypeStruct((rows, model), jnp.bfloat16),
            jax.ShapeDtypeStruct((width, rows), jnp.bfloat16),
            jax.ShapeDtypeStruct((2 * width, rows), jnp.bfloat16),
        ],
        compiler_params=pltpu.CompilerParams(vmem_limit_bytes=VMEM_LIMIT),
        cost_estimate=pl.CostEstimate(
            flops=6 * rows * model * width, bytes_accessed=4 * rows * model, transcendentals=0
        ),
    )(base, table, patches, places, gain, weight)


def attend_kernel(heads, low_ref, high_ref, base_ref, start_ref, end_ref, q_ref, *rest):
    parts, out_ref = rest[:-1], rest[-1]
    rows = q_ref.shape[1]
    width = heads * HEAD_DIM
    scale = math.log2(math.e) / math.sqrt(HEAD_DIM)
    for tile in range(rows // TILE):
        span = slice(tile * TILE, (tile + 1) * TILE)
        start = start_ref[:, span]
        end = end_ref[:, span]
        low = low_ref[tile]
        high = high_ref[tile]
        queries = [q_ref[h * HEAD_DIM : (h + 1) * HEAD_DIM, span] for h in range(heads)]
        carry = tuple(
            (
                jnp.full((1, TILE), LOW, jnp.float32),
                jnp.zeros((1, TILE), jnp.float32),
                jnp.zeros((HEAD_DIM, TILE), jnp.float32),
            )
            for _ in range(heads)
        )
        for number, part in enumerate(parts):
            base = base_ref[number]
            tiles = part.shape[1] // TILE
            first = jnp.clip((low - base) // TILE, 0, tiles)
            last = jnp.clip((high - base + TILE - 1) // TILE, 0, tiles)

            def step(place, carry, part=part, base=base, queries=queries, start=start, end=end):
                where = pl.ds(pl.multiple_of(place * TILE, TILE), TILE)
                index = base + place * TILE + lax.broadcasted_iota(jnp.int32, (TILE, TILE), 0)
                allowed = (index >= start) & (index < end)
                new = []
                for h in range(heads):
                    top, total, acc = carry[h]
                    key_rows = part[h * HEAD_DIM : (h + 1) * HEAD_DIM, where]
                    value_rows = part[width + h * HEAD_DIM : width + (h + 1) * HEAD_DIM, where]
                    scores = dot(key_rows, queries[h], TN) * scale
                    scores = jnp.where(allowed, scores, LOW)
                    higher = jnp.maximum(top, jnp.max(scores, axis=0, keepdims=True))
                    weights = jnp.exp2(scores - higher)
                    fade = jnp.exp2(top - higher)
                    total = total * fade + jnp.sum(weights, axis=0, keepdims=True)
                    acc = acc * fade + dot(value_rows, weights.astype(jnp.bfloat16))
                    new.append((higher, total, acc))
                return tuple(new)

            carry = lax.fori_loop(first, last, step, carry)
        for h in range(heads):
            _, total, acc = carry[h]
            out_ref[h * HEAD_DIM : (h + 1) * HEAD_DIM, span] = (acc / total).astype(jnp.bfloat16)


def attend(low, high, bases, start, end, queries, parts):
    width, rows = queries.shape
    heads = width // HEAD_DIM
    smem = pl.BlockSpec(memory_space=pltpu.SMEM)
    vmem = pl.BlockSpec(memory_space=pltpu.VMEM)
    return pl.pallas_call(
        functools.partial(attend_kernel, heads),
        in_specs=[smem] * 3 + [vmem] * (3 + len(parts)),
        out_specs=vmem,
        out_shape=jax.ShapeDtypeStruct((width, rows), jnp.bfloat16),
        compiler_params=pltpu.CompilerParams(vmem_limit_bytes=VMEM_LIMIT),
        cost_estimate=pl.CostEstimate(
            flops=4 * rows * rows * width,
            bytes_accessed=8 * rows * width,
            transcendentals=heads * rows * rows,
        ),
    )(low, high, bases, start, end, queries, *parts)


def mlp_kernel(
    blended_ref, embedded_ref, out_ref, gain_ref, up_ref, down_ref, residual_ref, partial_ref
):
    attended = dot(blended_ref[...], out_ref[...], TN)
    residual = (embedded_ref[...].astype(jnp.float32) + attended).astype(jnp.bfloat16)
    residual_ref[...] = residual
    normed = norm_rows(residual.astype(jnp.float32), gain_ref[...]).astype(jnp.bfloat16)
    lifted = dot(normed, up_ref[...])
    activated = (0.5 * lifted * (1.0 + lax.erf(lifted * math.sqrt(0.5)))).astype(jnp.bfloat16)
    partial_ref[...] = dot(activated, down_ref[...]).astype(jnp.bfloat16)


def mlp(blended, embedded, out_weight, gain, up_weight, down_weight):
    model, rows = blended.shape
    hidden = up_weight.shape[1]
    row_spec = pl.BlockSpec((TILE, model), lambda i: (i, 0))
    return pl.pallas_call(
        mlp_kernel,
        grid=(rows // TILE,),
        in_specs=[
            pl.BlockSpec((model, TILE), lambda i: (0, i)),
            row_spec,
            whole(out_weight.shape),
            whole(gain.shape),
            whole(up_weight.shape),
            whole(down_weight.shape),
        ],
        out_specs=[row_spec, row_spec],
        out_shape=[jax.ShapeDtypeStruct((rows, model), jnp.bfloat16)] * 2,
        compiler_params=pltpu.CompilerParams(vmem_limit_bytes=VMEM_LIMIT),
        cost_estimate=pl.CostEstimate(
            flops=2 * rows * model * (model + 2 * hidden),
            bytes_accessed=2 * (4 * rows * model + model * (model + 2 * hidden)),
            transcendentals=rows * hidden,
        ),
    )(blended, embedded, out_weight, gain, up_weight, down_weight)


def neighbour_keys(keys, band, bands):
    if bands == 4:
        across = lax.ppermute(keys, "req", [(0, 1), (1, 0), (2, 3), (3, 2)])
        along = lax.ppermute(across, "req", [(0, 2), (3, 1)])
        even = band % 2 == 0
        across_band = jnp.where(even, band + 1, band - 1)
        along_band = jnp.where(even, band - 1, band + 1)
        return (across, across_band), (along, along_band)
    after = lax.ppermute(keys, "req", [(i + 1, i) for i in range(bands - 1)])
    before = lax.ppermute(keys, "req", [(i, i + 1) for i in range(bands - 1)])
    return (before, band - 1), (after, band + 1)


def on_device(
    patches,
    segments,
    grid_sizes,
    owners,
    row_table,
    col_table,
    gain_attn,
    qkv_weight,
    out_weight,
    gain_mlp,
    up_weight,
    down_weight,
    merge_weight,
):
    rows, model = patches.shape
    bands = lax.axis_size("req")
    band = lax.axis_index("req")
    part_count = lax.axis_size("hid")
    requests = grid_sizes.shape[0]

    cells_across = grid_sizes[:, 1] // 2
    cell_count = grid_sizes[:, 0] // 2 * cells_across
    ordinal = jnp.arange(requests, dtype=jnp.int32)
    earlier = ordinal[None, :] < ordinal[:, None]
    cell_start = jnp.sum(jnp.where(earlier, cell_count[None, :], 0), axis=1)
    cell_end = cell_start + cell_count
    same_owner = earlier & (owners[:, None] == owners[None, :])
    preceding = jnp.sum(jnp.where(same_owner, cell_count[None, :], 0), axis=1)

    table = jnp.pad(
        jnp.stack([4 * cell_start, 4 * cell_end, cells_across]), ((0, 5), (0, LANES - requests))
    )
    places = jnp.concatenate([row_table, col_table], axis=0)
    base = (band * rows).astype(jnp.int32)
    embedded, queries, keys = project(
        base[None], table, patches, places, gain_attn[None, :], qkv_weight
    )

    (near, near_band), (far, far_band) = neighbour_keys(keys, band, bands)
    patch_index = base + jnp.arange(rows, dtype=jnp.int32)
    mine = (4 * cell_start[:, None] <= patch_index[None, :]) & (
        patch_index[None, :] < 4 * cell_end[:, None]
    )
    start = jnp.sum(jnp.where(mine, 4 * cell_start[:, None], 0), axis=0, keepdims=True)
    end = jnp.sum(jnp.where(mine, 4 * cell_end[:, None], 0), axis=0, keepdims=True)
    low = start[0, ::TILE]
    high = end[0, TILE - 1 :: TILE]
    beyond = 1 << 28
    part_bands = jnp.stack([band, near_band, far_band])
    bases = jnp.where((part_bands >= 0) & (part_bands < bands), part_bands * rows, beyond)
    blended = attend(low, high, bases, start, end, queries, (keys, near, far))

    gathered = lax.all_gather(blended, "hid", axis=0, tiled=True)
    residual, partial_sum = mlp(
        gathered, embedded, out_weight, gain_mlp[None, :], up_weight, down_weight
    )
    home = lax.axis_index("hid")
    summed = lax.psum_scatter(partial_sum, "hid", scatter_dimension=0, tiled=True)
    home_rows = rows // part_count
    own_residual = lax.dynamic_slice_in_dim(residual, home * home_rows, home_rows, 0)
    output_rows = (own_residual.astype(jnp.float32) + summed.astype(jnp.float32)).astype(
        jnp.bfloat16
    )
    merged = lax.all_gather(
        output_rows.reshape(home_rows // 4, 4 * model), "hid", axis=0, tiled=True
    )
    projected = jnp.dot(merged, merge_weight, preferred_element_type=jnp.float32).astype(
        jnp.bfloat16
    )

    merged_rows = projected.shape[0]
    slots = jnp.arange(merged_rows, dtype=jnp.int32)
    if bands == 4:
        shifts = (1, 2, 3)
        pieces = [projected] + [
            lax.ppermute(projected, "req", [(i, i ^ shift) for i in range(4)]) for shift in shifts
        ]
        piece_bands = [band] + [band ^ shift for shift in shifts]
    else:
        pieces = [lax.all_gather(projected, "req", axis=0, tiled=True)]
        piece_bands = [0]
    returned = jnp.zeros(projected.shape, jnp.float32)
    for piece, piece_band in zip(pieces, piece_bands):
        merged_index = piece_band * merged_rows + jnp.arange(piece.shape[0], dtype=jnp.int32)
        holding = (cell_start[None, :] <= merged_index[:, None]) & (
            merged_index[:, None] < cell_end[None, :]
        )
        holding = holding & (owners == band)[None, :]
        target = jnp.sum(
            jnp.where(holding, merged_index[:, None] + (preceding - cell_start)[None, :] + 1, 0),
            axis=1,
        )
        chosen = (target[None, :] == slots[:, None] + 1).astype(jnp.bfloat16)
        returned = returned + jnp.dot(chosen, piece, preferred_element_type=jnp.float32)
    return returned.astype(jnp.bfloat16)[None]


def solution(mesh):
    return jax.shard_map(
        on_device,
        mesh=mesh,
        in_specs=(
            P("req", None),
            P("req"),
            P(),
            P(),
            P(),
            P(),
            P(),
            P(None, None, "hid"),
            P(),
            P(),
            P(None, "hid"),
            P("hid", None),
            P(None, "hid"),
        ),
        out_specs=P("req", None, "hid"),
        check_vma=False,
    )
```

time: 323 us -> 240 us (0.74)
  matrix products: 57.2 us -> 6.93 us
  Pallas kernels: 0 us -> 46.2 us
  waiting for transfers between devices: 189 us -> 148 us
  other arithmetic: 28.7 us -> 5.29 us
  starting transfers between devices: 20.9 us -> 10.3 us
  local copies, waits for them, and re-layouts: 13.6 us -> 8.65 us
    psum x2 -> x0, waiting for transfers between devices: 152 us -> none  [the longest x1 80 us: on_device(): lax.psum(jnp.dot(blended, weight_rows, preferred_element_type=jnp.float32...]
    dot_general x12 -> x4, matrix products: 51.3 us -> 1.77 us  [on_device(): jnp.dot(chosen, piece, preferred_element_type=jnp.float32)]
    pallas_call x0 -> x3, Pallas kernels: none -> 46.2 us  [the longest x1 18.8 us: mlp(): pl.pallas_call(mlp_kernel, grid=(rows // TILE,), in_specs=[pl.BlockSpec((...]
    all_gather x1 -> x2, waiting for transfers between devices: 26.1 us -> 70.4 us  [the longest x1 35.4 us: on_device(): lax.all_gather(output_rows.reshape(home_rows // 4, 4 * model), 'hid', axi...]
    reduce_scatter x0 -> x1, waiting for transfers between devices: none -> 37.7 us  [on_device(): lax.psum_scatter(partial_sum, 'hid', scatter_dimension=0, tiled=True)]
    ppermute x6 -> x5, waiting for transfers between devices: 10.5 us -> 39.7 us  [the longest x1 16.3 us: neighbour_keys(): across = lax.ppermute(keys, 'req', [(0, 1), (1, 0), (2, 3), (3, 2)])]
    reduce_sum x8 -> x3, other arithmetic: 14.7 us -> 1.14 us  [the longest x1 0.91 us: on_device(): preceding = jnp.sum(jnp.where(same_owner, cell_count[None, :], 0), axis=1)]
    ppermute x6 -> x5, starting transfers between devices: 20.6 us -> 10.2 us  [the longest x1 3.71 us: neighbour_keys(): along = lax.ppermute(across, 'req', [(0, 2), (3, 1)])]
  transfers between devices with their start and end apart: 9 -> 8, of which waited for: 4 -> 7; matrix products, arithmetic and copies ran while one was open for 5% -> 1% of each run, Pallas kernels for 0% -> 0%
where the time goes in v1:
time: 240 us; the launch traced here: 239 us
  waiting for transfers between devices  148 us (62%)
  Pallas kernels  46.2 us (19%)
  between operations  13.3 us (6%)
  starting transfers between devices  10.3 us (4%)
  local copies, waits for them, and re-layouts  8.65 us (4%)
  matrix products  6.93 us (3%)
  other arithmetic  5.29 us (2%)
    reduce_scatter x1, waiting for transfers between devices, on_device(): lax.psum_scatter(partial_sum, 'hid', scatter_dimension=0, tiled=True)  37.7 us
    all_gather x1, waiting for transfers between devices, on_device(): lax.all_gather(output_rows.reshape(home_rows // 4, 4 * model), 'hid', axi...  35.4 us
    all_gather x1, waiting for transfers between devices, on_device(): gathered = lax.all_gather(blended, 'hid', axis=0, tiled=True)  35 us
    pallas_call x1, Pallas kernels, mlp(): pl.pallas_call(mlp_kernel, grid=(rows // TILE,), in_specs=[pl.BlockSpec((...  18.8 us
    pallas_call x1, Pallas kernels, attend(): pl.pallas_call(functools.partial(attend_kernel, heads), in_specs=[smem] *...  17.3 us
    ppermute x1, waiting for transfers between devices, neighbour_keys(): across = lax.ppermute(keys, 'req', [(0, 1), (1, 0), (2, 3), (3, 2)])  16.3 us
    ppermute x1, waiting for transfers between devices, neighbour_keys(): along = lax.ppermute(across, 'req', [(0, 2), (3, 1)])  12.4 us
    ppermute x3, waiting for transfers between devices, on_device(): lax.ppermute(projected, 'req', [(i, i ^ shift) for i in range(4)])  11 us
  transfers between devices with their start and end apart: 8, of which 7 were waited for; matrix products, arithmetic and copies ran while one was open for 1% of the time, Pallas kernels for 0%

profile of v1, /device:TPU:0, one launch (start us, length us, event | category | flops | bytes accessed | tf_op | source)
XLA Modules:
  0.0 238.6 jit_solution(12649649414154165721)
XLA Ops:
  6.5 0.0 all-gather.3.cloned.1.call-start
  6.5 0.8 fusion.21
  7.3 0.9 select_reduce_fusion.6
  8.2 0.8 fusion.18
  9.0 3.8 %copy.14.weight_ref = bf16[3,1408,176]{2,1,0:T(8,128)(2,1)} copy(bf16[3,1408,176]{1,2,0:T(8,128)(2,1)} %param.19) | data formatting | bytes 2973696 | tf_op args[7]
  12.8 0.0 copy-done.3
  12.8 0.6 broadcast_in_dim.61.gain_ref
  13.4 0.6 pad.4.table_ref
  14.0 0.0 copy-done.1
  14.0 0.0 copy-done
  14.0 0.7 pad_maximum_fusion.places_ref
  14.7 10.1 %shard_map.118 = (bf16[1024,1408]{1,0:T(8,128)(2,1)}, bf16[176,1024]{1,0:T(8,128)(2,1)}, bf16[352,1024]{1,0:T(8,128)(2,1)}) custom-call(s32[1]{0:T(128)} %bitcast.11.base_ref, s32[8,128]{1,0:T(8,128)} %pad.4.table_ref, bf16[1024,1408]{1,0:T(8,128)(2,1)} %patches_ref.1, bf16[64,1408]{1,0:T(8,128)(2,1)} %pad_maximum_fusion.places_ref, ...), custom_call_target="tpu_custom_call" | custom-call | flops 1522532352 | bytes 5767168 | tf_op jit(solution)/shard_map/pallas_call | solution.py:69
  24.8 2.9 %collective-permute-start = (bf16[352,1024]{1,0:T(8,128)(2,1)}, bf16[352,1024]{1,0:T(8,128)(2,1)S(1)}, u32[]{:S(2)}, u32[]{:S(2)}) collective-permute-start(bf16[352,1024]{1,0:T(8,128)(2,1)} %get-tuple-element.11.rest_0_), channel_id=1, source_target_pairs={{0,8},{8,0},{16,24},{24,16},{1,9},{9,1},{17,25},{25,17},{2,10},{10... | collective-permute-start | bytes 2162696 | tf_op jit(solution)/shard_map/ppermute | solution.py:209
  27.7 16.3 %collective-permute-done.rest_1_ = bf16[352,1024]{1,0:T(8,128)(2,1)S(1)} collective-permute-done((bf16[352,1024]{1,0:T(8,128)(2,1)}, bf16[352,1024]{1,0:T(8,128)(2,1)S(1)}, u32[]{:S(2)}, u32[]{:S(2)}) %collective-permute-start) | collective-permute-done | bytes 720928 | tf_op jit(solution)/shard_map/ppermute | solution.py:209
  44.1 3.7 %collective-permute-start.1 = (bf16[352,1024]{1,0:T(8,128)(2,1)S(1)}, bf16[352,1024]{1,0:T(8,128)(2,1)S(1)}, u32[]{:S(2)}, u32[]{:S(2)}) collective-permute-start(bf16[352,1024]{1,0:T(8,128)(2,1)S(1)} %collective-permute-done.rest_1_), channel_id=1, source_target_pairs={{0,16},{24,8},{1,17},{25,9},{2,18},{26,10},{3,19},{27,11},{4,20},{... | collective-permute-start | bytes 2162696 | tf_op jit(solution)/shard_map/ppermute | solution.py:210
  47.9 0.1 select_reduce_fusion
  48.0 0.0 copy-start.6
  48.0 0.6 slice.14
  48.6 0.6 slice.15
  49.2 0.7 and_select_fusion.2.base_ref
  49.9 12.4 %collective-permute-done.1.rest_2_ = bf16[352,1024]{1,0:T(8,128)(2,1)S(1)} collective-permute-done((bf16[352,1024]{1,0:T(8,128)(2,1)S(1)}, bf16[352,1024]{1,0:T(8,128)(2,1)S(1)}, u32[]{:S(2)}, u32[]{:S(2)}) %collective-permute-start.1) | collective-permute-done | bytes 720928 | tf_op jit(solution)/shard_map/ppermute | solution.py:210
  62.3 0.8 copy-done.9
  63.1 17.3 %shard_map.119 = bf16[176,1024]{1,0:T(8,128)(2,1)} custom-call(s32[4]{0:T(128)} %bitcast.76, s32[4]{0:T(128)} %bitcast.77, s32[3]{0:T(128)} %and_select_fusion.2.base_ref, s32[1,1024]{1,0:T(1,128)} %bitcast.75, s32[1,1024]{1,0:T(1,128)} %bitcast.73, bf16[176,1024]{1,0:T(8,128)(2,1)} %get-tuple-element.10.q_ref, bf16[352,1024]{1,0:T(8,128)(2,1)} %get-tuple-element.11.rest_0_, ...), custom_call_target="tpu_custom_call" | custom-call | flops 738197504 | bytes 1441792 | tf_op jit(solution)/shard_map/pallas_call | solution.py:155
  80.4 0.0 all-gather.3.cloned.1.call-update
  80.5 0.0 reduce-scatter.2.cloned.1.call-start
  80.5 0.6 broadcast_in_dim.62.gain_ref
  81.1 35.0 %all-gather.3.cloned.1.call-done.blended_ref = bf16[1408,1024]{1,0:T(8,128)(2,1)} async-done(((bf16[176,1024]{1,0:T(8,128)(2,1)}), bf16[1408,1024]{1,0:T(8,128)(2,1)}) %all-gather.3.cloned.1.call-update) | async-done | bytes 2883600 | tf_op jit(solution)/shard_map/all_gather | solution.py:273
  116.1 18.8 %shard_map.120 = (bf16[1024,1408]{1,0:T(8,128)(2,1)}, bf16[1024,1408]{1,0:T(8,128)(2,1)}) custom-call(bf16[1408,1024]{1,0:T(8,128)(2,1)} %all-gather.3.cloned.1.call-done.blended_ref, bf16[1024,1408]{1,0:T(8,128)(2,1)} %get-tuple-element.12.embedded_ref, bf16[1408,1408]{1,0:T(8,128)(2,1)} %out_ref.1, f32[1,1408]{1,0:T(1,128)} %broadcast_in_dim.62.gain_ref, ...), custom_call_target="tpu_custom_call" | custom-call | flops 8489271296 | bytes 19824640 | tf_op jit(solution)/shard_map/pallas_call | solution.py:185
  134.9 0.0 reduce-scatter.2.cloned.1.call-update
  134.9 0.0 all-gather.5.cloned.1.call-start
  135.0 37.7 %reduce-scatter.2.cloned.1.call-done = bf16[128,1408]{1,0:T(8,128)(2,1)} async-done(((bf16[1024,1408]{1,0:T(8,128)(2,1)}), bf16[128,1408]{1,0:T(8,128)(2,1)}) %reduce-scatter.2.cloned.1.call-update) | async-done | bytes 360464 | tf_op jit(solution)/shard_map/reduce_scatter | solution.py:278
  172.7 1.2 add_convert_fusion
  173.9 1.0 reshape.258
  174.9 0.0 all-gather.5.cloned.1.call-update
  175.0 0.0 copy-done.7
  175.0 0.1 select_reduce_fusion.3
  175.1 35.4 %all-gather.5.cloned.1.call-done = bf16[256,5632]{1,0:T(8,128)(2,1)} async-done(((bf16[32,5632]{1,0:T(8,128)(2,1)}), bf16[256,5632]{1,0:T(8,128)(2,1)}) %all-gather.5.cloned.1.call-update) | async-done | bytes 2883600 | tf_op jit(solution)/shard_map/all_gather | solution.py:284
  210.5 5.2 %convolution_convert_fusion = bf16[256,512]{1,0:T(8,128)(2,1)S(1)} fusion(bf16[256,5632]{1,0:T(8,128)(2,1)} %all-gather.5.cloned.1.call-done, bf16[5632,512]{1,0:T(8,128)(2,1)} %param.24), kind=kOutput, calls=%fused_computation.4 | convolution fusion | flops 1476526080 | bytes 8912896 | tf_op jit(solution)/shard_map/dot_general | solution.py:287
  215.7 2.4 %collective-permute-start.4 = (bf16[256,512]{1,0:T(8,128)(2,1)S(1)}, bf16[256,512]{1,0:T(8,128)(2,1)S(1)}, u32[]{:S(2)}, u32[]{:S(2)}) collective-permute-start(bf16[256,512]{1,0:T(8,128)(2,1)S(1)} %convolution_convert_fusion), channel_id=1, source_target_pairs={{0,24},{8,16},{16,8},{24,0},{1,25},{9,17},{17,9},{25,1},{2,26},{10... | collective-permute-start | bytes 786440 | tf_op jit(solution)/shard_map/ppermute | solution.py:296
  218.1 0.6 collective-permute-start.2
  218.7 0.6 collective-permute-start.3
  219.3 0.3 fusion.7
  219.5 6.3 %collective-permute-done.4 = bf16[256,512]{1,0:T(8,128)(2,1)S(1)} collective-permute-done((bf16[256,512]{1,0:T(8,128)(2,1)S(1)}, bf16[256,512]{1,0:T(8,128)(2,1)S(1)}, u32[]{:S(2)}, u32[]{:S(2)}) %collective-permute-start.4) | collective-permute-done | bytes 262176 | tf_op jit(solution)/shard_map/ppermute | solution.py:296
  225.9 0.3 fusion.3
  226.1 4.7 %collective-permute-done.2 = bf16[256,512]{1,0:T(8,128)(2,1)S(1)} collective-permute-done((bf16[256,512]{1,0:T(8,128)(2,1)S(1)}, bf16[256,512]{1,0:T(8,128)(2,1)S(1)}, u32[]{:S(2)}, u32[]{:S(2)}) %collective-permute-start.2) | collective-permute-done | bytes 262176 | tf_op jit(solution)/shard_map/ppermute | solution.py:296
  230.8 0.3 convolution_add_fusion.1
  231.1 0.0 collective-permute-done.3
  231.1 1.0 fusion.2
  (23 shorter events, 0.1 us)
Async XLA Ops:
  6.5 6.3 %copy-start.3 = (f32[1408]{0:T(1024)S(1)}, f32[1408]{0:T(1024)}, u32[]{:S(2)}) copy-start(f32[1408]{0:T(1024)} %param.18) | copy-start | bytes 16900
  6.5 7.5 %copy-start.1 = (bf16[32,1408]{1,0:T(8,128)(2,1)S(1)}, bf16[32,1408]{1,0:T(8,128)(2,1)}, u32[]{:S(2)}) copy-start(bf16[32,1408]{1,0:T(8,128)(2,1)} %param.16) | copy-start | bytes 270340
  6.5 7.5 %copy-start = (bf16[32,1408]{1,0:T(8,128)(2,1)S(1)}, bf16[32,1408]{1,0:T(8,128)(2,1)}, u32[]{:S(2)}) copy-start(bf16[32,1408]{1,0:T(8,128)(2,1)} %param.17) | copy-start | bytes 270340
  6.5 109.6 %all-gather.3.cloned.1.call-start = ((), (), s32[]{:S(2)}) async-start(), calls=%async_computation.1 | async-start | bytes 3244032 | tf_op jit(solution)/shard_map/all_gather | solution.py:273
  14.7 33.1 %copy-start.2 = (s32[32,2]{0,1:T(2,128)S(1)}, s32[32,2]{0,1:T(2,128)}, u32[]{:S(2)}) copy-start(s32[32,2]{0,1:T(2,128)} %param.14) | copy-start | bytes 772
  24.8 55.7 %copy-start.4 = (f32[1408]{0:T(1024)S(1)}, f32[1408]{0:T(1024)}, u32[]{:S(2)}) copy-start(f32[1408]{0:T(1024)} %param.21) | copy-start | bytes 16900
  24.8 19.3 %collective-permute-start = (bf16[352,1024]{1,0:T(8,128)(2,1)}, bf16[352,1024]{1,0:T(8,128)(2,1)S(1)}, u32[]{:S(2)}, u32[]{:S(2)}) collective-permute-start(bf16[352,1024]{1,0:T(8,128)(2,1)} %get-tuple-element.11.rest_0_), channel_id=1, source_target_pairs={{0,8},{8,0},{16,24},{24,16},{1,9},{9,1},{17,25},{25,17},{2,10},{10... | collective-permute-start | bytes 2162696 | tf_op jit(solution)/shard_map/ppermute | solution.py:209
  44.1 18.2 %copy-start.8 = (bf16[352,1024]{1,0:T(8,128)(2,1)}, bf16[352,1024]{1,0:T(8,128)(2,1)S(1)}, u32[]{:S(2)}) copy-start(bf16[352,1024]{1,0:T(8,128)(2,1)S(1)} %collective-permute-done.rest_1_) | copy-start | bytes 2162692
  44.1 18.2 %collective-permute-start.1 = (bf16[352,1024]{1,0:T(8,128)(2,1)S(1)}, bf16[352,1024]{1,0:T(8,128)(2,1)S(1)}, u32[]{:S(2)}, u32[]{:S(2)}) collective-permute-start(bf16[352,1024]{1,0:T(8,128)(2,1)S(1)} %collective-permute-done.rest_1_), channel_id=1, source_target_pairs={{0,16},{24,8},{1,17},{25,9},{2,18},{26,10},{3,19},{27,11},{4,20},{... | collective-permute-start | bytes 2162696 | tf_op jit(solution)/shard_map/ppermute | solution.py:210
  48.0 14.3 %copy-start.5 = (s32[1024]{0:T(1024)}, s32[1024]{0:T(1024)S(1)}, u32[]{:S(2)}) copy-start(s32[1024]{0:T(1024)S(1)} %get-tuple-element.15) | copy-start | bytes 12292
  48.0 14.3 %copy-start.6 = (s32[1024]{0:T(1024)}, s32[1024]{0:T(1024)S(1)}, u32[]{:S(2)}) copy-start(s32[1024]{0:T(1024)S(1)} %get-tuple-element.16) | copy-start | bytes 12292
  62.3 0.9 copy-start.9
  80.5 92.3 %reduce-scatter.2.cloned.1.call-start = ((), (), s32[]{:S(2)}) async-start(), calls=%async_computation.2 | async-start | bytes 3244032 | tf_op jit(solution)/shard_map/reduce_scatter | solution.py:278
  134.9 40.1 %copy-start.7 = (s32[32]{0:T(128)S(1)}, s32[32]{0:T(128)}, u32[]{:S(2)}) copy-start(s32[32]{0:T(128)} %param.15) | copy-start | bytes 388
  134.9 75.6 %all-gather.5.cloned.1.call-start = ((), (), s32[]{:S(2)}) async-start(), calls=%async_computation.3 | async-start | bytes 3244032 | tf_op jit(solution)/shard_map/all_gather | solution.py:284
  215.7 10.2 %collective-permute-start.4 = (bf16[256,512]{1,0:T(8,128)(2,1)S(1)}, bf16[256,512]{1,0:T(8,128)(2,1)S(1)}, u32[]{:S(2)}, u32[]{:S(2)}) collective-permute-start(bf16[256,512]{1,0:T(8,128)(2,1)S(1)} %convolution_convert_fusion), channel_id=1, source_target_pairs={{0,24},{8,16},{16,8},{24,0},{1,25},{9,17},{17,9},{25,1},{2,26},{10... | collective-permute-start | bytes 786440 | tf_op jit(solution)/shard_map/ppermute | solution.py:296
  218.1 12.6 %collective-permute-start.2 = (bf16[256,512]{1,0:T(8,128)(2,1)S(1)}, bf16[256,512]{1,0:T(8,128)(2,1)S(1)}, u32[]{:S(2)}, u32[]{:S(2)}) collective-permute-start(bf16[256,512]{1,0:T(8,128)(2,1)S(1)} %convolution_convert_fusion), channel_id=1, source_target_pairs={{0,8},{8,0},{16,24},{24,16},{1,9},{9,1},{17,25},{25,17},{2,10},{10... | collective-permute-start | bytes 786440 | tf_op jit(solution)/shard_map/ppermute | solution.py:296
  218.7 12.4 %collective-permute-start.3 = (bf16[256,512]{1,0:T(8,128)(2,1)S(1)}, bf16[256,512]{1,0:T(8,128)(2,1)S(1)}, u32[]{:S(2)}, u32[]{:S(2)}) collective-permute-start(bf16[256,512]{1,0:T(8,128)(2,1)S(1)} %convolution_convert_fusion), channel_id=1, source_target_pairs={{0,16},{8,24},{16,0},{24,8},{1,17},{9,25},{17,1},{25,9},{2,18},{10... | collective-permute-start | bytes 786440 | tf_op jit(solution)/shard_map/ppermute | solution.py:296
Sparse Core Ops, SparseCore 0:
  80.6 35.4 all-gather.2
  135.0 37.6 reduce-scatter.1
  175.0 35.4 all-gather.4

commit v2 on v1

v2 whole, which is shorter than its diff:
```python
import functools
import math

import jax
import jax.numpy as jnp
from jax import lax
from jax.experimental import pallas as pl
from jax.experimental.pallas import tpu as pltpu
from jax.sharding import PartitionSpec as P

HEAD_DIM = 88
TILE = 256
LANES = 128
LOW = -1e30
VMEM_LIMIT = 58 * 1024 * 1024
SHARED_VMEM = 24 * 1024 * 1024
ADD_VMEM = 8 * 1024 * 1024

NT = (((1,), (1,)), ((), ()))
TN = (((0,), (0,)), ((), ()))
TT = (((0,), (1,)), ((), ()))


def dot(left, right, dims=(((1,), (0,)), ((), ()))):
    return lax.dot_general(left, right, dims, preferred_element_type=jnp.float32)


def norm_rows(widened, gain_row):
    centered = widened - jnp.mean(widened, axis=-1, keepdims=True)
    variance = jnp.mean(centered * centered, axis=-1, keepdims=True)
    return centered * lax.rsqrt(variance + 1e-06) * gain_row


def whole(shape):
    return pl.BlockSpec(shape, lambda *_: (0,) * len(shape))


def project_kernel(
    base_ref, grid_ref, patches_ref, row_ref, col_ref, gain_ref, weight_ref, embedded_ref, q_ref, *kv_refs
):
    rows = patches_ref.shape[0]
    requests = grid_ref.shape[1]
    across = grid_ref[1:2, :] // 2
    cells = (grid_ref[0:1, :] // 2) * across
    before = lax.broadcasted_iota(jnp.int32, (requests, requests), 0)
    after = lax.broadcasted_iota(jnp.int32, (requests, requests), 1)
    earlier = jnp.where(before < after, 1.0, 0.0).astype(jnp.bfloat16)
    wide = jnp.broadcast_to(cells.astype(jnp.float32), (8, requests)).astype(jnp.bfloat16)
    starts = 4 * dot(wide, earlier)[0:1, :].astype(jnp.int32)
    index = base_ref[0] + pl.program_id(0) * rows
    index = index + lax.broadcasted_iota(jnp.int32, (rows, requests), 0)
    inside = (index >= starts) & (index < starts + 4 * cells)
    offset = jnp.sum(jnp.where(inside, index - starts, 0), axis=1, keepdims=True)
    cells_across = jnp.sum(jnp.where(inside, across, 0), axis=1, keepdims=True)
    shift = jnp.where(cells_across == 16, 4, jnp.where(cells_across == 8, 3, 2))
    block = offset >> 2
    corner = offset & 3
    row_place = 2 * (block >> shift) + (corner >> 1)
    col_place = 2 * (block & (cells_across - 1)) + (corner & 1)
    lane = lax.broadcasted_iota(jnp.int32, (rows, row_ref.shape[0]), 1)
    pick_row = jnp.where(lane == row_place, 1.0, 0.0).astype(jnp.bfloat16)
    pick_col = jnp.where(lane == col_place, 1.0, 0.0).astype(jnp.bfloat16)
    embedded = (
        patches_ref[...].astype(jnp.float32)
        + dot(pick_row, row_ref[...])
        + dot(pick_col, col_ref[...])
    ).astype(jnp.bfloat16)
    embedded_ref[...] = embedded
    normed = norm_rows(embedded.astype(jnp.float32), gain_ref[...]).astype(jnp.bfloat16)
    projected = dot(weight_ref[...], normed, NT).astype(jnp.bfloat16)
    width = q_ref.shape[0]
    q_ref[...] = projected[0:width]
    key_rows = projected[width : 2 * width]
    value_rows = projected[2 * width : 3 * width]
    for head, kv_ref in enumerate(kv_refs):
        span = slice(head * HEAD_DIM, (head + 1) * HEAD_DIM)
        kv_ref[0:HEAD_DIM, :] = key_rows[span]
        kv_ref[HEAD_DIM : 2 * HEAD_DIM, :] = value_rows[span]


def project(base, grid, patches, row_table, col_table, gain, weight):
    rows, model = patches.shape
    width = weight.shape[0] // 3
    return pl.pallas_call(
        project_kernel,
        grid_spec=pltpu.PrefetchScalarGridSpec(
            num_scalar_prefetch=1,
            grid=(rows // TILE,),
            in_specs=[
                whole(grid.shape),
                pl.BlockSpec((TILE, model), lambda i, _: (i, 0)),
                whole(row_table.shape),
                whole(col_table.shape),
                whole(gain.shape),
                whole(weight.shape),
            ],
            out_specs=[
                pl.BlockSpec((TILE, model), lambda i, _: (i, 0)),
                pl.BlockSpec((width, TILE), lambda i, _: (0, i)),
            ]
            + [pl.BlockSpec((2 * HEAD_DIM, TILE), lambda i, _: (0, i))] * (width // HEAD_DIM),
        ),
        out_shape=[
            jax.ShapeDtypeStruct((rows, model), jnp.bfloat16),
            jax.ShapeDtypeStruct((width, rows), jnp.bfloat16),
        ]
        + [jax.ShapeDtypeStruct((2 * HEAD_DIM, rows), jnp.bfloat16)] * (width // HEAD_DIM),
        compiler_params=pltpu.CompilerParams(vmem_limit_bytes=VMEM_LIMIT),
        cost_estimate=pl.CostEstimate(
            flops=6 * rows * model * width, bytes_accessed=4 * rows * model, transcendentals=0
        ),
    )(base, grid, patches, row_table, col_table, gain, weight)


def attend_kernel(taken, low_ref, high_ref, base_ref, start_ref, end_ref, q_ref, *rest):
    states, rest = rest[:taken], rest[taken:]
    count = len(rest) - (1 if taken else 3)
    parts, outs = rest[:count], rest[count:]
    rows = q_ref.shape[1]
    scale = math.log2(math.e) / math.sqrt(HEAD_DIM)
    for tile in range(rows // TILE):
        span = slice(tile * TILE, (tile + 1) * TILE)
        start = start_ref[:, span]
        end = end_ref[:, span]
        low = low_ref[tile]
        high = high_ref[tile]
        queries = q_ref[:, span]
        if taken:
            carry = tuple(state[:, span] for state in states)
        else:
            carry = (
                jnp.full((1, TILE), LOW, jnp.float32),
                jnp.zeros((1, TILE), jnp.float32),
                jnp.zeros((HEAD_DIM, TILE), jnp.float32),
            )
        for number, part in enumerate(parts):
            base = base_ref[number]
            tiles = part.shape[1] // TILE
            first = jnp.clip((low - base) // TILE, 0, tiles)
            last = jnp.clip((high - base + TILE - 1) // TILE, 0, tiles)

            def step(place, carry, part=part, base=base, queries=queries, start=start, end=end):
                where = pl.ds(pl.multiple_of(place * TILE, TILE), TILE)
                index = base + place * TILE + lax.broadcasted_iota(jnp.int32, (TILE, TILE), 0)
                allowed = (index >= start) & (index < end)
                top, total, acc = carry
                scores = dot(part[0:HEAD_DIM, where], queries, TN) * scale
                scores = jnp.where(allowed, scores, LOW)
                higher = jnp.maximum(top, jnp.max(scores, axis=0, keepdims=True))
                weights = jnp.exp2(scores - higher)
                fade = jnp.exp2(top - higher)
                total = total * fade + jnp.sum(weights, axis=0, keepdims=True)
                value_rows = part[HEAD_DIM : 2 * HEAD_DIM, where]
                acc = acc * fade + dot(value_rows, weights.astype(jnp.bfloat16))
                return higher, total, acc

            carry = lax.fori_loop(first, last, step, carry)
        if taken:
            _, total, acc = carry
            outs[0][:, span] = (acc / total).astype(jnp.bfloat16)
        else:
            for out, value in zip(outs, carry):
                out[:, span] = value


def attend(head, low, high, bases, start, end, queries, states, parts):
    rows = queries.shape[1]
    smem = pl.BlockSpec(memory_space=pltpu.SMEM)
    if states:
        shapes = [jax.ShapeDtypeStruct((HEAD_DIM, rows), jnp.bfloat16)]
    else:
        shapes = [
            jax.ShapeDtypeStruct((height, rows), jnp.float32) for height in (1, 1, HEAD_DIM)
        ]
    return pl.pallas_call(
        functools.partial(attend_kernel, len(states)),
        grid=(1,),
        in_specs=[smem] * 3
        + [whole(start.shape), whole(end.shape)]
        + [pl.BlockSpec((HEAD_DIM, rows), lambda i: (head, 0))]
        + [whole(value.shape) for value in (*states, *parts)],
        out_specs=[whole(x.shape) for x in shapes],
        out_shape=shapes,
        compiler_params=pltpu.CompilerParams(vmem_limit_bytes=VMEM_LIMIT),
        cost_estimate=pl.CostEstimate(
            flops=4 * rows * rows * HEAD_DIM,
            bytes_accessed=8 * rows * HEAD_DIM,
            transcendentals=rows * rows,
        ),
    )(low, high, bases, start, end, queries, *states, *parts)


def mlp_kernel(last, place_ref, *refs):
    blocks, refs = refs[:8], refs[8:]
    embedded_ref, gain_ref, *held = refs[:5]
    kept_ref, sent_ref = refs[5:7]
    blended_ref = refs[-1]
    height, core = place_ref[0], place_ref[1]
    width = blocks[0].shape[0]
    for k in range(4):
        for side in range(2):
            source = 2 * (height ^ k) + (core if side == 0 else 1 - core)
            blended_ref[pl.ds(pl.multiple_of(source * width, 16), width), :] = blocks[
                4 * side + k
            ][...]
    attended = dot(blended_ref[...], held[0][...], TN)
    residual = (embedded_ref[...].astype(jnp.float32) + attended).astype(jnp.bfloat16)
    rows = residual.shape[0] // 2
    normed = norm_rows(residual.astype(jnp.float32), gain_ref[...]).astype(jnp.bfloat16)
    lifted = dot(normed, held[1][...])
    activated = (0.5 * lifted * (1.0 + lax.erf(lifted * math.sqrt(0.5)))).astype(jnp.bfloat16)
    partial = dot(activated, held[2][...]).astype(jnp.bfloat16)
    for side in range(2):

        @pl.when(core == side)
        def _(side=side):
            mine = slice(side * rows, (side + 1) * rows)
            other = slice((1 - side) * rows, (2 - side) * rows)
            kept_ref[...] = partial[mine]
            sent_ref[...] = partial[other]
            if last:
                refs[7][...] = residual[mine]


def mlp(distance, place, blocks, embedded, out_weight, gain, up_weight, down_weight):
    model = embedded.shape[1]
    width = blocks[0].shape[0]
    rows = blocks[0].shape[1] // 4
    hidden = up_weight.shape[1]
    stored = (out_weight, up_weight, down_weight)
    resident = pl.BlockSpec(memory_space=pltpu.VMEM)
    last = distance == 0
    shapes = [jax.ShapeDtypeStruct((rows // 2, model), jnp.bfloat16)] * (3 if last else 2)
    return pl.pallas_call(
        functools.partial(mlp_kernel, last),
        grid_spec=pltpu.PrefetchScalarGridSpec(
            num_scalar_prefetch=1,
            grid=(1,),
            in_specs=[pl.BlockSpec((width, rows), lambda i, p: (0, p[0] ^ distance))] * 8
            + [
                pl.BlockSpec((rows, model), lambda i, p: (p[0] ^ distance, 0)),
                whole(gain.shape),
            ]
            + [resident] * 3,
            out_specs=[whole(x.shape) for x in shapes],
            scratch_shapes=[pltpu.VMEM((8 * width, rows), jnp.bfloat16)],
        ),
        out_shape=shapes,
        compiler_params=pltpu.CompilerParams(vmem_limit_bytes=SHARED_VMEM),
        cost_estimate=pl.CostEstimate(
            flops=2 * rows * model * (model + 2 * hidden),
            bytes_accessed=2 * (4 * rows * model + model * (model + 2 * hidden)),
            transcendentals=rows * hidden,
        ),
    )(place, *blocks, embedded, gain, *stored)


def add_kernel(*refs):
    total = refs[0][...].astype(jnp.float32)
    for ref in refs[1:-1]:
        total = total + ref[...].astype(jnp.float32)
    refs[-1][...] = total.astype(jnp.bfloat16)


def add(*terms):
    shape = terms[0].shape
    return pl.pallas_call(
        add_kernel,
        grid=(1,),
        in_specs=[whole(shape)] * len(terms),
        out_specs=whole(shape),
        out_shape=jax.ShapeDtypeStruct(shape, jnp.bfloat16),
        compiler_params=pltpu.CompilerParams(vmem_limit_bytes=ADD_VMEM),
        cost_estimate=pl.CostEstimate(
            flops=len(terms) * math.prod(shape),
            bytes_accessed=2 * (len(terms) + 1) * math.prod(shape),
            transcendentals=0,
        ),
    )(*terms)


def after(value, mark):
    return lax.optimization_barrier((value, mark))[0]


def along_hid(value, pairs):
    return lax.ppermute(
        value, "hid", [(2 * a + core, 2 * b + core) for a, b in pairs for core in range(2)]
    )


def swap_core(value):
    return lax.ppermute(value, "hid", [(i, i ^ 1) for i in range(8)])


NEXT = [(0, 1), (1, 0), (2, 3), (3, 2)]
SECOND = [(0, 2), (2, 0), (1, 3), (3, 1)]
MIDDLE = [(1, 2), (2, 1)]
OUTWARD = [(1, 0), (2, 3)]
INWARD = [(0, 1), (3, 2)]


def gather_line(value):
    second = along_hid(value, SECOND)
    first = along_hid(value, NEXT)
    outward = along_hid(second, OUTWARD)
    third = add(along_hid(after(value, second), MIDDLE), outward)
    return [value, first, second, third]


def across_keys(keys, bands):
    if bands == 4:
        return lax.ppermute(keys, "req", [(0, 1), (1, 0), (2, 3), (3, 2)])
    return lax.ppermute(keys, "req", [(i, i + 1) for i in range(bands - 1)])


def along_keys(keys, across, bands):
    if bands == 4:
        return lax.ppermute(across, "req", [(0, 2), (3, 1)])
    return lax.ppermute(keys, "req", [(i + 1, i) for i in range(bands - 1)])


def neighbour_bands(band, bands):
    if bands == 4:
        even = band % 2 == 0
        return jnp.where(even, band + 1, band - 1), jnp.where(even, band - 1, band + 1)
    return band - 1, band + 1


def on_device(
    patches,
    segments,
    grid_sizes,
    owners,
    row_table,
    col_table,
    gain_attn,
    qkv_weight,
    out_weight,
    gain_mlp,
    up_weight,
    down_weight,
    merge_weight,
):
    rows, model = patches.shape
    bands = lax.axis_size("req")
    band = lax.axis_index("req")
    part_count = lax.axis_size("hid")
    requests = grid_sizes.shape[0]

    cells_across = grid_sizes[:, 1] // 2
    cell_count = grid_sizes[:, 0] // 2 * cells_across
    ordinal = jnp.arange(requests, dtype=jnp.int32)
    earlier = ordinal[None, :] < ordinal[:, None]
    cell_start = jnp.sum(jnp.where(earlier, cell_count[None, :], 0), axis=1)
    cell_end = cell_start + cell_count
    same_owner = earlier & (owners[:, None] == owners[None, :])
    preceding = jnp.sum(jnp.where(same_owner, cell_count[None, :], 0), axis=1)

    base = (band * rows).astype(jnp.int32)
    embedded, queries, *keys = project(
        base[None],
        grid_sizes.T,
        patches,
        row_table,
        col_table,
        gain_attn[None, :],
        jnp.swapaxes(qkv_weight, 1, 2).reshape(-1, model),
    )

    patch_index = base + jnp.arange(rows, dtype=jnp.int32)
    mine = (4 * cell_start[:, None] <= patch_index[None, :]) & (
        patch_index[None, :] < 4 * cell_end[:, None]
    )
    start = jnp.sum(jnp.where(mine, 4 * cell_start[:, None], 0), axis=0, keepdims=True)
    end = jnp.sum(jnp.where(mine, 4 * cell_end[:, None], 0), axis=0, keepdims=True)
    low = start[0, ::TILE]
    high = end[0, TILE - 1 :: TILE]
    beyond = 1 << 28
    part_bands = jnp.stack(neighbour_bands(band, bands))
    bases = jnp.where((part_bands >= 0) & (part_bands < bands), part_bands * rows, beyond)
    near = [across_keys(own, bands) for own in keys]
    far, states = [], []
    own_base = base[None]
    for head, own in enumerate(keys):
        states.append(attend(head, low, high, own_base, start, end, queries, (), (own,)))
        near[head] = after(near[head], states[head][0])
        far.append(along_keys(own, near[head], bands))
        own_base = after(own_base, near[head])
    heads_blended = []
    for head in range(len(keys)):
        heads_blended += attend(
            head, low, high, bases, start, end, queries, states[head], (near[head], far[head])
        )

    member = lax.axis_index("hid")
    height, core = member // 2, member % 2
    place = jnp.stack([height, core]).astype(jnp.int32)
    home_cells = rows // (4 * part_count)
    merged_rows = rows // 4
    slots = jnp.arange(merged_rows, dtype=jnp.int32)

    blocks = gather_line(jnp.concatenate(heads_blended, axis=0))
    blocks = blocks + [swap_core(block) for block in blocks]
    rest = (blocks, embedded, out_weight, gain_mlp[None, :], up_weight, down_weight)

    kept, sent = mlp(3, place, *rest)
    third = add(kept, swap_core(sent))
    inward = along_hid(third, INWARD)
    middle = along_hid(third, MIDDLE)
    kept, sent = mlp(2, place, *rest)
    moved = swap_core(sent)
    kept_first, sent_first = mlp(1, after(place, third), *rest)
    second = add(kept, moved, inward)
    kept, sent, residual = mlp(0, after(place, second), *rest)
    first = add(kept_first, swap_core(sent_first))
    second = along_hid(second, SECOND)
    first = along_hid(first, NEXT)
    total = residual.astype(jnp.float32)
    for piece in (kept, swap_core(sent), middle, first, second):
        total = total + piece.astype(jnp.float32)
    output_rows = total.astype(jnp.bfloat16).reshape(home_cells, 4 * model)

    merged = gather_line(output_rows)
    returned = jnp.zeros((merged_rows, merge_weight.shape[1]), jnp.float32)
    projected = None
    for distances in ((0, 1, 2), (3,)):
        mine = [merged[k] for k in distances]
        if projected is not None:
            mine[-1] = after(mine[-1], projected)
        mine = mine + [swap_core(block) for block in mine]
        projected = jnp.dot(
            jnp.concatenate(mine, axis=0), merge_weight, preferred_element_type=jnp.float32
        ).astype(jnp.bfloat16)
        homes = jnp.stack(
            [2 * (height ^ k) + side for side in (core, 1 - core) for k in distances]
        )
        local = (
            homes[:, None] * home_cells + jnp.arange(home_cells, dtype=jnp.int32)[None, :]
        ).reshape(-1)
        if bands == 4:
            shifts = (3, 1, 2)
            pieces = [
                (lax.ppermute(projected, "req", [(i, i ^ shift) for i in range(4)]), band ^ shift)
                for shift in shifts
            ]
            pieces.append((projected, band))
            pieces = [(piece, piece_band * merged_rows + local) for piece, piece_band in pieces]
        else:
            every = jnp.arange(bands, dtype=jnp.int32)[:, None] * merged_rows + local[None, :]
            pieces = [(lax.all_gather(projected, "req", axis=0, tiled=True), every.reshape(-1))]
        for piece, merged_index in pieces:
            holding = (cell_start[None, :] <= merged_index[:, None]) & (
                merged_index[:, None] < cell_end[None, :]
            )
            holding = holding & (owners == band)[None, :]
            target = jnp.sum(
                jnp.where(holding, merged_index[:, None] + (preceding - cell_start)[None, :] + 1, 0),
                axis=1,
            )
            chosen = (target[None, :] == slots[:, None] + 1).astype(jnp.bfloat16)
            returned = returned + jnp.dot(chosen, piece, preferred_element_type=jnp.float32)
    return returned.astype(jnp.bfloat16)[None]


def solution(mesh):
    return jax.shard_map(
        on_device,
        mesh=mesh,
        in_specs=(
            P("req", None),
            P("req"),
            P(),
            P(),
            P(),
            P(),
            P(),
            P(None, None, "hid"),
            P(),
            P(),
            P(None, "hid"),
            P("hid", None),
            P(None, "hid"),
        ),
        out_specs=P("req", None, "hid"),
        check_vma=False,
    )
```

time: 240 us -> 195 us (0.81)
  waiting for transfers between devices: 148 us -> 73.2 us
  starting transfers between devices: 10.3 us -> 35.9 us
  Pallas kernels: 46.2 us -> 61.6 us
  between operations: 13.3 us -> 0.43 us
  local copies, waits for them, and re-layouts: 8.65 us -> 11.3 us
    all_gather x2 -> x0, waiting for transfers between devices: 70.4 us -> none  [the longest x1 35.4 us: on_device(): lax.all_gather(output_rows.reshape(home_rows // 4, 4 * model), 'hid', axi...]
    reduce_scatter x1 -> x0, waiting for transfers between devices: 37.7 us -> none  [on_device(): lax.psum_scatter(partial_sum, 'hid', scatter_dimension=0, tiled=True)]
    ppermute x2 -> x28, waiting for transfers between devices: 28.7 us -> 62.3 us  [the longest x12 50.9 us: along_hid(): lax.ppermute(value, 'hid', [(2 * a + core, 2 * b + core) for a, b in pair...]
    ppermute x2 -> x28, starting transfers between devices: 6.65 us -> 28.1 us  [the longest x12 19.8 us: along_hid(): lax.ppermute(value, 'hid', [(2 * a + core, 2 * b + core) for a, b in pair...]
    pallas_call x2 -> x13, Pallas kernels: 36.1 us -> 51.9 us  [the longest x4 26.2 us: attend(): pl.pallas_call(functools.partial(attend_kernel, len(states)), grid=(1,),...]
    ppermute x3 -> x6, starting transfers between devices: 3.55 us -> 7.75 us  [on_device(): lax.ppermute(projected, 'req', [(i, i ^ shift) for i in range(4)])]
    unnamed x21 -> x37, local copies, waits for them, and re-layouts: 4.69 us -> 7.77 us
    ppermute x3 -> x6, waiting for transfers between devices: 11 us -> 10.9 us  [on_device(): lax.ppermute(projected, 'req', [(i, i ^ shift) for i in range(4)])]
  transfers between devices with their start and end apart: 8 -> 34, of which waited for: 7 -> 15; matrix products, arithmetic and copies ran while one was open for 1% -> 5% of each run, Pallas kernels for 0% -> 22%
where the time goes in v2:
time: 195 us
  waiting for transfers between devices  73.2 us (38%)
  Pallas kernels  61.6 us (32%)
  starting transfers between devices  35.9 us (18%)
  local copies, waits for them, and re-layouts  11.3 us (6%)
  matrix products  8.06 us (4%)
  other arithmetic  4.21 us (2%)
    ppermute x12, waiting for transfers between devices, along_hid(): lax.ppermute(value, 'hid', [(2 * a + core, 2 * b + core) for a, b in pair...  50.9 us
    pallas_call x4, Pallas kernels, attend(): pl.pallas_call(functools.partial(attend_kernel, len(states)), grid=(1,),...  26.2 us
    pallas_call x4, Pallas kernels, mlp(): pl.pallas_call(functools.partial(mlp_kernel, last), grid_spec=pltpu.Prefe...  22.3 us
    ppermute x12, starting transfers between devices, along_hid(): lax.ppermute(value, 'hid', [(2 * a + core, 2 * b + core) for a, b in pair...  19.8 us
    ppermute x6, waiting for transfers between devices, on_device(): lax.ppermute(projected, 'req', [(i, i ^ shift) for i in range(4)])  10.9 us
    pallas_call x1, Pallas kernels, project(): pl.pallas_call(project_kernel, grid_spec=pltpu.PrefetchScalarGridSpec(num...  9.66 us
    ppermute x2, waiting for transfers between devices, along_keys(): return lax.ppermute(across, 'req', [(0, 2), (3, 1)])  8.02 us
    unnamed x37, local copies, waits for them, and re-layouts  7.77 us
  transfers between devices with their start and end apart: 34, of which 15 were waited for; matrix products, arithmetic and copies ran while one was open for 5% of the time, Pallas kernels for 22%

profile of v2, /device:TPU:0, one launch (start us, length us, event | category | flops | bytes accessed | tf_op | source)
XLA Modules:
  0.0 194.7 jit_solution(703676801996540260)
XLA Ops:
  0.0 1.3 broadcast_in_dim.67.gain_ref
  1.3 9.7 %shard_map.118 = (bf16[1024,1408]{1,0:T(8,128)(2,1)}, bf16[176,1024]{1,0:T(8,128)(2,1)}, bf16[176,1024]{1,0:T(8,128)(2,1)}, bf16[176,1024]{1,0:T(8,128)(2,1)}) custom-call(s32[1]{0:T(128)} %bitcast.18.base_ref, s32[2,32]{1,0:T(2,128)} %bitcast.68, bf16[1024,1408]{1,0:T(8,128)(2,1)} %patches_ref.1, bf16[32,1408]{1,0:T(8,128)(2,1)} %row_ref.1, ...), custom_call_target="tpu_custom_call" | custom-call | flops 1522532352 | bytes 5767168 | tf_op jit(solution)/shard_map/pallas_call | solution.py:84
  11.0 2.9 %collective-permute-start = (bf16[176,1024]{1,0:T(8,128)(2,1)}, bf16[176,1024]{1,0:T(8,128)(2,1)S(1)}, u32[]{:S(2)}, u32[]{:S(2)}) collective-permute-start(bf16[176,1024]{1,0:T(8,128)(2,1)} %get-tuple-element.33.rest_0_), channel_id=1, source_target_pairs={{0,8},{8,0},{16,24},{24,16},{1,9},{9,1},{17,25},{25,17},{2,10},{10... | collective-permute-start | bytes 1081352 | tf_op jit(solution)/shard_map/ppermute | solution.py:313
  15.6 9.1 %shard_map.119 = (f32[1,1024]{1,0:T(1,128)}, f32[1,1024]{1,0:T(1,128)}, f32[88,1024]{1,0:T(8,128)}) custom-call(s32[4]{0:T(128)} %bitcast.80, s32[4]{0:T(128)} %bitcast.84, s32[1]{0:T(128)} %bitcast.18.base_ref, s32[1,1024]{1,0:T(1,128)} %bitcast.75, s32[1,1024]{1,0:T(1,128)} %bitcast.70, bf16[176,1024]{1,0:T(8,128)(2,1)} %get-tuple-element.32.q_ref, ...), custom_call_target="tpu_custom_call" | custom-call | flops 369098752 | bytes 720896 | tf_op jit(solution)/shard_map/pallas_call | solution.py:175
  24.7 9.3 %shard_map.121 = (f32[1,1024]{1,0:T(1,128)}, f32[1,1024]{1,0:T(1,128)}, f32[88,1024]{1,0:T(8,128)}) custom-call(s32[4]{0:T(128)} %bitcast.81, s32[4]{0:T(128)} %bitcast.85, s32[1]{0:T(128)} %bitcast.18.base_ref, s32[1,1024]{1,0:T(1,128)} %bitcast.76, s32[1,1024]{1,0:T(1,128)} %bitcast.71, bf16[176,1024]{1,0:T(8,128)(2,1)} %get-tuple-element.32.q_ref, ...), custom_call_target="tpu_custom_call" | custom-call | flops 369098752 | bytes 720896 | tf_op jit(solution)/shard_map/pallas_call | solution.py:175
  34.0 1.3 collective-permute-start.3
  35.4 2.0 %collective-permute-start.1 = (bf16[176,1024]{1,0:T(8,128)(2,1)S(1)}, bf16[176,1024]{1,0:T(8,128)(2,1)}, u32[]{:S(2)}, u32[]{:S(2)}) collective-permute-start(bf16[176,1024]{1,0:T(8,128)(2,1)S(1)} %collective-permute-done.rest_3_), channel_id=1, source_target_pairs={{0,16},{24,8},{1,17},{25,9},{2,18},{26,10},{3,19},{27,11},{4,20},{... | collective-permute-start | bytes 1081352 | tf_op jit(solution)/shard_map/ppermute | solution.py:319
  38.0 6.1 %collective-permute-done.3.rest_4_ = bf16[176,1024]{1,0:T(8,128)(2,1)S(1)} collective-permute-done((bf16[176,1024]{1,0:T(8,128)(2,1)S(1)}, bf16[176,1024]{1,0:T(8,128)(2,1)S(1)}, u32[]{:S(2)}, u32[]{:S(2)}) %collective-permute-start.3) | collective-permute-done | bytes 360480 | tf_op jit(solution)/shard_map/ppermute | solution.py:319
  44.9 3.9 %shard_map.122 = bf16[88,1024]{1,0:T(8,128)(2,1)} custom-call(s32[4]{0:T(128)} %bitcast.82, s32[4]{0:T(128)} %bitcast.86, s32[2]{0:T(128)} %and_select_fusion.base_ref, s32[1,1024]{1,0:T(1,128)} %bitcast.77, s32[1,1024]{1,0:T(1,128)} %bitcast.72, bf16[176,1024]{1,0:T(8,128)(2,1)} %get-tuple-element.32.q_ref, f32[1,1024]{1,0:T(1,128)} %get-tuple-element.40.rest_0_, ...), custom_call_target="tpu_custom_call" | custom-call | flops 369098752 | bytes 720896 | tf_op jit(solution)/shard_map/pallas_call | solution.py:175
  48.8 1.9 collective-permute-done.1.rest_4_
  50.7 3.9 %shard_map.120 = bf16[88,1024]{1,0:T(8,128)(2,1)} custom-call(s32[4]{0:T(128)} %bitcast.83, s32[4]{0:T(128)} %bitcast.87, s32[2]{0:T(128)} %and_select_fusion.base_ref, s32[1,1024]{1,0:T(1,128)} %bitcast.78, s32[1,1024]{1,0:T(1,128)} %bitcast.73, bf16[176,1024]{1,0:T(8,128)(2,1)} %get-tuple-element.32.q_ref, f32[1,1024]{1,0:T(1,128)} %get-tuple-element.34.rest_0_, ...), custom_call_target="tpu_custom_call" | custom-call | flops 369098752 | bytes 720896 | tf_op jit(solution)/shard_map/pallas_call | solution.py:175
  54.6 1.0 pad_maximum_fusion.refs_0_
  55.7 2.8 %collective-permute-start.5 = (bf16[176,1024]{1,0:T(8,128)(2,1)S(1)}, bf16[176,1024]{1,0:T(8,128)(2,1)}, u32[]{:S(2)}, u32[]{:S(2)}) collective-permute-start(bf16[176,1024]{1,0:T(8,128)(2,1)S(1)} %pad_maximum_fusion.refs_0_), channel_id=1, source_target_pairs={{0,4},{1,5},{4,0},{5,1},{2,6},{3,7},{6,2},{7,3},{8,12},{9,13},{12,... | collective-permute-start | bytes 1081352 | tf_op jit(solution)/shard_map/ppermute | solution.py:287
  58.5 1.6 collective-permute-start.4
  60.1 13.8 %collective-permute-done.5.refs_2_ = bf16[176,1024]{1,0:T(8,128)(2,1)} collective-permute-done((bf16[176,1024]{1,0:T(8,128)(2,1)S(1)}, bf16[176,1024]{1,0:T(8,128)(2,1)}, u32[]{:S(2)}, u32[]{:S(2)}) %collective-permute-start.5) | collective-permute-done | bytes 360480 | tf_op jit(solution)/shard_map/ppermute | solution.py:287
  74.5 1.3 collective-permute-start.7
  76.5 9.6 %collective-permute-done.7.refs_1_ = bf16[176,1024]{1,0:T(8,128)(2,1)S(1)} collective-permute-done((bf16[176,1024]{1,0:T(8,128)(2,1)}, bf16[176,1024]{1,0:T(8,128)(2,1)S(1)}, u32[]{:S(2)}, u32[]{:S(2)}) %collective-permute-start.7) | collective-permute-done | bytes 360480 | tf_op jit(solution)/shard_map/ppermute | solution.py:287
  87.2 1.7 collective-permute-done.11.refs_7_
  89.0 2.1 %copy-done = bf16[1408,1408]{1,0:T(8,128)(2,1)S(1)} copy-done((bf16[1408,1408]{1,0:T(8,128)(2,1)S(1)}, bf16[1408,1408]{1,0:T(8,128)(2,1)}, u32[]{:S(2)}) %copy-start) | copy-done | bytes 3964952
  91.1 1.6 copy-done.2
  92.7 1.6 copy-done.3
  94.3 5.5 %shard_map.125 = (bf16[128,1408]{1,0:T(8,128)(2,1)S(1)}, bf16[128,1408]{1,0:T(8,128)(2,1)S(1)}) custom-call(s32[2]{0:T(128)S(1)} %pad_add_fusion.place_ref, bf16[176,1024]{1,0:T(8,128)(2,1)S(1)} %pad_maximum_fusion.refs_0_, bf16[176,1024]{1,0:T(8,128)(2,1)} %collective-permute-done.4.refs_1_, bf16[176,1024]{1,0:T(8,128)(2,1)} %collective-permute-done.5.refs_2_, ...), custom_call_target="tpu_custom_call" | custom-call | flops 2122317824 | bytes 11173888 | tf_op jit(solution)/shard_map/pallas_call | solution.py:234
  100.1 5.3 %shard_map.124 = (bf16[128,1408]{1,0:T(8,128)(2,1)S(1)}, bf16[128,1408]{1,0:T(8,128)(2,1)S(1)}) custom-call(s32[2]{0:T(128)S(1)} %pad_add_fusion.place_ref, bf16[176,1024]{1,0:T(8,128)(2,1)S(1)} %pad_maximum_fusion.refs_0_, bf16[176,1024]{1,0:T(8,128)(2,1)} %collective-permute-done.4.refs_1_, bf16[176,1024]{1,0:T(8,128)(2,1)} %collective-permute-done.5.refs_2_, ...), custom_call_target="tpu_custom_call" | custom-call | flops 2122317824 | bytes 11173888 | tf_op jit(solution)/shard_map/pallas_call | solution.py:234
  106.7 2.1 %collective-permute-start.14 = (bf16[128,1408]{1,0:T(8,128)(2,1)}, bf16[128,1408]{1,0:T(8,128)(2,1)S(1)}, u32[]{:S(2)}, u32[]{:S(2)}) collective-permute-start(bf16[128,1408]{1,0:T(8,128)(2,1)} %shard_map.126), channel_id=1, source_target_pairs={{0,2},{1,3},{6,4},{7,5},{8,10},{9,11},{14,12},{15,13},{16,18},{17,... | collective-permute-start | bytes 1081352 | tf_op jit(solution)/shard_map/ppermute | solution.py:287
  108.9 5.3 %shard_map.129 = (bf16[128,1408]{1,0:T(8,128)(2,1)S(1)}, bf16[128,1408]{1,0:T(8,128)(2,1)S(1)}) custom-call(s32[2]{0:T(128)S(1)} %pad_add_fusion.place_ref, bf16[176,1024]{1,0:T(8,128)(2,1)S(1)} %pad_maximum_fusion.refs_0_, bf16[176,1024]{1,0:T(8,128)(2,1)} %collective-permute-done.4.refs_1_, bf16[176,1024]{1,0:T(8,128)(2,1)} %collective-permute-done.5.refs_2_, ...), custom_call_target="tpu_custom_call" | custom-call | flops 2122317824 | bytes 11173888 | tf_op jit(solution)/shard_map/pallas_call | solution.py:234
  114.4 1.4 collective-permute-start.16
  115.8 1.3 collective-permute-done.14.refs_2_
  117.1 0.9 shard_map.127
  118.0 4.4 %collective-permute-start.19 = (bf16[128,1408]{1,0:T(8,128)(2,1)}, bf16[128,1408]{1,0:T(8,128)(2,1)}, u32[]{:S(2)}, u32[]{:S(2)}) collective-permute-start(bf16[128,1408]{1,0:T(8,128)(2,1)} %shard_map.127), channel_id=1, source_target_pairs={{0,4},{1,5},{4,0},{5,1},{2,6},{3,7},{6,2},{7,3},{8,12},{9,13},{12,... | collective-permute-start | bytes 1081352 | tf_op jit(solution)/shard_map/ppermute | solution.py:287
  123.2 6.1 %shard_map.128 = (bf16[128,1408]{1,0:T(8,128)(2,1)S(1)}, bf16[128,1408]{1,0:T(8,128)(2,1)}, bf16[128,1408]{1,0:T(8,128)(2,1)S(1)}) custom-call(s32[2]{0:T(128)S(1)} %pad_add_fusion.place_ref, bf16[176,1024]{1,0:T(8,128)(2,1)S(1)} %pad_maximum_fusion.refs_0_, bf16[176,1024]{1,0:T(8,128)(2,1)} %collective-permute-done.4.refs_1_, ...), custom_call_target="tpu_custom_call" | custom-call | flops 2122317824 | bytes 11173888 | tf_op jit(solution)/shard_map/pallas_call | solution.py:234
  131.7 10.8 %collective-permute-done.19 = bf16[128,1408]{1,0:T(8,128)(2,1)} collective-permute-done((bf16[128,1408]{1,0:T(8,128)(2,1)}, bf16[128,1408]{1,0:T(8,128)(2,1)}, u32[]{:S(2)}, u32[]{:S(2)}) %collective-permute-start.19) | collective-permute-done | bytes 360480 | tf_op jit(solution)/shard_map/ppermute | solution.py:287
  142.5 1.7 add_convert_fusion
  144.5 3.2 %collective-permute-start.20 = (bf16[32,5632]{1,0:T(8,128)(2,1)S(1)}, bf16[32,5632]{1,0:T(8,128)(2,1)S(1)}, u32[]{:S(2)}, u32[]{:S(2)}) collective-permute-start(bf16[32,5632]{1,0:T(8,128)(2,1)S(1)} %reshape.271), channel_id=1, source_target_pairs={{0,2},{1,3},{2,0},{3,1},{4,6},{5,7},{6,4},{7,5},{8,10},{9,11},{10,... | collective-permute-start | bytes 1081352 | tf_op jit(solution)/shard_map/ppermute | solution.py:287
  147.7 15.4 %collective-permute-done.21 = bf16[32,5632]{1,0:T(8,128)(2,1)S(1)} collective-permute-done((bf16[32,5632]{1,0:T(8,128)(2,1)S(1)}, bf16[32,5632]{1,0:T(8,128)(2,1)S(1)}, u32[]{:S(2)}, u32[]{:S(2)}) %collective-permute-start.21) | collective-permute-done | bytes 360480 | tf_op jit(solution)/shard_map/ppermute | solution.py:287
  163.8 1.5 collective-permute-start.29
  166.0 1.6 collective-permute-done.23
  167.6 4.1 %convolution_convert_fusion = bf16[192,512]{1,0:T(8,128)(2,1)S(1)} fusion(bf16[192,5632]{1,0:T(8,128)(2,1)S(1)} %constant_dynamic-update-slice_fusion, bf16[5632,512]{1,0:T(8,128)(2,1)} %param.24), kind=kOutput, calls=%fused_computation.8 | convolution fusion | flops 1107394560 | bytes 8126464 | tf_op jit(solution)/shard_map/dot_general | solution.py:432
  171.7 2.7 %collective-permute-start.27 = (bf16[192,512]{1,0:T(8,128)(2,1)S(1)}, bf16[192,512]{1,0:T(8,128)(2,1)S(1)}, u32[]{:S(2)}, u32[]{:S(2)}) collective-permute-start(bf16[192,512]{1,0:T(8,128)(2,1)S(1)} %convolution_convert_fusion), channel_id=1, source_target_pairs={{0,16},{8,24},{16,0},{24,8},{1,17},{9,25},{17,1},{25,9},{2,18},{10... | collective-permute-start | bytes 589832 | tf_op jit(solution)/shard_map/ppermute | solution.py:444
  174.4 1.5 collective-permute-start.25
  176.4 3.2 %collective-permute-done.27 = bf16[192,512]{1,0:T(8,128)(2,1)S(1)} collective-permute-done((bf16[192,512]{1,0:T(8,128)(2,1)S(1)}, bf16[192,512]{1,0:T(8,128)(2,1)S(1)}, u32[]{:S(2)}, u32[]{:S(2)}) %collective-permute-start.27) | collective-permute-done | bytes 196640 | tf_op jit(solution)/shard_map/ppermute | solution.py:444
  179.8 2.3 %collective-permute-done.26 = bf16[192,512]{1,0:T(8,128)(2,1)S(1)} collective-permute-done((bf16[192,512]{1,0:T(8,128)(2,1)S(1)}, bf16[192,512]{1,0:T(8,128)(2,1)S(1)}, u32[]{:S(2)}, u32[]{:S(2)}) %collective-permute-start.26) | collective-permute-done | bytes 196640 | tf_op jit(solution)/shard_map/ppermute | solution.py:444
  182.4 2.6 %collective-permute-done.25 = bf16[192,512]{1,0:T(8,128)(2,1)S(1)} collective-permute-done((bf16[192,512]{1,0:T(8,128)(2,1)S(1)}, bf16[192,512]{1,0:T(8,128)(2,1)S(1)}, u32[]{:S(2)}, u32[]{:S(2)}) %collective-permute-start.25) | collective-permute-done | bytes 196640 | tf_op jit(solution)/shard_map/ppermute | solution.py:444
  185.4 1.1 convolution_convert_fusion.1
  186.5 1.7 collective-permute-start.33
  188.5 1.5 collective-permute-start.31
  191.1 1.4 collective-permute-done.32
  192.7 0.9 collective-permute-done.31
  193.7 1.0 fusion.6
  (115 shorter events, 15.0 us)
Async XLA Ops:
  1.3 12.7 %copy-start.7 = (s32[32,2]{0,1:T(2,128)S(1)}, s32[32,2]{0,1:T(2,128)}, u32[]{:S(2)}) copy-start(s32[32,2]{0,1:T(2,128)} %param.14) | copy-start | bytes 772
  1.3 12.7 %copy-start.10 = (s32[32]{0:T(128)S(1)}, s32[32]{0:T(128)}, u32[]{:S(2)}) copy-start(s32[32]{0:T(128)} %param.15) | copy-start | bytes 388
  11.0 13.8 %collective-permute-start = (bf16[176,1024]{1,0:T(8,128)(2,1)}, bf16[176,1024]{1,0:T(8,128)(2,1)S(1)}, u32[]{:S(2)}, u32[]{:S(2)}) collective-permute-start(bf16[176,1024]{1,0:T(8,128)(2,1)} %get-tuple-element.33.rest_0_), channel_id=1, source_target_pairs={{0,8},{8,0},{16,24},{24,16},{1,9},{9,1},{17,25},{25,17},{2,10},{10... | collective-permute-start | bytes 1081352 | tf_op jit(solution)/shard_map/ppermute | solution.py:313
  13.9 20.1 %collective-permute-start.2 = (bf16[176,1024]{1,0:T(8,128)(2,1)}, bf16[176,1024]{1,0:T(8,128)(2,1)S(1)}, u32[]{:S(2)}, u32[]{:S(2)}) collective-permute-start(bf16[176,1024]{1,0:T(8,128)(2,1)} %get-tuple-element.39.rest_0_), channel_id=1, source_target_pairs={{0,8},{8,0},{16,24},{24,16},{1,9},{9,1},{17,25},{25,17},{2,10},{10... | collective-permute-start | bytes 1081352 | tf_op jit(solution)/shard_map/ppermute | solution.py:313
  14.3 1.3 copy-start.8
  14.3 1.3 copy-start.9
  24.7 26.0 %copy-start.11 = (bf16[176,1024]{1,0:T(8,128)(2,1)}, bf16[176,1024]{1,0:T(8,128)(2,1)S(1)}, u32[]{:S(2)}) copy-start(bf16[176,1024]{1,0:T(8,128)(2,1)S(1)} %collective-permute-done.rest_3_) | copy-start | bytes 1081348
  34.0 10.1 %copy-start.12 = (bf16[176,1024]{1,0:T(8,128)(2,1)}, bf16[176,1024]{1,0:T(8,128)(2,1)S(1)}, u32[]{:S(2)}) copy-start(bf16[176,1024]{1,0:T(8,128)(2,1)S(1)} %collective-permute-done.2.rest_3_) | copy-start | bytes 1081348
  34.0 10.1 %collective-permute-start.3 = (bf16[176,1024]{1,0:T(8,128)(2,1)S(1)}, bf16[176,1024]{1,0:T(8,128)(2,1)S(1)}, u32[]{:S(2)}, u32[]{:S(2)}) collective-permute-start(bf16[176,1024]{1,0:T(8,128)(2,1)S(1)} %collective-permute-done.2.rest_3_), channel_id=1, source_target_pairs={{0,16},{24,8},{1,17},{25,9},{2,18},{26,10},{3,19},{27,11},{4,20},{... | collective-permute-start | bytes 1081352 | tf_op jit(solution)/shard_map/ppermute | solution.py:319
  35.4 15.4 %collective-permute-start.1 = (bf16[176,1024]{1,0:T(8,128)(2,1)S(1)}, bf16[176,1024]{1,0:T(8,128)(2,1)}, u32[]{:S(2)}, u32[]{:S(2)}) collective-permute-start(bf16[176,1024]{1,0:T(8,128)(2,1)S(1)} %collective-permute-done.rest_3_), channel_id=1, source_target_pairs={{0,16},{24,8},{1,17},{25,9},{2,18},{26,10},{3,19},{27,11},{4,20},{... | collective-permute-start | bytes 1081352 | tf_op jit(solution)/shard_map/ppermute | solution.py:319
  44.1 0.8 copy-start.13
  48.8 38.2 %copy-start.6 = (f32[1408]{0:T(1024)S(1)}, f32[1408]{0:T(1024)}, u32[]{:S(2)}) copy-start(f32[1408]{0:T(1024)} %param.21) | copy-start | bytes 16900
  48.8 40.2 %copy-start.1 = (bf16[1024,1408]{1,0:T(8,128)(2,1)S(1)}, bf16[1024,1408]{1,0:T(8,128)(2,1)}, u32[]{:S(2)}) copy-start(bf16[1024,1408]{1,0:T(8,128)(2,1)} %get-tuple-element.45.refs_8_) | copy-start | bytes 8650756
  55.7 18.2 %collective-permute-start.5 = (bf16[176,1024]{1,0:T(8,128)(2,1)S(1)}, bf16[176,1024]{1,0:T(8,128)(2,1)}, u32[]{:S(2)}, u32[]{:S(2)}) collective-permute-start(bf16[176,1024]{1,0:T(8,128)(2,1)S(1)} %pad_maximum_fusion.refs_0_), channel_id=1, source_target_pairs={{0,4},{1,5},{4,0},{5,1},{2,6},{3,7},{6,2},{7,3},{8,12},{9,13},{12,... | collective-permute-start | bytes 1081352 | tf_op jit(solution)/shard_map/ppermute | solution.py:287
  58.5 17.9 %collective-permute-start.4 = (bf16[176,1024]{1,0:T(8,128)(2,1)S(1)}, bf16[176,1024]{1,0:T(8,128)(2,1)}, u32[]{:S(2)}, u32[]{:S(2)}) collective-permute-start(bf16[176,1024]{1,0:T(8,128)(2,1)S(1)} %pad_maximum_fusion.refs_0_), channel_id=1, source_target_pairs={{0,2},{1,3},{2,0},{3,1},{4,6},{5,7},{6,4},{7,5},{8,10},{9,11},{10,... | collective-permute-start | bytes 1081352 | tf_op jit(solution)/shard_map/ppermute | solution.py:287
  73.9 2.6 %collective-permute-start.6 = (bf16[176,1024]{1,0:T(8,128)(2,1)S(1)}, bf16[176,1024]{1,0:T(8,128)(2,1)S(1)}, u32[]{:S(2)}, u32[]{:S(2)}) collective-permute-start(bf16[176,1024]{1,0:T(8,128)(2,1)S(1)} %pad_maximum_fusion.refs_0_), channel_id=1, source_target_pairs={{2,4},{3,5},{4,2},{5,3},{10,12},{11,13},{12,10},{13,11},{18,20},{1... | collective-permute-start | bytes 1081352 | tf_op jit(solution)/shard_map/ppermute | solution.py:287
  74.5 11.6 %collective-permute-start.7 = (bf16[176,1024]{1,0:T(8,128)(2,1)}, bf16[176,1024]{1,0:T(8,128)(2,1)S(1)}, u32[]{:S(2)}, u32[]{:S(2)}) collective-permute-start(bf16[176,1024]{1,0:T(8,128)(2,1)} %collective-permute-done.5.refs_2_), channel_id=1, source_target_pairs={{2,0},{3,1},{4,6},{5,7},{10,8},{11,9},{12,14},{13,15},{18,16},{19,... | collective-permute-start | bytes 1081352 | tf_op jit(solution)/shard_map/ppermute | solution.py:287
  75.8 11.4 %collective-permute-start.8 = (bf16[176,1024]{1,0:T(8,128)(2,1)S(1)}, bf16[176,1024]{1,0:T(8,128)(2,1)}, u32[]{:S(2)}, u32[]{:S(2)}) collective-permute-start(bf16[176,1024]{1,0:T(8,128)(2,1)S(1)} %pad_maximum_fusion.refs_0_), channel_id=1, source_target_pairs={{0,1},{1,0},{2,3},{3,2},{4,5},{5,4},{6,7},{7,6},{8,9},{9,8},{10,11... | collective-permute-start | bytes 1081352 | tf_op jit(solution)/shard_map/ppermute | solution.py:293
  75.9 11.3 %collective-permute-start.10 = (bf16[176,1024]{1,0:T(8,128)(2,1)}, bf16[176,1024]{1,0:T(8,128)(2,1)}, u32[]{:S(2)}, u32[]{:S(2)}) collective-permute-start(bf16[176,1024]{1,0:T(8,128)(2,1)} %collective-permute-done.5.refs_2_), channel_id=1, source_target_pairs={{0,1},{1,0},{2,3},{3,2},{4,5},{5,4},{6,7},{7,6},{8,9},{9,8},{10,11... | collective-permute-start | bytes 1081352 | tf_op jit(solution)/shard_map/ppermute | solution.py:293
  76.4 10.8 %collective-permute-start.9 = (bf16[176,1024]{1,0:T(8,128)(2,1)}, bf16[176,1024]{1,0:T(8,128)(2,1)}, u32[]{:S(2)}, u32[]{:S(2)}) collective-permute-start(bf16[176,1024]{1,0:T(8,128)(2,1)} %collective-permute-done.4.refs_1_), channel_id=1, source_target_pairs={{0,1},{1,0},{2,3},{3,2},{4,5},{5,4},{6,7},{7,6},{8,9},{9,8},{10,11... | collective-permute-start | bytes 1081352 | tf_op jit(solution)/shard_map/ppermute | solution.py:293
  87.0 2.0 %collective-permute-start.11 = (bf16[176,1024]{1,0:T(8,128)(2,1)}, bf16[176,1024]{1,0:T(8,128)(2,1)}, u32[]{:S(2)}, u32[]{:S(2)}) collective-permute-start(bf16[176,1024]{1,0:T(8,128)(2,1)} %shard_map.123.refs_3_), channel_id=1, source_target_pairs={{0,1},{1,0},{2,3},{3,2},{4,5},{5,4},{6,7},{7,6},{8,9},{9,8},{10,11... | collective-permute-start | bytes 1081352 | tf_op jit(solution)/shard_map/ppermute | solution.py:293
  89.0 2.1 %copy-start = (bf16[1408,1408]{1,0:T(8,128)(2,1)S(1)}, bf16[1408,1408]{1,0:T(8,128)(2,1)}, u32[]{:S(2)}) copy-start(bf16[1408,1408]{1,0:T(8,128)(2,1)} %refs_10_.7) | copy-start | bytes 11894788
  91.1 1.6 copy-start.2
  92.7 1.6 copy-start.3
  99.8 6.1 %collective-permute-start.13 = (bf16[128,1408]{1,0:T(8,128)(2,1)S(1)}, bf16[128,1408]{1,0:T(8,128)(2,1)S(1)}, u32[]{:S(2)}, u32[]{:S(2)}) collective-permute-start(bf16[128,1408]{1,0:T(8,128)(2,1)S(1)} %get-tuple-element.49), channel_id=1, source_target_pairs={{0,1},{1,0},{2,3},{3,2},{4,5},{5,4},{6,7},{7,6},{8,9},{9,8},{10,11... | collective-permute-start | bytes 1081352 | tf_op jit(solution)/shard_map/ppermute | solution.py:293
  105.5 10.3 %collective-permute-start.12 = (bf16[128,1408]{1,0:T(8,128)(2,1)S(1)}, bf16[128,1408]{1,0:T(8,128)(2,1)S(1)}, u32[]{:S(2)}, u32[]{:S(2)}) collective-permute-start(bf16[128,1408]{1,0:T(8,128)(2,1)S(1)} %get-tuple-element.47), channel_id=1, source_target_pairs={{0,1},{1,0},{2,3},{3,2},{4,5},{5,4},{6,7},{7,6},{8,9},{9,8},{10,11... | collective-permute-start | bytes 1081352 | tf_op jit(solution)/shard_map/ppermute | solution.py:293
  106.7 10.4 %collective-permute-start.14 = (bf16[128,1408]{1,0:T(8,128)(2,1)}, bf16[128,1408]{1,0:T(8,128)(2,1)S(1)}, u32[]{:S(2)}, u32[]{:S(2)}) collective-permute-start(bf16[128,1408]{1,0:T(8,128)(2,1)} %shard_map.126), channel_id=1, source_target_pairs={{0,2},{1,3},{6,4},{7,5},{8,10},{9,11},{14,12},{15,13},{16,18},{17,... | collective-permute-start | bytes 1081352 | tf_op jit(solution)/shard_map/ppermute | solution.py:287
  114.2 8.2 %collective-permute-start.17 = (bf16[128,1408]{1,0:T(8,128)(2,1)S(1)}, bf16[128,1408]{1,0:T(8,128)(2,1)S(1)}, u32[]{:S(2)}, u32[]{:S(2)}) collective-permute-start(bf16[128,1408]{1,0:T(8,128)(2,1)S(1)} %get-tuple-element.56), channel_id=1, source_target_pairs={{0,1},{1,0},{2,3},{3,2},{4,5},{5,4},{6,7},{7,6},{8,9},{9,8},{10,11... | collective-permute-start | bytes 1081352 | tf_op jit(solution)/shard_map/ppermute | solution.py:293
  114.4 17.3 %collective-permute-start.16 = (bf16[128,1408]{1,0:T(8,128)(2,1)}, bf16[128,1408]{1,0:T(8,128)(2,1)}, u32[]{:S(2)}, u32[]{:S(2)}) collective-permute-start(bf16[128,1408]{1,0:T(8,128)(2,1)} %shard_map.126), channel_id=1, source_target_pairs={{2,4},{3,5},{4,2},{5,3},{10,12},{11,13},{12,10},{13,11},{18,20},{1... | collective-permute-start | bytes 1081352 | tf_op jit(solution)/shard_map/ppermute | solution.py:287
  118.0 24.5 %collective-permute-start.19 = (bf16[128,1408]{1,0:T(8,128)(2,1)}, bf16[128,1408]{1,0:T(8,128)(2,1)}, u32[]{:S(2)}, u32[]{:S(2)}) collective-permute-start(bf16[128,1408]{1,0:T(8,128)(2,1)} %shard_map.127), channel_id=1, source_target_pairs={{0,4},{1,5},{4,0},{5,1},{2,6},{3,7},{6,2},{7,3},{8,12},{9,13},{12,... | collective-permute-start | bytes 1081352 | tf_op jit(solution)/shard_map/ppermute | solution.py:287
  123.2 19.3 %collective-permute-start.18 = (bf16[128,1408]{1,0:T(8,128)(2,1)}, bf16[128,1408]{1,0:T(8,128)(2,1)}, u32[]{:S(2)}, u32[]{:S(2)}) collective-permute-start(bf16[128,1408]{1,0:T(8,128)(2,1)} %shard_map.130), channel_id=1, source_target_pairs={{0,2},{1,3},{2,0},{3,1},{4,6},{5,7},{6,4},{7,5},{8,10},{9,11},{10,... | collective-permute-start | bytes 1081352 | tf_op jit(solution)/shard_map/ppermute | solution.py:287
  130.8 11.7 %collective-permute-start.15 = (bf16[128,1408]{1,0:T(8,128)(2,1)}, bf16[128,1408]{1,0:T(8,128)(2,1)S(1)}, u32[]{:S(2)}, u32[]{:S(2)}) collective-permute-start(bf16[128,1408]{1,0:T(8,128)(2,1)} %get-tuple-element.53), channel_id=1, source_target_pairs={{0,1},{1,0},{2,3},{3,2},{4,5},{5,4},{6,7},{7,6},{8,9},{9,8},{10,11... | collective-permute-start | bytes 1081352 | tf_op jit(solution)/shard_map/ppermute | solution.py:293
  144.4 18.7 %collective-permute-start.21 = (bf16[32,5632]{1,0:T(8,128)(2,1)S(1)}, bf16[32,5632]{1,0:T(8,128)(2,1)S(1)}, u32[]{:S(2)}, u32[]{:S(2)}) collective-permute-start(bf16[32,5632]{1,0:T(8,128)(2,1)S(1)} %reshape.271), channel_id=1, source_target_pairs={{0,4},{1,5},{4,0},{5,1},{2,6},{3,7},{6,2},{7,3},{8,12},{9,13},{12,... | collective-permute-start | bytes 1081352 | tf_op jit(solution)/shard_map/ppermute | solution.py:287
  144.5 20.9 %collective-permute-start.20 = (bf16[32,5632]{1,0:T(8,128)(2,1)S(1)}, bf16[32,5632]{1,0:T(8,128)(2,1)S(1)}, u32[]{:S(2)}, u32[]{:S(2)}) collective-permute-start(bf16[32,5632]{1,0:T(8,128)(2,1)S(1)} %reshape.271), channel_id=1, source_target_pairs={{0,2},{1,3},{2,0},{3,1},{4,6},{5,7},{6,4},{7,5},{8,10},{9,11},{10,... | collective-permute-start | bytes 1081352 | tf_op jit(solution)/shard_map/ppermute | solution.py:287
  147.7 18.2 %collective-permute-start.22 = (bf16[32,5632]{1,0:T(8,128)(2,1)S(1)}, bf16[32,5632]{1,0:T(8,128)(2,1)S(1)}, u32[]{:S(2)}, u32[]{:S(2)}) collective-permute-start(bf16[32,5632]{1,0:T(8,128)(2,1)S(1)} %reshape.271), channel_id=1, source_target_pairs={{0,1},{1,0},{2,3},{3,2},{4,5},{5,4},{6,7},{7,6},{8,9},{9,8},{10,11... | collective-permute-start | bytes 1081352 | tf_op jit(solution)/shard_map/ppermute | solution.py:293
  163.1 12.8 %collective-permute-start.28 = (bf16[32,5632]{1,0:T(8,128)(2,1)S(1)}, bf16[32,5632]{1,0:T(8,128)(2,1)S(1)}, u32[]{:S(2)}, u32[]{:S(2)}) collective-permute-start(bf16[32,5632]{1,0:T(8,128)(2,1)S(1)} %reshape.271), channel_id=1, source_target_pairs={{2,4},{3,5},{4,2},{5,3},{10,12},{11,13},{12,10},{13,11},{18,20},{1... | collective-permute-start | bytes 1081352 | tf_op jit(solution)/shard_map/ppermute | solution.py:287
  163.8 12.2 %collective-permute-start.29 = (bf16[32,5632]{1,0:T(8,128)(2,1)S(1)}, bf16[32,5632]{1,0:T(8,128)(2,1)S(1)}, u32[]{:S(2)}, u32[]{:S(2)}) collective-permute-start(bf16[32,5632]{1,0:T(8,128)(2,1)S(1)} %collective-permute-done.21), channel_id=1, source_target_pairs={{2,0},{3,1},{4,6},{5,7},{10,8},{11,9},{12,14},{13,15},{18,16},{19,... | collective-permute-start | bytes 1081352 | tf_op jit(solution)/shard_map/ppermute | solution.py:287
  165.3 2.3 %collective-permute-start.24 = (bf16[32,5632]{1,0:T(8,128)(2,1)S(1)}, bf16[32,5632]{1,0:T(8,128)(2,1)S(1)}, u32[]{:S(2)}, u32[]{:S(2)}) collective-permute-start(bf16[32,5632]{1,0:T(8,128)(2,1)S(1)} %collective-permute-done.21), channel_id=1, source_target_pairs={{0,1},{1,0},{2,3},{3,2},{4,5},{5,4},{6,7},{7,6},{8,9},{9,8},{10,11... | collective-permute-start | bytes 1081352 | tf_op jit(solution)/shard_map/ppermute | solution.py:293
  165.4 2.2 %collective-permute-start.23 = (bf16[32,5632]{1,0:T(8,128)(2,1)S(1)}, bf16[32,5632]{1,0:T(8,128)(2,1)S(1)}, u32[]{:S(2)}, u32[]{:S(2)}) collective-permute-start(bf16[32,5632]{1,0:T(8,128)(2,1)S(1)} %collective-permute-done.20), channel_id=1, source_target_pairs={{0,1},{1,0},{2,3},{3,2},{4,5},{5,4},{6,7},{7,6},{8,9},{9,8},{10,11... | collective-permute-start | bytes 1081352 | tf_op jit(solution)/shard_map/ppermute | solution.py:293
  167.6 17.8 %slice-start = ((s8[5767168]{0:T(1024)(128)(4,1)}), s8[4194304]{0:T(1024)(128)(4,1)S(1)}, s32[]{:S(2)}) async-start(s8[5767168]{0:T(1024)(128)(4,1)} %bitcast.66), calls=%async_computation | async-start | bytes 8388608
  167.6 17.7 %slice-start.1 = ((s8[5767168]{0:T(1024)(128)(4,1)}), s8[1572864]{0:T(1024)(128)(4,1)S(1)}, s32[]{:S(2)}) async-start(s8[5767168]{0:T(1024)(128)(4,1)} %bitcast.66), calls=%async_computation.1 | async-start | bytes 3145728
  171.7 7.9 %collective-permute-start.27 = (bf16[192,512]{1,0:T(8,128)(2,1)S(1)}, bf16[192,512]{1,0:T(8,128)(2,1)S(1)}, u32[]{:S(2)}, u32[]{:S(2)}) collective-permute-start(bf16[192,512]{1,0:T(8,128)(2,1)S(1)} %convolution_convert_fusion), channel_id=1, source_target_pairs={{0,16},{8,24},{16,0},{24,8},{1,17},{9,25},{17,1},{25,9},{2,18},{10... | collective-permute-start | bytes 589832 | tf_op jit(solution)/shard_map/ppermute | solution.py:444
  174.4 7.8 %collective-permute-start.26 = (bf16[192,512]{1,0:T(8,128)(2,1)S(1)}, bf16[192,512]{1,0:T(8,128)(2,1)S(1)}, u32[]{:S(2)}, u32[]{:S(2)}) collective-permute-start(bf16[192,512]{1,0:T(8,128)(2,1)S(1)} %convolution_convert_fusion), channel_id=1, source_target_pairs={{0,8},{8,0},{16,24},{24,16},{1,9},{9,1},{17,25},{25,17},{2,10},{10... | collective-permute-start | bytes 589832 | tf_op jit(solution)/shard_map/ppermute | solution.py:444
  174.4 10.7 %collective-permute-start.25 = (bf16[192,512]{1,0:T(8,128)(2,1)S(1)}, bf16[192,512]{1,0:T(8,128)(2,1)S(1)}, u32[]{:S(2)}, u32[]{:S(2)}) collective-permute-start(bf16[192,512]{1,0:T(8,128)(2,1)S(1)} %convolution_convert_fusion), channel_id=1, source_target_pairs={{0,24},{8,16},{16,8},{24,0},{1,25},{9,17},{17,9},{25,1},{2,26},{10... | collective-permute-start | bytes 589832 | tf_op jit(solution)/shard_map/ppermute | solution.py:444
  176.0 9.3 %collective-permute-start.30 = (bf16[32,5632]{1,0:T(8,128)(2,1)S(1)}, bf16[32,5632]{1,0:T(8,128)(2,1)S(1)}, u32[]{:S(2)}, u32[]{:S(2)}) collective-permute-start(bf16[32,5632]{1,0:T(8,128)(2,1)S(1)} %shard_map.131), channel_id=1, source_target_pairs={{0,1},{1,0},{2,3},{3,2},{4,5},{5,4},{6,7},{7,6},{8,9},{9,8},{10,11... | collective-permute-start | bytes 1081352 | tf_op jit(solution)/shard_map/ppermute | solution.py:293
  186.5 4.3 %collective-permute-start.33 = (bf16[64,512]{1,0:T(8,128)(2,1)S(1)}, bf16[64,512]{1,0:T(8,128)(2,1)S(1)}, u32[]{:S(2)}, u32[]{:S(2)}) collective-permute-start(bf16[64,512]{1,0:T(8,128)(2,1)S(1)} %convolution_convert_fusion.1), channel_id=1, source_target_pairs={{0,16},{8,24},{16,0},{24,8},{1,17},{9,25},{17,1},{25,9},{2,18},{10... | collective-permute-start | bytes 196616 | tf_op jit(solution)/shard_map/ppermute | solution.py:444
  188.2 4.3 %collective-permute-start.32 = (bf16[64,512]{1,0:T(8,128)(2,1)S(1)}, bf16[64,512]{1,0:T(8,128)(2,1)S(1)}, u32[]{:S(2)}, u32[]{:S(2)}) collective-permute-start(bf16[64,512]{1,0:T(8,128)(2,1)S(1)} %convolution_convert_fusion.1), channel_id=1, source_target_pairs={{0,8},{8,0},{16,24},{24,16},{1,9},{9,1},{17,25},{25,17},{2,10},{10... | collective-permute-start | bytes 196616 | tf_op jit(solution)/shard_map/ppermute | solution.py:444
  188.5 5.2 %collective-permute-start.31 = (bf16[64,512]{1,0:T(8,128)(2,1)S(1)}, bf16[64,512]{1,0:T(8,128)(2,1)S(1)}, u32[]{:S(2)}, u32[]{:S(2)}) collective-permute-start(bf16[64,512]{1,0:T(8,128)(2,1)S(1)} %convolution_convert_fusion.1), channel_id=1, source_target_pairs={{0,24},{8,16},{16,8},{24,0},{1,25},{9,17},{17,9},{25,1},{2,26},{10... | collective-permute-start | bytes 196616 | tf_op jit(solution)/shard_map/ppermute | solution.py:444
  (2 other events, 1.5 us)

commit v3 on v2

--- a/solution.py
+++ b/solution.py
@@ -112,10 +112,10 @@
     )(base, grid, patches, row_table, col_table, gain, weight)
 
 
-def attend_kernel(taken, low_ref, high_ref, base_ref, start_ref, end_ref, q_ref, *rest):
-    states, rest = rest[:taken], rest[taken:]
-    count = len(rest) - (1 if taken else 3)
-    parts, outs = rest[:count], rest[count:]
+def attend_kernel(heads, taken, low_ref, high_ref, base_ref, start_ref, end_ref, q_ref, *rest):
+    count = base_ref.shape[0]
+    states, rest = rest[: taken * heads], rest[taken * heads :]
+    parts, outs = rest[: count * heads], rest[count * heads :]
     rows = q_ref.shape[1]
     scale = math.log2(math.e) / math.sqrt(HEAD_DIM)
     for tile in range(rows // TILE):
@@ -124,92 +124,145 @@
         end = end_ref[:, span]
         low = low_ref[tile]
         high = high_ref[tile]
-        queries = q_ref[:, span]
+        queries = [q_ref[h * HEAD_DIM : (h + 1) * HEAD_DIM, span] for h in range(heads)]
         if taken:
-            carry = tuple(state[:, span] for state in states)
+            carry = tuple(
+                tuple(state[:, span] for state in states[taken * h : taken * (h + 1)])
+                for h in range(heads)
+            )
         else:
-            carry = (
-                jnp.full((1, TILE), LOW, jnp.float32),
-                jnp.zeros((1, TILE), jnp.float32),
-                jnp.zeros((HEAD_DIM, TILE), jnp.float32),
+            carry = tuple(
+                (
+                    jnp.full((1, TILE), LOW, jnp.float32),
+                    jnp.zeros((1, TILE), jnp.float32),
+                    jnp.zeros((HEAD_DIM, TILE), jnp.float32),
+                )
+                for _ in range(heads)
             )
-        for number, part in enumerate(parts):
+        for number in range(count):
             base = base_ref[number]
-            tiles = part.shape[1] // TILE
+            tiles = rows // TILE
             first = jnp.clip((low - base) // TILE, 0, tiles)
             last = jnp.clip((high - base + TILE - 1) // TILE, 0, tiles)
 
-            def step(place, carry, part=part, base=base, queries=queries, start=start, end=end):
+            def step(place, carry, number=number, base=base, queries=queries, start=start, end=end):
                 where = pl.ds(pl.multiple_of(place * TILE, TILE), TILE)
                 index = base + place * TILE + lax.broadcasted_iota(jnp.int32, (TILE, TILE), 0)
                 allowed = (index >= start) & (index < end)
-                top, total, acc = carry
-                scores = dot(part[0:HEAD_DIM, where], queries, TN) * scale
-                scores = jnp.where(allowed, scores, LOW)
-                higher = jnp.maximum(top, jnp.max(scores, axis=0, keepdims=True))
-                weights = jnp.exp2(scores - higher)
-                fade = jnp.exp2(top - higher)
-                total = total * fade + jnp.sum(weights, axis=0, keepdims=True)
-                value_rows = part[HEAD_DIM : 2 * HEAD_DIM, where]
-                acc = acc * fade + dot(value_rows, weights.astype(jnp.bfloat16))
-                return higher, total, acc
+                new = []
+                for h in range(heads):
+                    part = parts[count * h + number]
+                    top, total, acc = carry[h]
+                    scores = dot(part[0:HEAD_DIM, where], queries[h], TN) * scale
+                    scores = jnp.where(allowed, scores, LOW)
+                    higher = jnp.maximum(top, jnp.max(scores, axis=0, keepdims=True))
+                    weights = jnp.exp2(scores - higher)
+                    fade = jnp.exp2(top - higher)
+                    total = total * fade + jnp.sum(weights, axis=0, keepdims=True)
+                    value_rows = part[HEAD_DIM : 2 * HEAD_DIM, where]
+                    acc = acc * fade + dot(value_rows, weights.astype(jnp.bfloat16))
+                    new.append((higher, total, acc))
+                return tuple(new)
 
             carry = lax.fori_loop(first, last, step, carry)
-        if taken:
-            _, total, acc = carry
-            outs[0][:, span] = (acc / total).astype(jnp.bfloat16)
-        else:
-            for out, value in zip(outs, carry):
-                out[:, span] = value
-
-
-def attend(head, low, high, bases, start, end, queries, states, parts):
+        for h in range(heads):
+            if taken:
+                _, total, acc = carry[h]
+                outs[h][:, span] = (acc / total).astype(jnp.bfloat16)
+            else:
+                for out, value in zip(outs[3 * h : 3 * h + 3], carry[h]):
+                    out[:, span] = value
+
+
+def attend(first_head, heads, low, high, bases, start, end, queries, states, parts):
     rows = queries.shape[1]
     smem = pl.BlockSpec(memory_space=pltpu.SMEM)
     if states:
-        shapes = [jax.ShapeDtypeStruct((HEAD_DIM, rows), jnp.bfloat16)]
+        shapes = [jax.ShapeDtypeStruct((HEAD_DIM, rows), jnp.bfloat16)] * heads
     else:
         shapes = [
             jax.ShapeDtypeStruct((height, rows), jnp.float32) for height in (1, 1, HEAD_DIM)
-        ]
+        ] * heads
     return pl.pallas_call(
-        functools.partial(attend_kernel, len(states)),
+        functools.partial(attend_kernel, heads, len(states) // heads),
         grid=(1,),
         in_specs=[smem] * 3
         + [whole(start.shape), whole(end.shape)]
-        + [pl.BlockSpec((HEAD_DIM, rows), lambda i: (head, 0))]
+        + [pl.BlockSpec((heads * HEAD_DIM, rows), lambda i: (first_head // heads, 0))]
         + [whole(value.shape) for value in (*states, *parts)],
         out_specs=[whole(x.shape) for x in shapes],
         out_shape=shapes,
         compiler_params=pltpu.CompilerParams(vmem_limit_bytes=VMEM_LIMIT),
         cost_estimate=pl.CostEstimate(
-            flops=4 * rows * rows * HEAD_DIM,
-            bytes_accessed=8 * rows * HEAD_DIM,
-            transcendentals=rows * rows,
+            flops=4 * rows * rows * heads * HEAD_DIM,
+            bytes_accessed=8 * rows * heads * HEAD_DIM,
+            transcendentals=heads * rows * rows,
         ),
     )(low, high, bases, start, end, queries, *states, *parts)
 
 
-def mlp_kernel(last, place_ref, *refs):
-    blocks, refs = refs[:8], refs[8:]
-    embedded_ref, gain_ref, *held = refs[:5]
-    kept_ref, sent_ref = refs[5:7]
-    blended_ref = refs[-1]
+def load_kernel(*refs):
+    stored, held, token_ref, sems = refs[:3], refs[-5:-2], refs[-2], refs[-1]
+    copies = [
+        pltpu.make_async_copy(source, target, sems.at[i])
+        for i, (source, target) in enumerate(zip(stored, held))
+    ]
+    for copy in copies:
+        copy.start()
+    token_ref[...] = jnp.zeros(token_ref.shape, token_ref.dtype)
+    for copy in copies:
+        copy.wait()
+
+
+def load(stored, marks):
+    resident = pl.BlockSpec(memory_space=pltpu.VMEM)
+    token = jax.ShapeDtypeStruct((8, LANES), jnp.float32)
+    *held, token = pl.pallas_call(
+        load_kernel,
+        in_specs=[pl.BlockSpec(memory_space=pltpu.HBM)] * 3
+        + [pl.BlockSpec(memory_space=pl.ANY)] * len(marks),
+        out_specs=[resident] * 4,
+        out_shape=[jax.ShapeDtypeStruct(x.shape, x.dtype) for x in stored] + [token],
+        scratch_shapes=[pltpu.SemaphoreType.DMA((3,))],
+        compiler_params=pltpu.CompilerParams(vmem_limit_bytes=ADD_VMEM),
+    )(*stored, *marks)
+    return held, token
+
+
+def mlp_kernel(distance, place_ref, *refs):
+    *refs, sems, pieces_ref, rows_ref, blended_ref = refs
+    heads = blended_ref.shape[1] // HEAD_DIM
+    blocks, refs = refs[: 8 * heads], refs[8 * heads :]
+    embedded_ref, gain_ref, out_ref, up_ref, down_ref, kept_ref, sent_ref = refs[:7]
     height, core = place_ref[0], place_ref[1]
-    width = blocks[0].shape[0]
+    tile = rows_ref.shape[0]
+    first_row = pl.multiple_of((height ^ distance) * tile, tile)
+    span = pl.ds(first_row, tile)
+    copies = [
+        pltpu.make_async_copy(block.at[:, span], pieces_ref.at[i], sems.at[i])
+        for i, block in enumerate(blocks)
+    ]
+    copies.append(
+        pltpu.make_async_copy(embedded_ref.at[span, :], rows_ref, sems.at[len(blocks)])
+    )
+    for copy in copies:
+        copy.start()
+    for copy in copies:
+        copy.wait()
     for k in range(4):
         for side in range(2):
             source = 2 * (height ^ k) + (core if side == 0 else 1 - core)
-            blended_ref[pl.ds(pl.multiple_of(source * width, 16), width), :] = blocks[
-                4 * side + k
-            ][...]
-    attended = dot(blended_ref[...], held[0][...], TN)
-    residual = (embedded_ref[...].astype(jnp.float32) + attended).astype(jnp.bfloat16)
-    rows = residual.shape[0] // 2
+            for h in range(heads):
+                where = slice(h * HEAD_DIM, (h + 1) * HEAD_DIM)
+                blended_ref[source, where, :] = pieces_ref[8 * h + 4 * side + k]
+    blended = blended_ref[...].reshape(-1, tile)
+    attended = dot(blended, out_ref[...], TN)
+    residual = (rows_ref[...].astype(jnp.float32) + attended).astype(jnp.bfloat16)
     normed = norm_rows(residual.astype(jnp.float32), gain_ref[...]).astype(jnp.bfloat16)
-    lifted = dot(normed, held[1][...])
+    lifted = dot(normed, up_ref[...])
     activated = (0.5 * lifted * (1.0 + lax.erf(lifted * math.sqrt(0.5)))).astype(jnp.bfloat16)
-    partial = dot(activated, held[2][...]).astype(jnp.bfloat16)
+    partial = dot(activated, down_ref[...]).astype(jnp.bfloat16)
+    rows = tile // 2
     for side in range(2):
 
         @pl.when(core == side)
@@ -218,41 +271,39 @@
             other = slice((1 - side) * rows, (2 - side) * rows)
             kept_ref[...] = partial[mine]
             sent_ref[...] = partial[other]
-            if last:
+            if distance == 0:
                 refs[7][...] = residual[mine]
 
 
-def mlp(distance, place, blocks, embedded, out_weight, gain, up_weight, down_weight):
+def mlp(distance, place, blocks, embedded, gain, held):
     model = embedded.shape[1]
-    width = blocks[0].shape[0]
+    heads = len(blocks) // 8
     rows = blocks[0].shape[1] // 4
-    hidden = up_weight.shape[1]
-    stored = (out_weight, up_weight, down_weight)
-    resident = pl.BlockSpec(memory_space=pltpu.VMEM)
-    last = distance == 0
-    shapes = [jax.ShapeDtypeStruct((rows // 2, model), jnp.bfloat16)] * (3 if last else 2)
+    hidden = held[1].shape[1]
+    away = pl.BlockSpec(memory_space=pltpu.HBM)
+    shapes = [jax.ShapeDtypeStruct((rows // 2, model), jnp.bfloat16)] * (2 + (distance == 0))
     return pl.pallas_call(
-        functools.partial(mlp_kernel, last),
-        grid_spec=pltpu.PrefetchScalarGridSpec(
-            num_scalar_prefetch=1,
-            grid=(1,),
-            in_specs=[pl.BlockSpec((width, rows), lambda i, p: (0, p[0] ^ distance))] * 8
-            + [
-                pl.BlockSpec((rows, model), lambda i, p: (p[0] ^ distance, 0)),
-                whole(gain.shape),
-            ]
-            + [resident] * 3,
-            out_specs=[whole(x.shape) for x in shapes],
-            scratch_shapes=[pltpu.VMEM((8 * width, rows), jnp.bfloat16)],
-        ),
+        functools.partial(mlp_kernel, distance),
+        grid=(1,),
+        in_specs=[pl.BlockSpec(memory_space=pltpu.SMEM)]
+        + [away] * (len(blocks) + 1)
+        + [whole(gain.shape)]
+        + [pl.BlockSpec(memory_space=pltpu.VMEM)] * 3,
+        out_specs=[whole(x.shape) for x in shapes],
         out_shape=shapes,
+        scratch_shapes=[
+            pltpu.SemaphoreType.DMA((len(blocks) + 1,)),
+            pltpu.VMEM((len(blocks), HEAD_DIM, rows), jnp.bfloat16),
+            pltpu.VMEM((rows, model), jnp.bfloat16),
+            pltpu.VMEM((8, heads * HEAD_DIM, rows), jnp.bfloat16),
+        ],
         compiler_params=pltpu.CompilerParams(vmem_limit_bytes=SHARED_VMEM),
         cost_estimate=pl.CostEstimate(
             flops=2 * rows * model * (model + 2 * hidden),
             bytes_accessed=2 * (4 * rows * model + model * (model + 2 * hidden)),
             transcendentals=rows * hidden,
         ),
-    )(place, *blocks, embedded, gain, *stored)
+    )(place, *blocks, embedded, gain, *held)
 
 
 def add_kernel(*refs):
@@ -300,11 +351,13 @@
 INWARD = [(0, 1), (3, 2)]
 
 
-def gather_line(value):
+def gather_line(value, mark=None):
     second = along_hid(value, SECOND)
     first = along_hid(value, NEXT)
-    outward = along_hid(second, OUTWARD)
-    third = add(along_hid(after(value, second), MIDDLE), outward)
+    passed, kept = (second, after(value, second))
+    if mark is not None:
+        passed, kept = after(passed, mark), after(kept, mark)
+    third = add(along_hid(kept, MIDDLE), along_hid(passed, OUTWARD))
     return [value, first, second, third]
 
 
@@ -364,7 +417,7 @@
         patches,
         row_table,
         col_table,
-        gain_attn[None, :],
+        gain_attn,
         jnp.swapaxes(qkv_weight, 1, 2).reshape(-1, model),
     )
 
@@ -380,17 +433,23 @@
     part_bands = jnp.stack(neighbour_bands(band, bands))
     bases = jnp.where((part_bands >= 0) & (part_bands < bands), part_bands * rows, beyond)
     near = [across_keys(own, bands) for own in keys]
-    far, states = [], []
-    own_base = base[None]
-    for head, own in enumerate(keys):
-        states.append(attend(head, low, high, own_base, start, end, queries, (), (own,)))
-        near[head] = after(near[head], states[head][0])
-        far.append(along_keys(own, near[head], bands))
-        own_base = after(own_base, near[head])
-    heads_blended = []
-    for head in range(len(keys)):
-        heads_blended += attend(
-            head, low, high, bases, start, end, queries, states[head], (near[head], far[head])
+    heads = len(keys)
+    states = attend(0, heads, low, high, base[None], start, end, queries, (), keys)
+    near[0] = after(near[0], states[0])
+    far = [along_keys(own, across, bands) for own, across in zip(keys, near)]
+    blended = []
+    for head in range(heads):
+        blended += attend(
+            head,
+            1,
+            low,
+            high,
+            bases,
+            start,
+            end,
+            queries,
+            states[3 * head : 3 * head + 3],
+            (near[head], far[head]),
         )
 
     member = lax.axis_index("hid")
@@ -400,18 +459,22 @@
     merged_rows = rows // 4
     slots = jnp.arange(merged_rows, dtype=jnp.int32)
 
-    blocks = gather_line(jnp.concatenate(heads_blended, axis=0))
-    blocks = blocks + [swap_core(block) for block in blocks]
-    rest = (blocks, embedded, out_weight, gain_mlp[None, :], up_weight, down_weight)
+    gain_row = gain_mlp[None, :]
+    held, token = load((out_weight, up_weight, down_weight), (place, gain_row, blended[-1]))
+    blocks = []
+    for head, piece in enumerate(blended):
+        piece = gather_line(piece, token if head == heads - 1 else None)
+        blocks += piece + [swap_core(block) for block in piece]
+    rest = (blocks, embedded, gain_row, held)
 
     kept, sent = mlp(3, place, *rest)
     third = add(kept, swap_core(sent))
     inward = along_hid(third, INWARD)
     middle = along_hid(third, MIDDLE)
-    kept, sent = mlp(2, place, *rest)
+    kept, sent = mlp(2, after(place, third), *rest)
     moved = swap_core(sent)
-    kept_first, sent_first = mlp(1, after(place, third), *rest)
-    second = add(kept, moved, inward)
+    kept_first, sent_first = mlp(1, after(place, kept), *rest)
+    second = add(kept, moved, after(inward, kept_first))
     kept, sent, residual = mlp(0, after(place, second), *rest)
     first = add(kept_first, swap_core(sent_first))
     second = along_hid(second, SECOND)
@@ -421,17 +484,17 @@
         total = total + piece.astype(jnp.float32)
     output_rows = total.astype(jnp.bfloat16).reshape(home_cells, 4 * model)
 
-    merged = gather_line(output_rows)
-    returned = jnp.zeros((merged_rows, merge_weight.shape[1]), jnp.float32)
-    projected = None
-    for distances in ((0, 1, 2), (3,)):
-        mine = [merged[k] for k in distances]
-        if projected is not None:
-            mine[-1] = after(mine[-1], projected)
-        mine = mine + [swap_core(block) for block in mine]
-        projected = jnp.dot(
-            jnp.concatenate(mine, axis=0), merge_weight, preferred_element_type=jnp.float32
+    def project_merged(blocks):
+        blocks = blocks + [swap_core(block) for block in blocks]
+        return jnp.dot(
+            jnp.concatenate(blocks, axis=0), merge_weight, preferred_element_type=jnp.float32
         ).astype(jnp.bfloat16)
+
+    *nearer, third = gather_line(output_rows)
+    most = project_merged(nearer)
+    last = project_merged([after(third, most)])
+    routed = []
+    for projected, distances in ((most, (0, 1, 2)), (last, (3,))):
         homes = jnp.stack(
             [2 * (height ^ k) + side for side in (core, 1 - core) for k in distances]
         )
@@ -439,27 +502,30 @@
             homes[:, None] * home_cells + jnp.arange(home_cells, dtype=jnp.int32)[None, :]
         ).reshape(-1)
         if bands == 4:
-            shifts = (3, 1, 2)
-            pieces = [
-                (lax.ppermute(projected, "req", [(i, i ^ shift) for i in range(4)]), band ^ shift)
-                for shift in shifts
+            routed += [
+                (lax.ppermute(projected, "req", [(i, i ^ shift) for i in range(4)]), band ^ shift, local)
+                for shift in (3, 1, 2)
             ]
-            pieces.append((projected, band))
-            pieces = [(piece, piece_band * merged_rows + local) for piece, piece_band in pieces]
+            routed.append((projected, band, local))
         else:
             every = jnp.arange(bands, dtype=jnp.int32)[:, None] * merged_rows + local[None, :]
-            pieces = [(lax.all_gather(projected, "req", axis=0, tiled=True), every.reshape(-1))]
-        for piece, merged_index in pieces:
-            holding = (cell_start[None, :] <= merged_index[:, None]) & (
-                merged_index[:, None] < cell_end[None, :]
+            routed.append(
+                (lax.all_gather(projected, "req", axis=0, tiled=True), 0, every.reshape(-1))
             )
-            holding = holding & (owners == band)[None, :]
-            target = jnp.sum(
-                jnp.where(holding, merged_index[:, None] + (preceding - cell_start)[None, :] + 1, 0),
-                axis=1,
-            )
-            chosen = (target[None, :] == slots[:, None] + 1).astype(jnp.bfloat16)
-            returned = returned + jnp.dot(chosen, piece, preferred_element_type=jnp.float32)
+    returned = jnp.zeros((merged_rows, merge_weight.shape[1]), jnp.float32)
+    for piece, piece_band, local in routed:
+        merged_index = piece_band * merged_rows + local
+        holding = (cell_start[None, :] <= merged_index[:, None]) & (
+            merged_index[:, None] < cell_end[None, :]
+        )
+        holding = holding & (owners == band)[None, :]
+        target = jnp.sum(
+            jnp.where(holding, merged_index[:, None] + (preceding - cell_start)[None, :] + 1, 0),
+            axis=1,
+        )
+        chosen = (target[None, :] == slots[:, None] + 1).astype(jnp.bfloat16)
+        piece = after(piece, last)
+        returned = returned + jnp.dot(chosen, piece, preferred_element_type=jnp.float32)
     return returned.astype(jnp.bfloat16)[None]
 
 

time: 195 us -> 185 us (0.949)
  waiting for transfers between devices: 73.2 us -> 43.9 us
  local copies, waits for them, and re-layouts: 11.3 us -> 25.7 us
  starting transfers between devices: 35.9 us -> 44 us
  Pallas kernels: 61.6 us -> 58.1 us
  other arithmetic: 4.21 us -> 1.74 us
  matrix products: 8.06 us -> 10.5 us
    ppermute x12 -> x16, waiting for transfers between devices: 50.9 us -> 28.2 us  [along_hid(): lax.ppermute(value, 'hid', [(2 * a + core, 2 * b + core) for a, b in pair...]
    unnamed x37 -> x99, local copies, waits for them, and re-layouts: 7.77 us -> 23.5 us
    ppermute x6, waiting for transfers between devices: 10.9 us -> 3.35 us  [on_device(): lax.ppermute(projected, 'req', [(i, i ^ shift) for i in range(4)])]
    ppermute x12 -> x16, starting transfers between devices: 19.8 us -> 25.4 us  [along_hid(): lax.ppermute(value, 'hid', [(2 * a + core, 2 * b + core) for a, b in pair...]
    pallas_call x8, Pallas kernels: 48.5 us -> 45.2 us  [the longest x4 22.1 us: mlp(): pl.pallas_call(functools.partial(mlp_kernel, distance), grid=(1,), in_spe...]
    dot_general x2, matrix products: 5.16 us -> 7.64 us  [project_merged(): jnp.dot(jnp.concatenate(blocks, axis=0), merge_weight, preferred_element_...]
    ppermute x12 -> x16, waiting for transfers between devices: 3.34 us -> 5.43 us  [swap_core(): return lax.ppermute(value, 'hid', [(i, i ^ 1) for i in range(8)])]
  transfers between devices with their start and end apart: 34 -> 42, of which waited for: 15 -> 14; matrix products, arithmetic and copies ran while one was open for 5% -> 7% of each run, Pallas kernels for 22% -> 23%
where the time goes in v3:
time: 185 us
  Pallas kernels  58.1 us (31%)
  starting transfers between devices  44 us (24%)
  waiting for transfers between devices  43.9 us (24%)
  local copies, waits for them, and re-layouts  25.7 us (14%)
  matrix products  10.5 us (6%)
    ppermute x16, waiting for transfers between devices, along_hid(): lax.ppermute(value, 'hid', [(2 * a + core, 2 * b + core) for a, b in pair...  28.2 us
    ppermute x16, starting transfers between devices, along_hid(): lax.ppermute(value, 'hid', [(2 * a + core, 2 * b + core) for a, b in pair...  25.4 us
    unnamed x99, local copies, waits for them, and re-layouts  23.5 us
    pallas_call x4, Pallas kernels, mlp(): pl.pallas_call(functools.partial(mlp_kernel, distance), grid=(1,), in_spe...  22.1 us
    pallas_call x3, Pallas kernels, attend(): pl.pallas_call(functools.partial(attend_kernel, heads, len(states) // hea...  21.7 us
    pallas_call x1, Pallas kernels, project(): pl.pallas_call(project_kernel, grid_spec=pltpu.PrefetchScalarGridSpec(num...  9.63 us
    dot_general x2, matrix products, project_merged(): jnp.dot(jnp.concatenate(blocks, axis=0), merge_weight, preferred_element_...  7.64 us
    ppermute x6, starting transfers between devices, on_device(): lax.ppermute(projected, 'req', [(i, i ^ shift) for i in range(4)])  7.11 us
  transfers between devices with their start and end apart: 42, of which 14 were waited for; matrix products, arithmetic and copies ran while one was open for 7% of the time, Pallas kernels for 23%

profile of v3, /device:TPU:0, one launch (start us, length us, event | category | flops | bytes accessed | tf_op | source)
XLA Modules:
  0.0 184.7 jit_solution(2716261036789261760)
XLA Ops:
  0.0 9.6 %shard_map.118 = (bf16[1024,1408]{1,0:T(8,128)(2,1)}, bf16[176,1024]{1,0:T(8,128)(2,1)}, bf16[176,1024]{1,0:T(8,128)(2,1)}, bf16[176,1024]{1,0:T(8,128)(2,1)}) custom-call(s32[1]{0:T(128)} %bitcast.18.base_ref, s32[2,32]{1,0:T(2,128)} %bitcast.66, bf16[1024,1408]{1,0:T(8,128)(2,1)} %patches_ref.1, bf16[32,1408]{1,0:T(8,128)(2,1)} %row_ref.1, ...), custom_call_target="tpu_custom_call" | custom-call | flops 1522532352 | bytes 5767168 | tf_op jit(solution)/shard_map/pallas_call | solution.py:84
  9.6 2.9 %collective-permute-start = (bf16[176,1024]{1,0:T(8,128)(2,1)}, bf16[176,1024]{1,0:T(8,128)(2,1)S(1)}, u32[]{:S(2)}, u32[]{:S(2)}) collective-permute-start(bf16[176,1024]{1,0:T(8,128)(2,1)} %get-tuple-element.48.rest_0_), channel_id=1, source_target_pairs={{0,8},{8,0},{16,24},{24,16},{1,9},{9,1},{17,25},{25,17},{2,10},{10... | collective-permute-start | bytes 1081352 | tf_op jit(solution)/shard_map/ppermute | solution.py:366
  14.3 14.0 %shard_map.119 = (f32[1,1024]{1,0:T(1,128)}, f32[1,1024]{1,0:T(1,128)}, f32[88,1024]{1,0:T(8,128)}, f32[1,1024]{1,0:T(1,128)}, f32[1,1024]{1,0:T(1,128)}, /*index=5*/f32[88,1024]{1,0:T(8,128)}) custom-call(s32[4]{0:T(128)} %bitcast.76, s32[4]{0:T(128)} %bitcast.79, s32[1]{0:T(128)} %bitcast.18.base_ref, s32[1,1024]{1,0:T(1,128)} %bitcast.72, ...), custom_call_target="tpu_custom_call" | custom-call | flops 738197504 | bytes 1441792 | tf_op jit(solution)/shard_map/pallas_call | solution.py:186
  28.3 3.9 %collective-permute-start.1 = (bf16[176,1024]{1,0:T(8,128)(2,1)S(1)}, bf16[176,1024]{1,0:T(8,128)(2,1)S(1)}, u32[]{:S(2)}, u32[]{:S(2)}) collective-permute-start(bf16[176,1024]{1,0:T(8,128)(2,1)S(1)} %collective-permute-done.rest_3_), channel_id=1, source_target_pairs={{0,16},{24,8},{1,17},{25,9},{2,18},{26,10},{3,19},{27,11},{4,20},{... | collective-permute-start | bytes 1081352 | tf_op jit(solution)/shard_map/ppermute | solution.py:372
  32.2 1.3 collective-permute-start.11
  34.2 6.9 %collective-permute-done.1.rest_4_ = bf16[176,1024]{1,0:T(8,128)(2,1)S(1)} collective-permute-done((bf16[176,1024]{1,0:T(8,128)(2,1)S(1)}, bf16[176,1024]{1,0:T(8,128)(2,1)S(1)}, u32[]{:S(2)}, u32[]{:S(2)}) %collective-permute-start.1) | collective-permute-done | bytes 360480 | tf_op jit(solution)/shard_map/ppermute | solution.py:372
  41.8 3.9 %shard_map.120.refs_0_ = bf16[88,1024]{1,0:T(8,128)(2,1)} custom-call(s32[4]{0:T(128)} %bitcast.77, s32[4]{0:T(128)} %bitcast.80, s32[2]{0:T(128)} %and_select_fusion.base_ref, s32[1,1024]{1,0:T(1,128)} %bitcast.73, s32[1,1024]{1,0:T(1,128)} %bitcast.69, bf16[176,1024]{1,0:T(8,128)(2,1)} %get-tuple-element.47.q_ref, f32[1,1024]{1,0:T(1,128)} %get-tuple-element.50.rest_0_, ...), custom_call_target="tpu_custom_call" | custom-call | flops 369098752 | bytes 720896 | tf_op jit(solution)/shard_map/pallas_call | solution.py:186
  45.7 2.6 %collective-permute-start.3 = (bf16[88,1024]{1,0:T(8,128)(2,1)}, bf16[88,1024]{1,0:T(8,128)(2,1)}, u32[]{:S(2)}, u32[]{:S(2)}) collective-permute-start(bf16[88,1024]{1,0:T(8,128)(2,1)} %shard_map.120.refs_0_), channel_id=1, source_target_pairs={{0,4},{1,5},{4,0},{5,1},{2,6},{3,7},{6,2},{7,3},{8,12},{9,13},{12,... | collective-permute-start | bytes 540680 | tf_op jit(solution)/shard_map/ppermute | solution.py:338
  49.0 3.9 %shard_map.122.refs_5_.refs_8_ = bf16[88,1024]{1,0:T(8,128)(2,1)} custom-call(s32[4]{0:T(128)} %bitcast.78, s32[4]{0:T(128)} %bitcast.81, s32[2]{0:T(128)} %and_select_fusion.base_ref, s32[1,1024]{1,0:T(1,128)} %bitcast.74, s32[1,1024]{1,0:T(1,128)} %bitcast.70, bf16[176,1024]{1,0:T(8,128)(2,1)} %get-tuple-element.47.q_ref, ...), custom_call_target="tpu_custom_call" | custom-call | flops 369098752 | bytes 720896 | tf_op jit(solution)/shard_map/pallas_call | solution.py:186
  52.9 1.3 collective-permute-start.13
  54.3 1.6 collective-permute-start.2
  55.9 2.1 %copy-done.7 = bf16[1408,1408]{1,0:T(8,128)(2,1)S(1)} copy-done((bf16[1408,1408]{1,0:T(8,128)(2,1)S(1)}, bf16[1408,1408]{1,0:T(8,128)(2,1)}, u32[]{:S(2)}) %copy-start.7) | copy-done | bytes 3964952
  58.0 1.6 copy-done.32
  59.6 1.6 copy-done.33
  61.2 1.4 shard_map.123
  63.4 1.3 collective-permute-start.5
  65.3 1.5 collective-permute-start.15
  66.9 5.2 %collective-permute-start.12 = (bf16[88,1024]{1,0:T(8,128)(2,1)}, bf16[88,1024]{1,0:T(8,128)(2,1)S(1)}, u32[]{:S(2)}, u32[]{:S(2)}) collective-permute-start(bf16[88,1024]{1,0:T(8,128)(2,1)} %shard_map.122.refs_5_.refs_8_), channel_id=1, source_target_pairs={{0,2},{1,3},{2,0},{3,1},{4,6},{5,7},{6,4},{7,5},{8,10},{9,11},{10,... | collective-permute-start | bytes 540680 | tf_op jit(solution)/shard_map/ppermute | solution.py:338
  72.7 4.5 %collective-permute-done.15.refs_1_ = bf16[88,1024]{1,0:T(8,128)(2,1)S(1)} collective-permute-done((bf16[88,1024]{1,0:T(8,128)(2,1)S(1)}, bf16[88,1024]{1,0:T(8,128)(2,1)S(1)}, u32[]{:S(2)}, u32[]{:S(2)}) %collective-permute-start.15) | collective-permute-done | bytes 180256 | tf_op jit(solution)/shard_map/ppermute | solution.py:338
  77.9 1.6 collective-permute-done.12.refs_9_
  81.4 1.0 copy-done.10
  82.4 5.1 %shard_map.125 = (bf16[128,1408]{1,0:T(8,128)(2,1)S(1)}, bf16[128,1408]{1,0:T(8,128)(2,1)S(1)}) custom-call(s32[2]{0:T(128)S(1)} %pad_add_fusion.refs_3_.place_ref, bf16[88,1024]{1,0:T(8,128)(2,1)S(1)} %copy-done.8, bf16[88,1024]{1,0:T(8,128)(2,1)S(1)} %collective-permute-done.2.refs_1_, bf16[88,1024]{1,0:T(8,128)(2,1)} %collective-permute-done.3.refs_2_, ...), custom_call_target="tpu_custom_call" | custom-call | flops 2122317824 | bytes 11173888 | tf_op jit(solution)/shard_map/pallas_call | solution.py:285
  87.9 1.4 collective-permute-done.20.refs_1_
  90.1 2.4 %collective-permute-start.22 = (bf16[128,1408]{1,0:T(8,128)(2,1)}, bf16[128,1408]{1,0:T(8,128)(2,1)}, u32[]{:S(2)}, u32[]{:S(2)}) collective-permute-start(bf16[128,1408]{1,0:T(8,128)(2,1)} %shard_map.126), channel_id=1, source_target_pairs={{0,2},{1,3},{6,4},{7,5},{8,10},{9,11},{14,12},{15,13},{16,18},{17,... | collective-permute-start | bytes 1081352 | tf_op jit(solution)/shard_map/ppermute | solution.py:338
  92.5 5.9 %shard_map.127 = (bf16[128,1408]{1,0:T(8,128)(2,1)S(1)}, bf16[128,1408]{1,0:T(8,128)(2,1)}) custom-call(s32[2]{0:T(128)S(1)} %pad_add_fusion.refs_3_.place_ref, bf16[88,1024]{1,0:T(8,128)(2,1)S(1)} %copy-done.8, bf16[88,1024]{1,0:T(8,128)(2,1)S(1)} %collective-permute-done.2.refs_1_, bf16[88,1024]{1,0:T(8,128)(2,1)} %collective-permute-done.3.refs_2_, ...), custom_call_target="tpu_custom_call" | custom-call | flops 2122317824 | bytes 11173888 | tf_op jit(solution)/shard_map/pallas_call | solution.py:285
  99.3 5.9 %shard_map.128 = (bf16[128,1408]{1,0:T(8,128)(2,1)S(1)}, bf16[128,1408]{1,0:T(8,128)(2,1)}) custom-call(s32[2]{0:T(128)S(1)} %pad_add_fusion.refs_3_.place_ref, bf16[88,1024]{1,0:T(8,128)(2,1)S(1)} %copy-done.8, bf16[88,1024]{1,0:T(8,128)(2,1)S(1)} %collective-permute-done.2.refs_1_, bf16[88,1024]{1,0:T(8,128)(2,1)} %collective-permute-done.3.refs_2_, ...), custom_call_target="tpu_custom_call" | custom-call | flops 2122317824 | bytes 11173888 | tf_op jit(solution)/shard_map/pallas_call | solution.py:285
  106.7 1.0 collective-permute-start.24
  108.7 1.2 shard_map.129
  109.9 1.4 collective-permute-start.27
  111.3 1.0 copy-done.35
  112.3 1.1 shard_map.131
  113.4 1.7 collective-permute-start.26
  115.2 2.1 %copy-done.1 = bf16[1408,1408]{1,0:T(8,128)(2,1)S(1)} copy-done((bf16[1408,1408]{1,0:T(8,128)(2,1)S(1)}, bf16[1408,1408]{1,0:T(8,128)(2,1)}, u32[]{:S(2)}) %copy-start.1) | copy-done | bytes 3964952
  117.3 1.6 copy-done.6
  127.2 5.2 %shard_map.130 = (bf16[128,1408]{1,0:T(8,128)(2,1)S(1)}, bf16[128,1408]{1,0:T(8,128)(2,1)S(1)}, bf16[128,1408]{1,0:T(8,128)(2,1)S(1)}) custom-call(s32[2]{0:T(128)S(1)} %pad_add_fusion.refs_3_.place_ref, bf16[88,1024]{1,0:T(8,128)(2,1)S(1)} %copy-done.8, bf16[88,1024]{1,0:T(8,128)(2,1)S(1)} %copy-done.13, bf16[88,1024]{1,0:T(8,128)(2,1)} %collective-permute-done.3.refs_2_, ...), custom_call_target="tpu_custom_call" | custom-call | flops 2122317824 | bytes 11173888 | tf_op jit(solution)/shard_map/pallas_call | solution.py:285
  133.0 1.1 collective-permute-done.23
  134.6 1.4 collective-permute-start.29
  136.7 17.0 %collective-permute-done.29 = bf16[32,5632]{1,0:T(8,128)(2,1)S(1)} collective-permute-done((bf16[32,5632]{1,0:T(8,128)(2,1)S(1)}, bf16[32,5632]{1,0:T(8,128)(2,1)S(1)}, u32[]{:S(2)}, u32[]{:S(2)}) %collective-permute-start.29) | collective-permute-done | bytes 360480 | tf_op jit(solution)/shard_map/ppermute | solution.py:338
  154.4 1.3 collective-permute-start.35
  156.3 1.6 collective-permute-done.31
  158.0 3.9 %convolution_convert_fusion = bf16[192,512]{1,0:T(8,128)(2,1)S(1)} fusion(bf16[192,5632]{1,0:T(8,128)(2,1)S(1)} %constant_dynamic-update-slice_fusion, bf16[5632,512]{1,0:T(8,128)(2,1)} %param.24), kind=kOutput, calls=%fused_computation.8 | convolution fusion | flops 1107394560 | bytes 8126464 | tf_op jit(solution)/shard_map/dot_general | solution.py:489
  161.9 4.6 %collective-permute-done.35.refs_1_ = bf16[32,5632]{1,0:T(8,128)(2,1)S(1)} collective-permute-done((bf16[32,5632]{1,0:T(8,128)(2,1)S(1)}, bf16[32,5632]{1,0:T(8,128)(2,1)S(1)}, u32[]{:S(2)}, u32[]{:S(2)}) %collective-permute-start.35) | collective-permute-done | bytes 360480 | tf_op jit(solution)/shard_map/ppermute | solution.py:338
  168.9 2.3 %collective-permute-start.33 = (bf16[192,512]{1,0:T(8,128)(2,1)S(1)}, bf16[192,512]{1,0:T(8,128)(2,1)S(1)}, u32[]{:S(2)}, u32[]{:S(2)}) collective-permute-start(bf16[192,512]{1,0:T(8,128)(2,1)S(1)} %convolution_convert_fusion), channel_id=1, source_target_pairs={{0,24},{8,16},{16,8},{24,0},{1,25},{9,17},{17,9},{25,1},{2,26},{10... | collective-permute-start | bytes 589832 | tf_op jit(solution)/shard_map/ppermute | solution.py:506
  171.2 3.7 %convolution_convert_fusion.1 = bf16[64,512]{1,0:T(8,128)(2,1)S(1)} fusion(bf16[5632,512]{1,0:T(8,128)(2,1)} %param.24, bf16[32,5632]{1,0:T(8,128)(2,1)S(1)} %collective-permute-done.36, bf16[32,5632]{1,0:T(8,128)(2,1)S(1)} %shard_map.132), kind=kOutput, calls=%fused_computation.10 | convolution fusion | flops 370573312 | bytes 6553600 | tf_op jit(solution)/shard_map/dot_general | solution.py:489
  174.9 1.0 collective-permute-start.41
  176.2 2.3 %collective-permute-start.39 = (bf16[64,512]{1,0:T(8,128)(2,1)S(1)}, bf16[64,512]{1,0:T(8,128)(2,1)S(1)}, u32[]{:S(2)}, u32[]{:S(2)}) collective-permute-start(bf16[64,512]{1,0:T(8,128)(2,1)S(1)} %convolution_convert_fusion.1), channel_id=1, source_target_pairs={{0,24},{8,16},{16,8},{24,0},{1,25},{9,17},{17,9},{25,1},{2,26},{10... | collective-permute-start | bytes 196616 | tf_op jit(solution)/shard_map/ppermute | solution.py:506
  178.5 2.7 %collective-permute-done.33 = bf16[192,512]{1,0:T(8,128)(2,1)S(1)} collective-permute-done((bf16[192,512]{1,0:T(8,128)(2,1)S(1)}, bf16[192,512]{1,0:T(8,128)(2,1)S(1)}, u32[]{:S(2)}, u32[]{:S(2)}) %collective-permute-start.33) | collective-permute-done | bytes 196640 | tf_op jit(solution)/shard_map/ppermute | solution.py:506
  183.7 1.0 fusion.6
  (191 shorter events, 29.4 us)
Async XLA Ops:
  9.6 18.7 %collective-permute-start = (bf16[176,1024]{1,0:T(8,128)(2,1)}, bf16[176,1024]{1,0:T(8,128)(2,1)S(1)}, u32[]{:S(2)}, u32[]{:S(2)}) collective-permute-start(bf16[176,1024]{1,0:T(8,128)(2,1)} %get-tuple-element.48.rest_0_), channel_id=1, source_target_pairs={{0,8},{8,0},{16,24},{24,16},{1,9},{9,1},{17,25},{25,17},{2,10},{10... | collective-permute-start | bytes 1081352 | tf_op jit(solution)/shard_map/ppermute | solution.py:366
  12.6 19.6 %collective-permute-start.10 = (bf16[176,1024]{1,0:T(8,128)(2,1)}, bf16[176,1024]{1,0:T(8,128)(2,1)S(1)}, u32[]{:S(2)}, u32[]{:S(2)}) collective-permute-start(bf16[176,1024]{1,0:T(8,128)(2,1)} %get-tuple-element.49.rest_1_), channel_id=1, source_target_pairs={{0,8},{8,0},{16,24},{24,16},{1,9},{9,1},{17,25},{25,17},{2,10},{10... | collective-permute-start | bytes 1081352 | tf_op jit(solution)/shard_map/ppermute | solution.py:366
  28.3 25.9 %copy-start.38 = (f32[1408]{0:T(1024)S(1)}, f32[1408]{0:T(1024)}, u32[]{:S(2)}) copy-start(f32[1408]{0:T(1024)} %param.21) | copy-start | bytes 16900
  28.3 12.7 %collective-permute-start.1 = (bf16[176,1024]{1,0:T(8,128)(2,1)S(1)}, bf16[176,1024]{1,0:T(8,128)(2,1)S(1)}, u32[]{:S(2)}, u32[]{:S(2)}) collective-permute-start(bf16[176,1024]{1,0:T(8,128)(2,1)S(1)} %collective-permute-done.rest_3_), channel_id=1, source_target_pairs={{0,16},{24,8},{1,17},{25,9},{2,18},{26,10},{3,19},{27,11},{4,20},{... | collective-permute-start | bytes 1081352 | tf_op jit(solution)/shard_map/ppermute | solution.py:372
  32.2 16.0 %collective-permute-start.11 = (bf16[176,1024]{1,0:T(8,128)(2,1)S(1)}, bf16[176,1024]{1,0:T(8,128)(2,1)S(1)}, u32[]{:S(2)}, u32[]{:S(2)}) collective-permute-start(bf16[176,1024]{1,0:T(8,128)(2,1)S(1)} %collective-permute-done.10.rest_3_), channel_id=1, source_target_pairs={{0,16},{24,8},{1,17},{25,9},{2,18},{26,10},{3,19},{27,11},{4,20},{... | collective-permute-start | bytes 1081352 | tf_op jit(solution)/shard_map/ppermute | solution.py:372
  45.7 17.0 %collective-permute-start.3 = (bf16[88,1024]{1,0:T(8,128)(2,1)}, bf16[88,1024]{1,0:T(8,128)(2,1)}, u32[]{:S(2)}, u32[]{:S(2)}) collective-permute-start(bf16[88,1024]{1,0:T(8,128)(2,1)} %shard_map.120.refs_0_), channel_id=1, source_target_pairs={{0,4},{1,5},{4,0},{5,1},{2,6},{3,7},{6,2},{7,3},{8,12},{9,13},{12,... | collective-permute-start | bytes 540680 | tf_op jit(solution)/shard_map/ppermute | solution.py:338
  52.9 10.5 %collective-permute-start.13 = (bf16[88,1024]{1,0:T(8,128)(2,1)}, bf16[88,1024]{1,0:T(8,128)(2,1)S(1)}, u32[]{:S(2)}, u32[]{:S(2)}) collective-permute-start(bf16[88,1024]{1,0:T(8,128)(2,1)} %shard_map.122.refs_5_.refs_8_), channel_id=1, source_target_pairs={{0,4},{1,5},{4,0},{5,1},{2,6},{3,7},{6,2},{7,3},{8,12},{9,13},{12,... | collective-permute-start | bytes 540680 | tf_op jit(solution)/shard_map/ppermute | solution.py:338
  54.3 12.5 %collective-permute-start.2 = (bf16[88,1024]{1,0:T(8,128)(2,1)}, bf16[88,1024]{1,0:T(8,128)(2,1)S(1)}, u32[]{:S(2)}, u32[]{:S(2)}) collective-permute-start(bf16[88,1024]{1,0:T(8,128)(2,1)} %shard_map.120.refs_0_), channel_id=1, source_target_pairs={{0,2},{1,3},{2,0},{3,1},{4,6},{5,7},{6,4},{7,5},{8,10},{9,11},{10,... | collective-permute-start | bytes 540680 | tf_op jit(solution)/shard_map/ppermute | solution.py:338
  62.6 36.6 %copy-start = (bf16[1408,1408]{1,0:T(8,128)(2,1)}, bf16[1408,1408]{1,0:T(8,128)(2,1)S(1)}, u32[]{:S(2)}) copy-start(bf16[1408,1408]{1,0:T(8,128)(2,1)S(1)} %get-tuple-element.63.refs_18_) | copy-start | bytes 11894788
  62.6 36.6 %copy-start.3 = (bf16[1408,768]{1,0:T(8,128)(2,1)}, bf16[1408,768]{1,0:T(8,128)(2,1)S(1)}, u32[]{:S(2)}) copy-start(bf16[1408,768]{1,0:T(8,128)(2,1)S(1)} %get-tuple-element.64.refs_19_) | copy-start | bytes 6488068
  62.6 36.6 %copy-start.5 = (bf16[768,1408]{1,0:T(8,128)(2,1)}, bf16[768,1408]{1,0:T(8,128)(2,1)S(1)}, u32[]{:S(2)}) copy-start(bf16[768,1408]{1,0:T(8,128)(2,1)S(1)} %get-tuple-element.65.refs_20_) | copy-start | bytes 6488068
  62.7 4.3 %collective-permute-start.4 = (bf16[88,1024]{1,0:T(8,128)(2,1)S(1)}, bf16[88,1024]{1,0:T(8,128)(2,1)S(1)}, u32[]{:S(2)}, u32[]{:S(2)}) collective-permute-start(bf16[88,1024]{1,0:T(8,128)(2,1)S(1)} %copy-done.8), channel_id=1, source_target_pairs={{2,4},{3,5},{4,2},{5,3},{10,12},{11,13},{12,10},{13,11},{18,20},{1... | collective-permute-start | bytes 540680 | tf_op jit(solution)/shard_map/ppermute | solution.py:338
  63.4 8.8 %collective-permute-start.5 = (bf16[88,1024]{1,0:T(8,128)(2,1)}, bf16[88,1024]{1,0:T(8,128)(2,1)S(1)}, u32[]{:S(2)}, u32[]{:S(2)}) collective-permute-start(bf16[88,1024]{1,0:T(8,128)(2,1)} %collective-permute-done.3.refs_2_), channel_id=1, source_target_pairs={{2,0},{3,1},{4,6},{5,7},{10,8},{11,9},{12,14},{13,15},{18,16},{19,... | collective-permute-start | bytes 540680 | tf_op jit(solution)/shard_map/ppermute | solution.py:338
  64.7 7.7 %collective-permute-start.14 = (bf16[88,1024]{1,0:T(8,128)(2,1)}, bf16[88,1024]{1,0:T(8,128)(2,1)S(1)}, u32[]{:S(2)}, u32[]{:S(2)}) collective-permute-start(bf16[88,1024]{1,0:T(8,128)(2,1)} %shard_map.122.refs_5_.refs_8_), channel_id=1, source_target_pairs={{2,4},{3,5},{4,2},{5,3},{10,12},{11,13},{12,10},{13,11},{18,20},{1... | collective-permute-start | bytes 540680 | tf_op jit(solution)/shard_map/ppermute | solution.py:338
  65.3 11.9 %collective-permute-start.15 = (bf16[88,1024]{1,0:T(8,128)(2,1)S(1)}, bf16[88,1024]{1,0:T(8,128)(2,1)S(1)}, u32[]{:S(2)}, u32[]{:S(2)}) collective-permute-start(bf16[88,1024]{1,0:T(8,128)(2,1)S(1)} %collective-permute-done.13.refs_10_), channel_id=1, source_target_pairs={{2,0},{3,1},{4,6},{5,7},{10,8},{11,9},{12,14},{13,15},{18,16},{19,... | collective-permute-start | bytes 540680 | tf_op jit(solution)/shard_map/ppermute | solution.py:338
  66.8 32.4 %copy-start.12 = (bf16[88,1024]{1,0:T(8,128)(2,1)}, bf16[88,1024]{1,0:T(8,128)(2,1)S(1)}, u32[]{:S(2)}) copy-start(bf16[88,1024]{1,0:T(8,128)(2,1)S(1)} %collective-permute-done.2.refs_1_) | copy-start | bytes 540676
  66.8 10.4 %collective-permute-start.6 = (bf16[88,1024]{1,0:T(8,128)(2,1)S(1)}, bf16[88,1024]{1,0:T(8,128)(2,1)S(1)}, u32[]{:S(2)}, u32[]{:S(2)}) collective-permute-start(bf16[88,1024]{1,0:T(8,128)(2,1)S(1)} %copy-done.8), channel_id=1, source_target_pairs={{0,1},{1,0},{2,3},{3,2},{4,5},{5,4},{6,7},{7,6},{8,9},{9,8},{10,11... | collective-permute-start | bytes 540680 | tf_op jit(solution)/shard_map/ppermute | solution.py:344
  66.9 12.5 %collective-permute-start.12 = (bf16[88,1024]{1,0:T(8,128)(2,1)}, bf16[88,1024]{1,0:T(8,128)(2,1)S(1)}, u32[]{:S(2)}, u32[]{:S(2)}) collective-permute-start(bf16[88,1024]{1,0:T(8,128)(2,1)} %shard_map.122.refs_5_.refs_8_), channel_id=1, source_target_pairs={{0,2},{1,3},{2,0},{3,1},{4,6},{5,7},{6,4},{7,5},{8,10},{9,11},{10,... | collective-permute-start | bytes 540680 | tf_op jit(solution)/shard_map/ppermute | solution.py:338
  72.2 7.3 %collective-permute-start.16 = (bf16[88,1024]{1,0:T(8,128)(2,1)}, bf16[88,1024]{1,0:T(8,128)(2,1)S(1)}, u32[]{:S(2)}, u32[]{:S(2)}) collective-permute-start(bf16[88,1024]{1,0:T(8,128)(2,1)} %shard_map.122.refs_5_.refs_8_), channel_id=1, source_target_pairs={{0,1},{1,0},{2,3},{3,2},{4,5},{5,4},{6,7},{7,6},{8,9},{9,8},{10,11... | collective-permute-start | bytes 540680 | tf_op jit(solution)/shard_map/ppermute | solution.py:344
  72.3 7.7 %collective-permute-start.7 = (bf16[88,1024]{1,0:T(8,128)(2,1)S(1)}, bf16[88,1024]{1,0:T(8,128)(2,1)S(1)}, u32[]{:S(2)}, u32[]{:S(2)}) collective-permute-start(bf16[88,1024]{1,0:T(8,128)(2,1)S(1)} %collective-permute-done.2.refs_1_), channel_id=1, source_target_pairs={{0,1},{1,0},{2,3},{3,2},{4,5},{5,4},{6,7},{7,6},{8,9},{9,8},{10,11... | collective-permute-start | bytes 540680 | tf_op jit(solution)/shard_map/ppermute | solution.py:344
  77.2 2.8 %collective-permute-start.8 = (bf16[88,1024]{1,0:T(8,128)(2,1)}, bf16[88,1024]{1,0:T(8,128)(2,1)S(1)}, u32[]{:S(2)}, u32[]{:S(2)}) collective-permute-start(bf16[88,1024]{1,0:T(8,128)(2,1)} %collective-permute-done.3.refs_2_), channel_id=1, source_target_pairs={{0,1},{1,0},{2,3},{3,2},{4,5},{5,4},{6,7},{7,6},{8,9},{9,8},{10,11... | collective-permute-start | bytes 540680 | tf_op jit(solution)/shard_map/ppermute | solution.py:344
  77.3 21.9 %copy-start.14 = (bf16[88,1024]{1,0:T(8,128)(2,1)}, bf16[88,1024]{1,0:T(8,128)(2,1)S(1)}, u32[]{:S(2)}) copy-start(bf16[88,1024]{1,0:T(8,128)(2,1)S(1)} %collective-permute-done.6.refs_4_) | copy-start | bytes 540676
  77.3 3.6 %collective-permute-start.18 = (bf16[88,1024]{1,0:T(8,128)(2,1)}, bf16[88,1024]{1,0:T(8,128)(2,1)S(1)}, u32[]{:S(2)}, u32[]{:S(2)}) collective-permute-start(bf16[88,1024]{1,0:T(8,128)(2,1)} %copy-done.9), channel_id=1, source_target_pairs={{0,1},{1,0},{2,3},{3,2},{4,5},{5,4},{6,7},{7,6},{8,9},{9,8},{10,11... | collective-permute-start | bytes 540680 | tf_op jit(solution)/shard_map/ppermute | solution.py:344
  79.5 1.4 collective-permute-start.17
  79.5 1.7 collective-permute-start.9
  80.0 1.4 collective-permute-start.19
  87.5 1.7 collective-permute-start.20
  90.1 17.6 %collective-permute-start.22 = (bf16[128,1408]{1,0:T(8,128)(2,1)}, bf16[128,1408]{1,0:T(8,128)(2,1)}, u32[]{:S(2)}, u32[]{:S(2)}) collective-permute-start(bf16[128,1408]{1,0:T(8,128)(2,1)} %shard_map.126), channel_id=1, source_target_pairs={{0,2},{1,3},{6,4},{7,5},{8,10},{9,11},{14,12},{15,13},{16,18},{17,... | collective-permute-start | bytes 1081352 | tf_op jit(solution)/shard_map/ppermute | solution.py:338
  99.2 8.5 %collective-permute-start.21 = (bf16[128,1408]{1,0:T(8,128)(2,1)}, bf16[128,1408]{1,0:T(8,128)(2,1)}, u32[]{:S(2)}, u32[]{:S(2)}) collective-permute-start(bf16[128,1408]{1,0:T(8,128)(2,1)} %get-tuple-element.70), channel_id=1, source_target_pairs={{0,1},{1,0},{2,3},{3,2},{4,5},{5,4},{6,7},{7,6},{8,9},{9,8},{10,11... | collective-permute-start | bytes 1081352 | tf_op jit(solution)/shard_map/ppermute | solution.py:344
  105.9 5.4 %collective-permute-start.25 = (bf16[128,1408]{1,0:T(8,128)(2,1)}, bf16[128,1408]{1,0:T(8,128)(2,1)}, u32[]{:S(2)}, u32[]{:S(2)}) collective-permute-start(bf16[128,1408]{1,0:T(8,128)(2,1)} %get-tuple-element.78), channel_id=1, source_target_pairs={{0,1},{1,0},{2,3},{3,2},{4,5},{5,4},{6,7},{7,6},{8,9},{9,8},{10,11... | collective-permute-start | bytes 1081352 | tf_op jit(solution)/shard_map/ppermute | solution.py:344
  106.7 25.9 %collective-permute-start.24 = (bf16[128,1408]{1,0:T(8,128)(2,1)}, bf16[128,1408]{1,0:T(8,128)(2,1)S(1)}, u32[]{:S(2)}, u32[]{:S(2)}) collective-permute-start(bf16[128,1408]{1,0:T(8,128)(2,1)} %shard_map.126), channel_id=1, source_target_pairs={{2,4},{3,5},{4,2},{5,3},{10,12},{11,13},{12,10},{13,11},{18,20},{1... | collective-permute-start | bytes 1081352 | tf_op jit(solution)/shard_map/ppermute | solution.py:338
  109.9 23.1 %collective-permute-start.27 = (bf16[128,1408]{1,0:T(8,128)(2,1)S(1)}, bf16[128,1408]{1,0:T(8,128)(2,1)S(1)}, u32[]{:S(2)}, u32[]{:S(2)}) collective-permute-start(bf16[128,1408]{1,0:T(8,128)(2,1)S(1)} %shard_map.129), channel_id=1, source_target_pairs={{0,4},{1,5},{4,0},{5,1},{2,6},{3,7},{6,2},{7,3},{8,12},{9,13},{12,... | collective-permute-start | bytes 1081352 | tf_op jit(solution)/shard_map/ppermute | solution.py:338
  113.4 19.6 %collective-permute-start.26 = (bf16[128,1408]{1,0:T(8,128)(2,1)S(1)}, bf16[128,1408]{1,0:T(8,128)(2,1)S(1)}, u32[]{:S(2)}, u32[]{:S(2)}) collective-permute-start(bf16[128,1408]{1,0:T(8,128)(2,1)S(1)} %shard_map.131), channel_id=1, source_target_pairs={{0,2},{1,3},{2,0},{3,1},{4,6},{5,7},{6,4},{7,5},{8,10},{9,11},{10,... | collective-permute-start | bytes 1081352 | tf_op jit(solution)/shard_map/ppermute | solution.py:338
  132.4 1.7 collective-permute-start.23
  134.6 19.0 %collective-permute-start.29 = (bf16[32,5632]{1,0:T(8,128)(2,1)S(1)}, bf16[32,5632]{1,0:T(8,128)(2,1)S(1)}, u32[]{:S(2)}, u32[]{:S(2)}) collective-permute-start(bf16[32,5632]{1,0:T(8,128)(2,1)S(1)} %reshape.271), channel_id=1, source_target_pairs={{0,4},{1,5},{4,0},{5,1},{2,6},{3,7},{6,2},{7,3},{8,12},{9,13},{12,... | collective-permute-start | bytes 1081352 | tf_op jit(solution)/shard_map/ppermute | solution.py:338
  136.0 19.7 %collective-permute-start.28 = (bf16[32,5632]{1,0:T(8,128)(2,1)S(1)}, bf16[32,5632]{1,0:T(8,128)(2,1)S(1)}, u32[]{:S(2)}, u32[]{:S(2)}) collective-permute-start(bf16[32,5632]{1,0:T(8,128)(2,1)S(1)} %reshape.271), channel_id=1, source_target_pairs={{0,2},{1,3},{2,0},{3,1},{4,6},{5,7},{6,4},{7,5},{8,10},{9,11},{10,... | collective-permute-start | bytes 1081352 | tf_op jit(solution)/shard_map/ppermute | solution.py:338
  136.7 19.6 %collective-permute-start.30 = (bf16[32,5632]{1,0:T(8,128)(2,1)S(1)}, bf16[32,5632]{1,0:T(8,128)(2,1)S(1)}, u32[]{:S(2)}, u32[]{:S(2)}) collective-permute-start(bf16[32,5632]{1,0:T(8,128)(2,1)S(1)} %reshape.271), channel_id=1, source_target_pairs={{0,1},{1,0},{2,3},{3,2},{4,5},{5,4},{6,7},{7,6},{8,9},{9,8},{10,11... | collective-permute-start | bytes 1081352 | tf_op jit(solution)/shard_map/ppermute | solution.py:344
  153.7 8.2 %collective-permute-start.34 = (bf16[32,5632]{1,0:T(8,128)(2,1)S(1)}, bf16[32,5632]{1,0:T(8,128)(2,1)S(1)}, u32[]{:S(2)}, u32[]{:S(2)}) collective-permute-start(bf16[32,5632]{1,0:T(8,128)(2,1)S(1)} %reshape.271), channel_id=1, source_target_pairs={{2,4},{3,5},{4,2},{5,3},{10,12},{11,13},{12,10},{13,11},{18,20},{1... | collective-permute-start | bytes 1081352 | tf_op jit(solution)/shard_map/ppermute | solution.py:338
  154.4 12.2 %collective-permute-start.35 = (bf16[32,5632]{1,0:T(8,128)(2,1)S(1)}, bf16[32,5632]{1,0:T(8,128)(2,1)S(1)}, u32[]{:S(2)}, u32[]{:S(2)}) collective-permute-start(bf16[32,5632]{1,0:T(8,128)(2,1)S(1)} %collective-permute-done.29), channel_id=1, source_target_pairs={{2,0},{3,1},{4,6},{5,7},{10,8},{11,9},{12,14},{13,15},{18,16},{19,... | collective-permute-start | bytes 1081352 | tf_op jit(solution)/shard_map/ppermute | solution.py:338
  155.7 2.3 %collective-permute-start.32 = (bf16[32,5632]{1,0:T(8,128)(2,1)S(1)}, bf16[32,5632]{1,0:T(8,128)(2,1)S(1)}, u32[]{:S(2)}, u32[]{:S(2)}) collective-permute-start(bf16[32,5632]{1,0:T(8,128)(2,1)S(1)} %collective-permute-done.29), channel_id=1, source_target_pairs={{0,1},{1,0},{2,3},{3,2},{4,5},{5,4},{6,7},{7,6},{8,9},{9,8},{10,11... | collective-permute-start | bytes 1081352 | tf_op jit(solution)/shard_map/ppermute | solution.py:344
  155.7 2.2 %collective-permute-start.31 = (bf16[32,5632]{1,0:T(8,128)(2,1)S(1)}, bf16[32,5632]{1,0:T(8,128)(2,1)S(1)}, u32[]{:S(2)}, u32[]{:S(2)}) collective-permute-start(bf16[32,5632]{1,0:T(8,128)(2,1)S(1)} %collective-permute-done.28), channel_id=1, source_target_pairs={{0,1},{1,0},{2,3},{3,2},{4,5},{5,4},{6,7},{7,6},{8,9},{9,8},{10,11... | collective-permute-start | bytes 1081352 | tf_op jit(solution)/shard_map/ppermute | solution.py:344
  166.6 4.5 %collective-permute-start.36 = (bf16[32,5632]{1,0:T(8,128)(2,1)S(1)}, bf16[32,5632]{1,0:T(8,128)(2,1)S(1)}, u32[]{:S(2)}, u32[]{:S(2)}) collective-permute-start(bf16[32,5632]{1,0:T(8,128)(2,1)S(1)} %shard_map.132), channel_id=1, source_target_pairs={{0,1},{1,0},{2,3},{3,2},{4,5},{5,4},{6,7},{7,6},{8,9},{9,8},{10,11... | collective-permute-start | bytes 1081352 | tf_op jit(solution)/shard_map/ppermute | solution.py:344
  167.6 8.6 %collective-permute-start.38 = (bf16[192,512]{1,0:T(8,128)(2,1)S(1)}, bf16[192,512]{1,0:T(8,128)(2,1)S(1)}, u32[]{:S(2)}, u32[]{:S(2)}) collective-permute-start(bf16[192,512]{1,0:T(8,128)(2,1)S(1)} %convolution_convert_fusion), channel_id=1, source_target_pairs={{0,16},{8,24},{16,0},{24,8},{1,17},{9,25},{17,1},{25,9},{2,18},{10... | collective-permute-start | bytes 589832 | tf_op jit(solution)/shard_map/ppermute | solution.py:506
  168.6 9.9 %collective-permute-start.37 = (bf16[192,512]{1,0:T(8,128)(2,1)S(1)}, bf16[192,512]{1,0:T(8,128)(2,1)S(1)}, u32[]{:S(2)}, u32[]{:S(2)}) collective-permute-start(bf16[192,512]{1,0:T(8,128)(2,1)S(1)} %convolution_convert_fusion), channel_id=1, source_target_pairs={{0,8},{8,0},{16,24},{24,16},{1,9},{9,1},{17,25},{25,17},{2,10},{10... | collective-permute-start | bytes 589832 | tf_op jit(solution)/shard_map/ppermute | solution.py:506
  168.9 12.2 %collective-permute-start.33 = (bf16[192,512]{1,0:T(8,128)(2,1)S(1)}, bf16[192,512]{1,0:T(8,128)(2,1)S(1)}, u32[]{:S(2)}, u32[]{:S(2)}) collective-permute-start(bf16[192,512]{1,0:T(8,128)(2,1)S(1)} %convolution_convert_fusion), channel_id=1, source_target_pairs={{0,24},{8,16},{16,8},{24,0},{1,25},{9,17},{17,9},{25,1},{2,26},{10... | collective-permute-start | bytes 589832 | tf_op jit(solution)/shard_map/ppermute | solution.py:506
  174.9 7.6 %collective-permute-start.41 = (bf16[64,512]{1,0:T(8,128)(2,1)S(1)}, bf16[64,512]{1,0:T(8,128)(2,1)S(1)}, u32[]{:S(2)}, u32[]{:S(2)}) collective-permute-start(bf16[64,512]{1,0:T(8,128)(2,1)S(1)} %convolution_convert_fusion.1), channel_id=1, source_target_pairs={{0,16},{8,24},{16,0},{24,8},{1,17},{9,25},{17,1},{25,9},{2,18},{10... | collective-permute-start | bytes 196616 | tf_op jit(solution)/shard_map/ppermute | solution.py:506
  175.9 6.6 %collective-permute-start.40 = (bf16[64,512]{1,0:T(8,128)(2,1)S(1)}, bf16[64,512]{1,0:T(8,128)(2,1)S(1)}, u32[]{:S(2)}, u32[]{:S(2)}) collective-permute-start(bf16[64,512]{1,0:T(8,128)(2,1)S(1)} %convolution_convert_fusion.1), channel_id=1, source_target_pairs={{0,8},{8,0},{16,24},{24,16},{1,9},{9,1},{17,25},{25,17},{2,10},{10... | collective-permute-start | bytes 196616 | tf_op jit(solution)/shard_map/ppermute | solution.py:506
  176.2 7.0 %collective-permute-start.39 = (bf16[64,512]{1,0:T(8,128)(2,1)S(1)}, bf16[64,512]{1,0:T(8,128)(2,1)S(1)}, u32[]{:S(2)}, u32[]{:S(2)}) collective-permute-start(bf16[64,512]{1,0:T(8,128)(2,1)S(1)} %convolution_convert_fusion.1), channel_id=1, source_target_pairs={{0,24},{8,16},{16,8},{24,0},{1,25},{9,17},{17,9},{25,1},{2,26},{10... | collective-permute-start | bytes 196616 | tf_op jit(solution)/shard_map/ppermute | solution.py:506
  (41 other events, 292.1 us)

commit v4 on v3

--- a/solution.py
+++ b/solution.py
@@ -85,20 +85,20 @@
         project_kernel,
         grid_spec=pltpu.PrefetchScalarGridSpec(
             num_scalar_prefetch=1,
-            grid=(rows // TILE,),
+            grid=(rows // 512,),
             in_specs=[
                 whole(grid.shape),
-                pl.BlockSpec((TILE, model), lambda i, _: (i, 0)),
+                pl.BlockSpec((512, model), lambda i, _: (i, 0)),
                 whole(row_table.shape),
                 whole(col_table.shape),
                 whole(gain.shape),
                 whole(weight.shape),
             ],
             out_specs=[
-                pl.BlockSpec((TILE, model), lambda i, _: (i, 0)),
-                pl.BlockSpec((width, TILE), lambda i, _: (0, i)),
+                pl.BlockSpec((512, model), lambda i, _: (i, 0)),
+                pl.BlockSpec((width, 512), lambda i, _: (0, i)),
             ]
-            + [pl.BlockSpec((2 * HEAD_DIM, TILE), lambda i, _: (0, i))] * (width // HEAD_DIM),
+            + [pl.BlockSpec((2 * HEAD_DIM, 512), lambda i, _: (0, i))] * (width // HEAD_DIM),
         ),
         out_shape=[
             jax.ShapeDtypeStruct((rows, model), jnp.bfloat16),

time: 185 us -> 185 us (level)
  starting transfers between devices: 44 us -> 45.9 us
    ppermute x6, starting transfers between devices: 7.11 us -> 9.17 us  [on_device(): lax.ppermute(projected, 'req', [(i, i ^ shift) for i in range(4)])]
  transfers between devices with their start and end apart: 42 -> 42, of which waited for: 14 -> 15; matrix products, arithmetic and copies ran while one was open for 7% -> 7% of each run, Pallas kernels for 23% -> 23%
where the time goes in v4:
time: 185 us
  Pallas kernels  57.7 us (31%)
  starting transfers between devices  45.9 us (25%)
  waiting for transfers between devices  42.3 us (23%)
  local copies, waits for them, and re-layouts  25.7 us (14%)
  matrix products  10.5 us (6%)
    ppermute x16, waiting for transfers between devices, along_hid(): lax.ppermute(value, 'hid', [(2 * a + core, 2 * b + core) for a, b in pair...  28.2 us
    ppermute x16, starting transfers between devices, along_hid(): lax.ppermute(value, 'hid', [(2 * a + core, 2 * b + core) for a, b in pair...  26.1 us
    unnamed x99, local copies, waits for them, and re-layouts  23.5 us
    pallas_call x4, Pallas kernels, mlp(): pl.pallas_call(functools.partial(mlp_kernel, distance), grid=(1,), in_spe...  22.1 us
    pallas_call x3, Pallas kernels, attend(): pl.pallas_call(functools.partial(attend_kernel, heads, len(states) // hea...  21.7 us
    ppermute x6, starting transfers between devices, on_device(): lax.ppermute(projected, 'req', [(i, i ^ shift) for i in range(4)])  9.17 us
    pallas_call x1, Pallas kernels, project(): pl.pallas_call(project_kernel, grid_spec=pltpu.PrefetchScalarGridSpec(num...  9.16 us
    dot_general x2, matrix products, project_merged(): jnp.dot(jnp.concatenate(blocks, axis=0), merge_weight, preferred_element_...  7.64 us
  transfers between devices with their start and end apart: 42, of which 15 were waited for; matrix products, arithmetic and copies ran while one was open for 7% of the time, Pallas kernels for 23%

profile of v4, /device:TPU:0, one launch (start us, length us, event | category | flops | bytes accessed | tf_op | source)
XLA Modules:
  0.0 184.6 jit_solution(4361708547470636017)
XLA Ops:
  0.0 9.2 %shard_map.118 = (bf16[1024,1408]{1,0:T(8,128)(2,1)}, bf16[176,1024]{1,0:T(8,128)(2,1)}, bf16[176,1024]{1,0:T(8,128)(2,1)}, bf16[176,1024]{1,0:T(8,128)(2,1)}) custom-call(s32[1]{0:T(128)} %bitcast.18.base_ref, s32[2,32]{1,0:T(2,128)} %bitcast.66, bf16[1024,1408]{1,0:T(8,128)(2,1)} %patches_ref.1, bf16[32,1408]{1,0:T(8,128)(2,1)} %row_ref.1, ...), custom_call_target="tpu_custom_call" | custom-call | flops 1522532352 | bytes 5767168 | tf_op jit(solution)/shard_map/pallas_call | solution.py:84
  9.2 2.9 %collective-permute-start = (bf16[176,1024]{1,0:T(8,128)(2,1)}, bf16[176,1024]{1,0:T(8,128)(2,1)S(1)}, u32[]{:S(2)}, u32[]{:S(2)}) collective-permute-start(bf16[176,1024]{1,0:T(8,128)(2,1)} %get-tuple-element.48.rest_0_), channel_id=1, source_target_pairs={{0,8},{8,0},{16,24},{24,16},{1,9},{9,1},{17,25},{25,17},{2,10},{10... | collective-permute-start | bytes 1081352 | tf_op jit(solution)/shard_map/ppermute | solution.py:366
  13.8 14.0 %shard_map.119 = (f32[1,1024]{1,0:T(1,128)}, f32[1,1024]{1,0:T(1,128)}, f32[88,1024]{1,0:T(8,128)}, f32[1,1024]{1,0:T(1,128)}, f32[1,1024]{1,0:T(1,128)}, /*index=5*/f32[88,1024]{1,0:T(8,128)}) custom-call(s32[4]{0:T(128)} %bitcast.76, s32[4]{0:T(128)} %bitcast.79, s32[1]{0:T(128)} %bitcast.18.base_ref, s32[1,1024]{1,0:T(1,128)} %bitcast.72, ...), custom_call_target="tpu_custom_call" | custom-call | flops 738197504 | bytes 1441792 | tf_op jit(solution)/shard_map/pallas_call | solution.py:186
  27.8 1.3 collective-permute-start.1
  29.2 3.0 %collective-permute-start.11 = (bf16[176,1024]{1,0:T(8,128)(2,1)S(1)}, bf16[176,1024]{1,0:T(8,128)(2,1)S(1)}, u32[]{:S(2)}, u32[]{:S(2)}) collective-permute-start(bf16[176,1024]{1,0:T(8,128)(2,1)S(1)} %collective-permute-done.10.rest_3_), channel_id=1, source_target_pairs={{0,16},{24,8},{1,17},{25,9},{2,18},{26,10},{3,19},{27,11},{4,20},{... | collective-permute-start | bytes 1081352 | tf_op jit(solution)/shard_map/ppermute | solution.py:372
  32.8 5.2 %collective-permute-done.1.rest_4_ = bf16[176,1024]{1,0:T(8,128)(2,1)S(1)} collective-permute-done((bf16[176,1024]{1,0:T(8,128)(2,1)S(1)}, bf16[176,1024]{1,0:T(8,128)(2,1)S(1)}, u32[]{:S(2)}, u32[]{:S(2)}) %collective-permute-start.1) | collective-permute-done | bytes 360480 | tf_op jit(solution)/shard_map/ppermute | solution.py:372
  38.7 3.9 %shard_map.120.refs_0_ = bf16[88,1024]{1,0:T(8,128)(2,1)} custom-call(s32[4]{0:T(128)} %bitcast.77, s32[4]{0:T(128)} %bitcast.80, s32[2]{0:T(128)} %and_select_fusion.base_ref, s32[1,1024]{1,0:T(1,128)} %bitcast.73, s32[1,1024]{1,0:T(1,128)} %bitcast.69, bf16[176,1024]{1,0:T(8,128)(2,1)} %get-tuple-element.47.q_ref, f32[1,1024]{1,0:T(1,128)} %get-tuple-element.50.rest_0_, ...), custom_call_target="tpu_custom_call" | custom-call | flops 369098752 | bytes 720896 | tf_op jit(solution)/shard_map/pallas_call | solution.py:186
  42.6 3.1 %collective-permute-start.3 = (bf16[88,1024]{1,0:T(8,128)(2,1)}, bf16[88,1024]{1,0:T(8,128)(2,1)}, u32[]{:S(2)}, u32[]{:S(2)}) collective-permute-start(bf16[88,1024]{1,0:T(8,128)(2,1)} %shard_map.120.refs_0_), channel_id=1, source_target_pairs={{0,4},{1,5},{4,0},{5,1},{2,6},{3,7},{6,2},{7,3},{8,12},{9,13},{12,... | collective-permute-start | bytes 540680 | tf_op jit(solution)/shard_map/ppermute | solution.py:338
  46.4 3.9 %shard_map.122.refs_5_.refs_8_ = bf16[88,1024]{1,0:T(8,128)(2,1)} custom-call(s32[4]{0:T(128)} %bitcast.78, s32[4]{0:T(128)} %bitcast.81, s32[2]{0:T(128)} %and_select_fusion.base_ref, s32[1,1024]{1,0:T(1,128)} %bitcast.74, s32[1,1024]{1,0:T(1,128)} %bitcast.70, bf16[176,1024]{1,0:T(8,128)(2,1)} %get-tuple-element.47.q_ref, ...), custom_call_target="tpu_custom_call" | custom-call | flops 369098752 | bytes 720896 | tf_op jit(solution)/shard_map/pallas_call | solution.py:186
  50.3 1.6 collective-permute-start.13
  52.0 1.6 collective-permute-start.2
  53.6 2.1 %copy-done.7 = bf16[1408,1408]{1,0:T(8,128)(2,1)S(1)} copy-done((bf16[1408,1408]{1,0:T(8,128)(2,1)S(1)}, bf16[1408,1408]{1,0:T(8,128)(2,1)}, u32[]{:S(2)}) %copy-start.7) | copy-done | bytes 3964952
  55.7 1.6 copy-done.32
  57.3 1.6 copy-done.33
  58.9 1.4 shard_map.123
  61.0 1.3 collective-permute-start.5
  63.0 1.5 collective-permute-start.15
  64.6 5.0 %collective-permute-start.12 = (bf16[88,1024]{1,0:T(8,128)(2,1)}, bf16[88,1024]{1,0:T(8,128)(2,1)S(1)}, u32[]{:S(2)}, u32[]{:S(2)}) collective-permute-start(bf16[88,1024]{1,0:T(8,128)(2,1)} %shard_map.122.refs_5_.refs_8_), channel_id=1, source_target_pairs={{0,2},{1,3},{2,0},{3,1},{4,6},{5,7},{6,4},{7,5},{8,10},{9,11},{10,... | collective-permute-start | bytes 540680 | tf_op jit(solution)/shard_map/ppermute | solution.py:338
  70.2 4.5 %collective-permute-done.15.refs_1_ = bf16[88,1024]{1,0:T(8,128)(2,1)S(1)} collective-permute-done((bf16[88,1024]{1,0:T(8,128)(2,1)S(1)}, bf16[88,1024]{1,0:T(8,128)(2,1)S(1)}, u32[]{:S(2)}, u32[]{:S(2)}) %collective-permute-start.15) | collective-permute-done | bytes 180256 | tf_op jit(solution)/shard_map/ppermute | solution.py:338
  75.4 1.5 collective-permute-done.12.refs_9_
  78.8 1.0 copy-done.10
  79.8 5.1 %shard_map.125 = (bf16[128,1408]{1,0:T(8,128)(2,1)S(1)}, bf16[128,1408]{1,0:T(8,128)(2,1)S(1)}) custom-call(s32[2]{0:T(128)S(1)} %pad_add_fusion.refs_3_.place_ref, bf16[88,1024]{1,0:T(8,128)(2,1)S(1)} %copy-done.8, bf16[88,1024]{1,0:T(8,128)(2,1)S(1)} %collective-permute-done.2.refs_1_, bf16[88,1024]{1,0:T(8,128)(2,1)} %collective-permute-done.3.refs_2_, ...), custom_call_target="tpu_custom_call" | custom-call | flops 2122317824 | bytes 11173888 | tf_op jit(solution)/shard_map/pallas_call | solution.py:285
  85.2 1.4 collective-permute-done.20.refs_1_
  87.5 2.6 %collective-permute-start.22 = (bf16[128,1408]{1,0:T(8,128)(2,1)}, bf16[128,1408]{1,0:T(8,128)(2,1)}, u32[]{:S(2)}, u32[]{:S(2)}) collective-permute-start(bf16[128,1408]{1,0:T(8,128)(2,1)} %shard_map.126), channel_id=1, source_target_pairs={{0,2},{1,3},{6,4},{7,5},{8,10},{9,11},{14,12},{15,13},{16,18},{17,... | collective-permute-start | bytes 1081352 | tf_op jit(solution)/shard_map/ppermute | solution.py:338
  90.0 5.9 %shard_map.127 = (bf16[128,1408]{1,0:T(8,128)(2,1)S(1)}, bf16[128,1408]{1,0:T(8,128)(2,1)}) custom-call(s32[2]{0:T(128)S(1)} %pad_add_fusion.refs_3_.place_ref, bf16[88,1024]{1,0:T(8,128)(2,1)S(1)} %copy-done.8, bf16[88,1024]{1,0:T(8,128)(2,1)S(1)} %collective-permute-done.2.refs_1_, bf16[88,1024]{1,0:T(8,128)(2,1)} %collective-permute-done.3.refs_2_, ...), custom_call_target="tpu_custom_call" | custom-call | flops 2122317824 | bytes 11173888 | tf_op jit(solution)/shard_map/pallas_call | solution.py:285
  96.8 5.9 %shard_map.128 = (bf16[128,1408]{1,0:T(8,128)(2,1)S(1)}, bf16[128,1408]{1,0:T(8,128)(2,1)}) custom-call(s32[2]{0:T(128)S(1)} %pad_add_fusion.refs_3_.place_ref, bf16[88,1024]{1,0:T(8,128)(2,1)S(1)} %copy-done.8, bf16[88,1024]{1,0:T(8,128)(2,1)S(1)} %collective-permute-done.2.refs_1_, bf16[88,1024]{1,0:T(8,128)(2,1)} %collective-permute-done.3.refs_2_, ...), custom_call_target="tpu_custom_call" | custom-call | flops 2122317824 | bytes 11173888 | tf_op jit(solution)/shard_map/pallas_call | solution.py:285
  104.2 1.0 collective-permute-start.24
  106.2 1.2 shard_map.129
  107.4 1.4 collective-permute-start.27
  109.8 1.1 shard_map.131
  110.9 1.6 collective-permute-start.26
  112.5 2.1 %copy-done.1 = bf16[1408,1408]{1,0:T(8,128)(2,1)S(1)} copy-done((bf16[1408,1408]{1,0:T(8,128)(2,1)S(1)}, bf16[1408,1408]{1,0:T(8,128)(2,1)}, u32[]{:S(2)}) %copy-start.1) | copy-done | bytes 3964952
  114.7 1.6 copy-done.6
  124.6 5.2 %shard_map.130 = (bf16[128,1408]{1,0:T(8,128)(2,1)S(1)}, bf16[128,1408]{1,0:T(8,128)(2,1)S(1)}, bf16[128,1408]{1,0:T(8,128)(2,1)S(1)}) custom-call(s32[2]{0:T(128)S(1)} %pad_add_fusion.refs_3_.place_ref, bf16[88,1024]{1,0:T(8,128)(2,1)S(1)} %copy-done.8, bf16[88,1024]{1,0:T(8,128)(2,1)S(1)} %copy-done.13, bf16[88,1024]{1,0:T(8,128)(2,1)} %collective-permute-done.3.refs_2_, ...), custom_call_target="tpu_custom_call" | custom-call | flops 2122317824 | bytes 11173888 | tf_op jit(solution)/shard_map/pallas_call | solution.py:285
  130.5 1.0 collective-permute-done.23
  132.0 1.4 collective-permute-start.29
  134.2 17.0 %collective-permute-done.29 = bf16[32,5632]{1,0:T(8,128)(2,1)S(1)} collective-permute-done((bf16[32,5632]{1,0:T(8,128)(2,1)S(1)}, bf16[32,5632]{1,0:T(8,128)(2,1)S(1)}, u32[]{:S(2)}, u32[]{:S(2)}) %collective-permute-start.29) | collective-permute-done | bytes 360480 | tf_op jit(solution)/shard_map/ppermute | solution.py:338
  151.8 1.3 collective-permute-start.35
  153.8 1.6 collective-permute-done.31
  155.5 3.9 %convolution_convert_fusion = bf16[192,512]{1,0:T(8,128)(2,1)S(1)} fusion(bf16[192,5632]{1,0:T(8,128)(2,1)S(1)} %constant_dynamic-update-slice_fusion, bf16[5632,512]{1,0:T(8,128)(2,1)} %param.24), kind=kOutput, calls=%fused_computation.8 | convolution fusion | flops 1107394560 | bytes 8126464 | tf_op jit(solution)/shard_map/dot_general | solution.py:489
  159.4 4.6 %collective-permute-done.35.refs_1_ = bf16[32,5632]{1,0:T(8,128)(2,1)S(1)} collective-permute-done((bf16[32,5632]{1,0:T(8,128)(2,1)S(1)}, bf16[32,5632]{1,0:T(8,128)(2,1)S(1)}, u32[]{:S(2)}, u32[]{:S(2)}) %collective-permute-start.35) | collective-permute-done | bytes 360480 | tf_op jit(solution)/shard_map/ppermute | solution.py:338
  165.1 4.1 %collective-permute-start.38 = (bf16[192,512]{1,0:T(8,128)(2,1)S(1)}, bf16[192,512]{1,0:T(8,128)(2,1)S(1)}, u32[]{:S(2)}, u32[]{:S(2)}) collective-permute-start(bf16[192,512]{1,0:T(8,128)(2,1)S(1)} %convolution_convert_fusion), channel_id=1, source_target_pairs={{0,16},{8,24},{16,0},{24,8},{1,17},{9,25},{17,1},{25,9},{2,18},{10... | collective-permute-start | bytes 589832 | tf_op jit(solution)/shard_map/ppermute | solution.py:506
  169.2 1.5 collective-permute-start.33
  170.7 3.7 %convolution_convert_fusion.1 = bf16[64,512]{1,0:T(8,128)(2,1)S(1)} fusion(bf16[5632,512]{1,0:T(8,128)(2,1)} %param.24, bf16[32,5632]{1,0:T(8,128)(2,1)S(1)} %collective-permute-done.36, bf16[32,5632]{1,0:T(8,128)(2,1)S(1)} %shard_map.132), kind=kOutput, calls=%fused_computation.10 | convolution fusion | flops 370573312 | bytes 6553600 | tf_op jit(solution)/shard_map/dot_general | solution.py:489
  174.4 2.0 %collective-permute-start.41 = (bf16[64,512]{1,0:T(8,128)(2,1)S(1)}, bf16[64,512]{1,0:T(8,128)(2,1)S(1)}, u32[]{:S(2)}, u32[]{:S(2)}) collective-permute-start(bf16[64,512]{1,0:T(8,128)(2,1)S(1)} %convolution_convert_fusion.1), channel_id=1, source_target_pairs={{0,16},{8,24},{16,0},{24,8},{1,17},{9,25},{17,1},{25,9},{2,18},{10... | collective-permute-start | bytes 196616 | tf_op jit(solution)/shard_map/ppermute | solution.py:506
  176.5 1.5 collective-permute-start.39
  178.0 2.6 %collective-permute-done.33 = bf16[192,512]{1,0:T(8,128)(2,1)S(1)} collective-permute-done((bf16[192,512]{1,0:T(8,128)(2,1)S(1)}, bf16[192,512]{1,0:T(8,128)(2,1)S(1)}, u32[]{:S(2)}, u32[]{:S(2)}) %collective-permute-start.33) | collective-permute-done | bytes 196640 | tf_op jit(solution)/shard_map/ppermute | solution.py:506
  183.6 1.0 fusion.6
  (191 shorter events, 29.4 us)
Async XLA Ops:
  9.2 18.6 %collective-permute-start = (bf16[176,1024]{1,0:T(8,128)(2,1)}, bf16[176,1024]{1,0:T(8,128)(2,1)S(1)}, u32[]{:S(2)}, u32[]{:S(2)}) collective-permute-start(bf16[176,1024]{1,0:T(8,128)(2,1)} %get-tuple-element.48.rest_0_), channel_id=1, source_target_pairs={{0,8},{8,0},{16,24},{24,16},{1,9},{9,1},{17,25},{25,17},{2,10},{10... | collective-permute-start | bytes 1081352 | tf_op jit(solution)/shard_map/ppermute | solution.py:366
  12.1 17.0 %collective-permute-start.10 = (bf16[176,1024]{1,0:T(8,128)(2,1)}, bf16[176,1024]{1,0:T(8,128)(2,1)S(1)}, u32[]{:S(2)}, u32[]{:S(2)}) collective-permute-start(bf16[176,1024]{1,0:T(8,128)(2,1)} %get-tuple-element.49.rest_1_), channel_id=1, source_target_pairs={{0,8},{8,0},{16,24},{24,16},{1,9},{9,1},{17,25},{25,17},{2,10},{10... | collective-permute-start | bytes 1081352 | tf_op jit(solution)/shard_map/ppermute | solution.py:366
  27.8 24.1 %copy-start.38 = (f32[1408]{0:T(1024)S(1)}, f32[1408]{0:T(1024)}, u32[]{:S(2)}) copy-start(f32[1408]{0:T(1024)} %param.21) | copy-start | bytes 16900
  27.8 10.1 %collective-permute-start.1 = (bf16[176,1024]{1,0:T(8,128)(2,1)S(1)}, bf16[176,1024]{1,0:T(8,128)(2,1)S(1)}, u32[]{:S(2)}, u32[]{:S(2)}) collective-permute-start(bf16[176,1024]{1,0:T(8,128)(2,1)S(1)} %collective-permute-done.rest_3_), channel_id=1, source_target_pairs={{0,16},{24,8},{1,17},{25,9},{2,18},{26,10},{3,19},{27,11},{4,20},{... | collective-permute-start | bytes 1081352 | tf_op jit(solution)/shard_map/ppermute | solution.py:372
  29.2 16.5 %collective-permute-start.11 = (bf16[176,1024]{1,0:T(8,128)(2,1)S(1)}, bf16[176,1024]{1,0:T(8,128)(2,1)S(1)}, u32[]{:S(2)}, u32[]{:S(2)}) collective-permute-start(bf16[176,1024]{1,0:T(8,128)(2,1)S(1)} %collective-permute-done.10.rest_3_), channel_id=1, source_target_pairs={{0,16},{24,8},{1,17},{25,9},{2,18},{26,10},{3,19},{27,11},{4,20},{... | collective-permute-start | bytes 1081352 | tf_op jit(solution)/shard_map/ppermute | solution.py:372
  42.6 17.8 %collective-permute-start.3 = (bf16[88,1024]{1,0:T(8,128)(2,1)}, bf16[88,1024]{1,0:T(8,128)(2,1)}, u32[]{:S(2)}, u32[]{:S(2)}) collective-permute-start(bf16[88,1024]{1,0:T(8,128)(2,1)} %shard_map.120.refs_0_), channel_id=1, source_target_pairs={{0,4},{1,5},{4,0},{5,1},{2,6},{3,7},{6,2},{7,3},{8,12},{9,13},{12,... | collective-permute-start | bytes 540680 | tf_op jit(solution)/shard_map/ppermute | solution.py:338
  50.3 10.7 %collective-permute-start.13 = (bf16[88,1024]{1,0:T(8,128)(2,1)}, bf16[88,1024]{1,0:T(8,128)(2,1)S(1)}, u32[]{:S(2)}, u32[]{:S(2)}) collective-permute-start(bf16[88,1024]{1,0:T(8,128)(2,1)} %shard_map.122.refs_5_.refs_8_), channel_id=1, source_target_pairs={{0,4},{1,5},{4,0},{5,1},{2,6},{3,7},{6,2},{7,3},{8,12},{9,13},{12,... | collective-permute-start | bytes 540680 | tf_op jit(solution)/shard_map/ppermute | solution.py:338
  52.0 12.5 %collective-permute-start.2 = (bf16[88,1024]{1,0:T(8,128)(2,1)}, bf16[88,1024]{1,0:T(8,128)(2,1)S(1)}, u32[]{:S(2)}, u32[]{:S(2)}) collective-permute-start(bf16[88,1024]{1,0:T(8,128)(2,1)} %shard_map.120.refs_0_), channel_id=1, source_target_pairs={{0,2},{1,3},{2,0},{3,1},{4,6},{5,7},{6,4},{7,5},{8,10},{9,11},{10,... | collective-permute-start | bytes 540680 | tf_op jit(solution)/shard_map/ppermute | solution.py:338
  60.3 36.4 %copy-start = (bf16[1408,1408]{1,0:T(8,128)(2,1)}, bf16[1408,1408]{1,0:T(8,128)(2,1)S(1)}, u32[]{:S(2)}) copy-start(bf16[1408,1408]{1,0:T(8,128)(2,1)S(1)} %get-tuple-element.63.refs_18_) | copy-start | bytes 11894788
  60.3 36.4 %copy-start.3 = (bf16[1408,768]{1,0:T(8,128)(2,1)}, bf16[1408,768]{1,0:T(8,128)(2,1)S(1)}, u32[]{:S(2)}) copy-start(bf16[1408,768]{1,0:T(8,128)(2,1)S(1)} %get-tuple-element.64.refs_19_) | copy-start | bytes 6488068
  60.3 36.4 %copy-start.5 = (bf16[768,1408]{1,0:T(8,128)(2,1)}, bf16[768,1408]{1,0:T(8,128)(2,1)S(1)}, u32[]{:S(2)}) copy-start(bf16[768,1408]{1,0:T(8,128)(2,1)S(1)} %get-tuple-element.65.refs_20_) | copy-start | bytes 6488068
  60.3 4.3 %collective-permute-start.4 = (bf16[88,1024]{1,0:T(8,128)(2,1)S(1)}, bf16[88,1024]{1,0:T(8,128)(2,1)S(1)}, u32[]{:S(2)}, u32[]{:S(2)}) collective-permute-start(bf16[88,1024]{1,0:T(8,128)(2,1)S(1)} %copy-done.8), channel_id=1, source_target_pairs={{2,4},{3,5},{4,2},{5,3},{10,12},{11,13},{12,10},{13,11},{18,20},{1... | collective-permute-start | bytes 540680 | tf_op jit(solution)/shard_map/ppermute | solution.py:338
  61.0 8.6 %collective-permute-start.5 = (bf16[88,1024]{1,0:T(8,128)(2,1)}, bf16[88,1024]{1,0:T(8,128)(2,1)S(1)}, u32[]{:S(2)}, u32[]{:S(2)}) collective-permute-start(bf16[88,1024]{1,0:T(8,128)(2,1)} %collective-permute-done.3.refs_2_), channel_id=1, source_target_pairs={{2,0},{3,1},{4,6},{5,7},{10,8},{11,9},{12,14},{13,15},{18,16},{19,... | collective-permute-start | bytes 540680 | tf_op jit(solution)/shard_map/ppermute | solution.py:338
  62.3 7.5 %collective-permute-start.14 = (bf16[88,1024]{1,0:T(8,128)(2,1)}, bf16[88,1024]{1,0:T(8,128)(2,1)S(1)}, u32[]{:S(2)}, u32[]{:S(2)}) collective-permute-start(bf16[88,1024]{1,0:T(8,128)(2,1)} %shard_map.122.refs_5_.refs_8_), channel_id=1, source_target_pairs={{2,4},{3,5},{4,2},{5,3},{10,12},{11,13},{12,10},{13,11},{18,20},{1... | collective-permute-start | bytes 540680 | tf_op jit(solution)/shard_map/ppermute | solution.py:338
  63.0 11.7 %collective-permute-start.15 = (bf16[88,1024]{1,0:T(8,128)(2,1)S(1)}, bf16[88,1024]{1,0:T(8,128)(2,1)S(1)}, u32[]{:S(2)}, u32[]{:S(2)}) collective-permute-start(bf16[88,1024]{1,0:T(8,128)(2,1)S(1)} %collective-permute-done.13.refs_10_), channel_id=1, source_target_pairs={{2,0},{3,1},{4,6},{5,7},{10,8},{11,9},{12,14},{13,15},{18,16},{19,... | collective-permute-start | bytes 540680 | tf_op jit(solution)/shard_map/ppermute | solution.py:338
  64.5 32.2 %copy-start.12 = (bf16[88,1024]{1,0:T(8,128)(2,1)}, bf16[88,1024]{1,0:T(8,128)(2,1)S(1)}, u32[]{:S(2)}) copy-start(bf16[88,1024]{1,0:T(8,128)(2,1)S(1)} %collective-permute-done.2.refs_1_) | copy-start | bytes 540676
  64.5 10.2 %collective-permute-start.6 = (bf16[88,1024]{1,0:T(8,128)(2,1)S(1)}, bf16[88,1024]{1,0:T(8,128)(2,1)S(1)}, u32[]{:S(2)}, u32[]{:S(2)}) collective-permute-start(bf16[88,1024]{1,0:T(8,128)(2,1)S(1)} %copy-done.8), channel_id=1, source_target_pairs={{0,1},{1,0},{2,3},{3,2},{4,5},{5,4},{6,7},{7,6},{8,9},{9,8},{10,11... | collective-permute-start | bytes 540680 | tf_op jit(solution)/shard_map/ppermute | solution.py:344
  64.6 12.2 %collective-permute-start.12 = (bf16[88,1024]{1,0:T(8,128)(2,1)}, bf16[88,1024]{1,0:T(8,128)(2,1)S(1)}, u32[]{:S(2)}, u32[]{:S(2)}) collective-permute-start(bf16[88,1024]{1,0:T(8,128)(2,1)} %shard_map.122.refs_5_.refs_8_), channel_id=1, source_target_pairs={{0,2},{1,3},{2,0},{3,1},{4,6},{5,7},{6,4},{7,5},{8,10},{9,11},{10,... | collective-permute-start | bytes 540680 | tf_op jit(solution)/shard_map/ppermute | solution.py:338
  69.6 7.2 %collective-permute-start.16 = (bf16[88,1024]{1,0:T(8,128)(2,1)}, bf16[88,1024]{1,0:T(8,128)(2,1)S(1)}, u32[]{:S(2)}, u32[]{:S(2)}) collective-permute-start(bf16[88,1024]{1,0:T(8,128)(2,1)} %shard_map.122.refs_5_.refs_8_), channel_id=1, source_target_pairs={{0,1},{1,0},{2,3},{3,2},{4,5},{5,4},{6,7},{7,6},{8,9},{9,8},{10,11... | collective-permute-start | bytes 540680 | tf_op jit(solution)/shard_map/ppermute | solution.py:344
  69.8 7.6 %collective-permute-start.7 = (bf16[88,1024]{1,0:T(8,128)(2,1)S(1)}, bf16[88,1024]{1,0:T(8,128)(2,1)S(1)}, u32[]{:S(2)}, u32[]{:S(2)}) collective-permute-start(bf16[88,1024]{1,0:T(8,128)(2,1)S(1)} %collective-permute-done.2.refs_1_), channel_id=1, source_target_pairs={{0,1},{1,0},{2,3},{3,2},{4,5},{5,4},{6,7},{7,6},{8,9},{9,8},{10,11... | collective-permute-start | bytes 540680 | tf_op jit(solution)/shard_map/ppermute | solution.py:344
  74.7 2.7 %collective-permute-start.8 = (bf16[88,1024]{1,0:T(8,128)(2,1)}, bf16[88,1024]{1,0:T(8,128)(2,1)S(1)}, u32[]{:S(2)}, u32[]{:S(2)}) collective-permute-start(bf16[88,1024]{1,0:T(8,128)(2,1)} %collective-permute-done.3.refs_2_), channel_id=1, source_target_pairs={{0,1},{1,0},{2,3},{3,2},{4,5},{5,4},{6,7},{7,6},{8,9},{9,8},{10,11... | collective-permute-start | bytes 540680 | tf_op jit(solution)/shard_map/ppermute | solution.py:344
  74.8 21.9 %copy-start.14 = (bf16[88,1024]{1,0:T(8,128)(2,1)}, bf16[88,1024]{1,0:T(8,128)(2,1)S(1)}, u32[]{:S(2)}) copy-start(bf16[88,1024]{1,0:T(8,128)(2,1)S(1)} %collective-permute-done.6.refs_4_) | copy-start | bytes 540676
  74.8 3.5 %collective-permute-start.18 = (bf16[88,1024]{1,0:T(8,128)(2,1)}, bf16[88,1024]{1,0:T(8,128)(2,1)S(1)}, u32[]{:S(2)}, u32[]{:S(2)}) collective-permute-start(bf16[88,1024]{1,0:T(8,128)(2,1)} %copy-done.9), channel_id=1, source_target_pairs={{0,1},{1,0},{2,3},{3,2},{4,5},{5,4},{6,7},{7,6},{8,9},{9,8},{10,11... | collective-permute-start | bytes 540680 | tf_op jit(solution)/shard_map/ppermute | solution.py:344
  76.8 1.4 collective-permute-start.17
  76.9 1.7 collective-permute-start.9
  77.4 1.4 collective-permute-start.19
  84.9 1.7 collective-permute-start.20
  87.5 17.7 %collective-permute-start.22 = (bf16[128,1408]{1,0:T(8,128)(2,1)}, bf16[128,1408]{1,0:T(8,128)(2,1)}, u32[]{:S(2)}, u32[]{:S(2)}) collective-permute-start(bf16[128,1408]{1,0:T(8,128)(2,1)} %shard_map.126), channel_id=1, source_target_pairs={{0,2},{1,3},{6,4},{7,5},{8,10},{9,11},{14,12},{15,13},{16,18},{17,... | collective-permute-start | bytes 1081352 | tf_op jit(solution)/shard_map/ppermute | solution.py:338
  96.7 8.5 %collective-permute-start.21 = (bf16[128,1408]{1,0:T(8,128)(2,1)}, bf16[128,1408]{1,0:T(8,128)(2,1)}, u32[]{:S(2)}, u32[]{:S(2)}) collective-permute-start(bf16[128,1408]{1,0:T(8,128)(2,1)} %get-tuple-element.70), channel_id=1, source_target_pairs={{0,1},{1,0},{2,3},{3,2},{4,5},{5,4},{6,7},{7,6},{8,9},{9,8},{10,11... | collective-permute-start | bytes 1081352 | tf_op jit(solution)/shard_map/ppermute | solution.py:344
  103.4 5.4 %collective-permute-start.25 = (bf16[128,1408]{1,0:T(8,128)(2,1)}, bf16[128,1408]{1,0:T(8,128)(2,1)}, u32[]{:S(2)}, u32[]{:S(2)}) collective-permute-start(bf16[128,1408]{1,0:T(8,128)(2,1)} %get-tuple-element.78), channel_id=1, source_target_pairs={{0,1},{1,0},{2,3},{3,2},{4,5},{5,4},{6,7},{7,6},{8,9},{9,8},{10,11... | collective-permute-start | bytes 1081352 | tf_op jit(solution)/shard_map/ppermute | solution.py:344
  104.2 25.8 %collective-permute-start.24 = (bf16[128,1408]{1,0:T(8,128)(2,1)}, bf16[128,1408]{1,0:T(8,128)(2,1)S(1)}, u32[]{:S(2)}, u32[]{:S(2)}) collective-permute-start(bf16[128,1408]{1,0:T(8,128)(2,1)} %shard_map.126), channel_id=1, source_target_pairs={{2,4},{3,5},{4,2},{5,3},{10,12},{11,13},{12,10},{13,11},{18,20},{1... | collective-permute-start | bytes 1081352 | tf_op jit(solution)/shard_map/ppermute | solution.py:338
  107.4 23.1 %collective-permute-start.27 = (bf16[128,1408]{1,0:T(8,128)(2,1)S(1)}, bf16[128,1408]{1,0:T(8,128)(2,1)S(1)}, u32[]{:S(2)}, u32[]{:S(2)}) collective-permute-start(bf16[128,1408]{1,0:T(8,128)(2,1)S(1)} %shard_map.129), channel_id=1, source_target_pairs={{0,4},{1,5},{4,0},{5,1},{2,6},{3,7},{6,2},{7,3},{8,12},{9,13},{12,... | collective-permute-start | bytes 1081352 | tf_op jit(solution)/shard_map/ppermute | solution.py:338
  110.9 19.6 %collective-permute-start.26 = (bf16[128,1408]{1,0:T(8,128)(2,1)S(1)}, bf16[128,1408]{1,0:T(8,128)(2,1)S(1)}, u32[]{:S(2)}, u32[]{:S(2)}) collective-permute-start(bf16[128,1408]{1,0:T(8,128)(2,1)S(1)} %shard_map.131), channel_id=1, source_target_pairs={{0,2},{1,3},{2,0},{3,1},{4,6},{5,7},{6,4},{7,5},{8,10},{9,11},{10,... | collective-permute-start | bytes 1081352 | tf_op jit(solution)/shard_map/ppermute | solution.py:338
  129.7 1.7 collective-permute-start.23
  132.0 19.1 %collective-permute-start.29 = (bf16[32,5632]{1,0:T(8,128)(2,1)S(1)}, bf16[32,5632]{1,0:T(8,128)(2,1)S(1)}, u32[]{:S(2)}, u32[]{:S(2)}) collective-permute-start(bf16[32,5632]{1,0:T(8,128)(2,1)S(1)} %reshape.271), channel_id=1, source_target_pairs={{0,4},{1,5},{4,0},{5,1},{2,6},{3,7},{6,2},{7,3},{8,12},{9,13},{12,... | collective-permute-start | bytes 1081352 | tf_op jit(solution)/shard_map/ppermute | solution.py:338
  133.4 19.8 %collective-permute-start.28 = (bf16[32,5632]{1,0:T(8,128)(2,1)S(1)}, bf16[32,5632]{1,0:T(8,128)(2,1)S(1)}, u32[]{:S(2)}, u32[]{:S(2)}) collective-permute-start(bf16[32,5632]{1,0:T(8,128)(2,1)S(1)} %reshape.271), channel_id=1, source_target_pairs={{0,2},{1,3},{2,0},{3,1},{4,6},{5,7},{6,4},{7,5},{8,10},{9,11},{10,... | collective-permute-start | bytes 1081352 | tf_op jit(solution)/shard_map/ppermute | solution.py:338
  134.1 19.6 %collective-permute-start.30 = (bf16[32,5632]{1,0:T(8,128)(2,1)S(1)}, bf16[32,5632]{1,0:T(8,128)(2,1)S(1)}, u32[]{:S(2)}, u32[]{:S(2)}) collective-permute-start(bf16[32,5632]{1,0:T(8,128)(2,1)S(1)} %reshape.271), channel_id=1, source_target_pairs={{0,1},{1,0},{2,3},{3,2},{4,5},{5,4},{6,7},{7,6},{8,9},{9,8},{10,11... | collective-permute-start | bytes 1081352 | tf_op jit(solution)/shard_map/ppermute | solution.py:344
  151.2 8.2 %collective-permute-start.34 = (bf16[32,5632]{1,0:T(8,128)(2,1)S(1)}, bf16[32,5632]{1,0:T(8,128)(2,1)S(1)}, u32[]{:S(2)}, u32[]{:S(2)}) collective-permute-start(bf16[32,5632]{1,0:T(8,128)(2,1)S(1)} %reshape.271), channel_id=1, source_target_pairs={{2,4},{3,5},{4,2},{5,3},{10,12},{11,13},{12,10},{13,11},{18,20},{1... | collective-permute-start | bytes 1081352 | tf_op jit(solution)/shard_map/ppermute | solution.py:338
  151.8 12.2 %collective-permute-start.35 = (bf16[32,5632]{1,0:T(8,128)(2,1)S(1)}, bf16[32,5632]{1,0:T(8,128)(2,1)S(1)}, u32[]{:S(2)}, u32[]{:S(2)}) collective-permute-start(bf16[32,5632]{1,0:T(8,128)(2,1)S(1)} %collective-permute-done.29), channel_id=1, source_target_pairs={{2,0},{3,1},{4,6},{5,7},{10,8},{11,9},{12,14},{13,15},{18,16},{19,... | collective-permute-start | bytes 1081352 | tf_op jit(solution)/shard_map/ppermute | solution.py:338
  153.1 2.3 %collective-permute-start.32 = (bf16[32,5632]{1,0:T(8,128)(2,1)S(1)}, bf16[32,5632]{1,0:T(8,128)(2,1)S(1)}, u32[]{:S(2)}, u32[]{:S(2)}) collective-permute-start(bf16[32,5632]{1,0:T(8,128)(2,1)S(1)} %collective-permute-done.29), channel_id=1, source_target_pairs={{0,1},{1,0},{2,3},{3,2},{4,5},{5,4},{6,7},{7,6},{8,9},{9,8},{10,11... | collective-permute-start | bytes 1081352 | tf_op jit(solution)/shard_map/ppermute | solution.py:344
  153.2 2.2 %collective-permute-start.31 = (bf16[32,5632]{1,0:T(8,128)(2,1)S(1)}, bf16[32,5632]{1,0:T(8,128)(2,1)S(1)}, u32[]{:S(2)}, u32[]{:S(2)}) collective-permute-start(bf16[32,5632]{1,0:T(8,128)(2,1)S(1)} %collective-permute-done.28), channel_id=1, source_target_pairs={{0,1},{1,0},{2,3},{3,2},{4,5},{5,4},{6,7},{7,6},{8,9},{9,8},{10,11... | collective-permute-start | bytes 1081352 | tf_op jit(solution)/shard_map/ppermute | solution.py:344
  164.1 6.6 %collective-permute-start.36 = (bf16[32,5632]{1,0:T(8,128)(2,1)S(1)}, bf16[32,5632]{1,0:T(8,128)(2,1)S(1)}, u32[]{:S(2)}, u32[]{:S(2)}) collective-permute-start(bf16[32,5632]{1,0:T(8,128)(2,1)S(1)} %shard_map.132), channel_id=1, source_target_pairs={{0,1},{1,0},{2,3},{3,2},{4,5},{5,4},{6,7},{7,6},{8,9},{9,8},{10,11... | collective-permute-start | bytes 1081352 | tf_op jit(solution)/shard_map/ppermute | solution.py:344
  165.1 11.4 %collective-permute-start.38 = (bf16[192,512]{1,0:T(8,128)(2,1)S(1)}, bf16[192,512]{1,0:T(8,128)(2,1)S(1)}, u32[]{:S(2)}, u32[]{:S(2)}) collective-permute-start(bf16[192,512]{1,0:T(8,128)(2,1)S(1)} %convolution_convert_fusion), channel_id=1, source_target_pairs={{0,16},{8,24},{16,0},{24,8},{1,17},{9,25},{17,1},{25,9},{2,18},{10... | collective-permute-start | bytes 589832 | tf_op jit(solution)/shard_map/ppermute | solution.py:506
  169.2 8.8 %collective-permute-start.37 = (bf16[192,512]{1,0:T(8,128)(2,1)S(1)}, bf16[192,512]{1,0:T(8,128)(2,1)S(1)}, u32[]{:S(2)}, u32[]{:S(2)}) collective-permute-start(bf16[192,512]{1,0:T(8,128)(2,1)S(1)} %convolution_convert_fusion), channel_id=1, source_target_pairs={{0,8},{8,0},{16,24},{24,16},{1,9},{9,1},{17,25},{25,17},{2,10},{10... | collective-permute-start | bytes 589832 | tf_op jit(solution)/shard_map/ppermute | solution.py:506
  169.2 11.5 %collective-permute-start.33 = (bf16[192,512]{1,0:T(8,128)(2,1)S(1)}, bf16[192,512]{1,0:T(8,128)(2,1)S(1)}, u32[]{:S(2)}, u32[]{:S(2)}) collective-permute-start(bf16[192,512]{1,0:T(8,128)(2,1)S(1)} %convolution_convert_fusion), channel_id=1, source_target_pairs={{0,24},{8,16},{16,8},{24,0},{1,25},{9,17},{17,9},{25,1},{2,26},{10... | collective-permute-start | bytes 589832 | tf_op jit(solution)/shard_map/ppermute | solution.py:506
  174.4 7.6 %collective-permute-start.41 = (bf16[64,512]{1,0:T(8,128)(2,1)S(1)}, bf16[64,512]{1,0:T(8,128)(2,1)S(1)}, u32[]{:S(2)}, u32[]{:S(2)}) collective-permute-start(bf16[64,512]{1,0:T(8,128)(2,1)S(1)} %convolution_convert_fusion.1), channel_id=1, source_target_pairs={{0,16},{8,24},{16,0},{24,8},{1,17},{9,25},{17,1},{25,9},{2,18},{10... | collective-permute-start | bytes 196616 | tf_op jit(solution)/shard_map/ppermute | solution.py:506
  176.5 6.1 %collective-permute-start.40 = (bf16[64,512]{1,0:T(8,128)(2,1)S(1)}, bf16[64,512]{1,0:T(8,128)(2,1)S(1)}, u32[]{:S(2)}, u32[]{:S(2)}) collective-permute-start(bf16[64,512]{1,0:T(8,128)(2,1)S(1)} %convolution_convert_fusion.1), channel_id=1, source_target_pairs={{0,8},{8,0},{16,24},{24,16},{1,9},{9,1},{17,25},{25,17},{2,10},{10... | collective-permute-start | bytes 196616 | tf_op jit(solution)/shard_map/ppermute | solution.py:506
  176.5 6.6 %collective-permute-start.39 = (bf16[64,512]{1,0:T(8,128)(2,1)S(1)}, bf16[64,512]{1,0:T(8,128)(2,1)S(1)}, u32[]{:S(2)}, u32[]{:S(2)}) collective-permute-start(bf16[64,512]{1,0:T(8,128)(2,1)S(1)} %convolution_convert_fusion.1), channel_id=1, source_target_pairs={{0,24},{8,16},{16,8},{24,0},{1,25},{9,17},{17,9},{25,1},{2,26},{10... | collective-permute-start | bytes 196616 | tf_op jit(solution)/shard_map/ppermute | solution.py:506
  (41 other events, 289.0 us)

commit v5 on v4

--- a/solution.py
+++ b/solution.py
@@ -460,10 +460,10 @@
     slots = jnp.arange(merged_rows, dtype=jnp.int32)
 
     gain_row = gain_mlp[None, :]
-    held, token = load((out_weight, up_weight, down_weight), (place, gain_row, blended[-1]))
+    held, token = load((out_weight, up_weight, down_weight), (place, gain_row, blended[0]))
     blocks = []
     for head, piece in enumerate(blended):
-        piece = gather_line(piece, token if head == heads - 1 else None)
+        piece = gather_line(piece, token if head == 0 else None)
         blocks += piece + [swap_core(block) for block in piece]
     rest = (blocks, embedded, gain_row, held)
 

time: 185 us -> 187 us (1.011); the launches traced: 185 us -> 184 us
    unnamed x99 -> x103, local copies, waits for them, and re-layouts: 23.5 us -> 24.4 us
  transfers between devices with their start and end apart: 42 -> 42, of which waited for: 15 -> 14; matrix products, arithmetic and copies ran while one was open for 7% -> 7% of each run, Pallas kernels for 23% -> 23%
where the time goes in v5:
time: 187 us; the launch traced here: 184 us
  Pallas kernels  57.5 us (31%)
  starting transfers between devices  44.7 us (24%)
  waiting for transfers between devices  42.2 us (23%)
  local copies, waits for them, and re-layouts  26.7 us (14%)
  matrix products  10.5 us (6%)
    ppermute x16, waiting for transfers between devices, along_hid(): lax.ppermute(value, 'hid', [(2 * a + core, 2 * b + core) for a, b in pair...  27.6 us
    ppermute x16, starting transfers between devices, along_hid(): lax.ppermute(value, 'hid', [(2 * a + core, 2 * b + core) for a, b in pair...  25.9 us
    unnamed x103, local copies, waits for them, and re-layouts  24.4 us
    pallas_call x4, Pallas kernels, mlp(): pl.pallas_call(functools.partial(mlp_kernel, distance), grid=(1,), in_spe...  21.9 us
    pallas_call x3, Pallas kernels, attend(): pl.pallas_call(functools.partial(attend_kernel, heads, len(states) // hea...  21.8 us
    pallas_call x1, Pallas kernels, project(): pl.pallas_call(project_kernel, grid_spec=pltpu.PrefetchScalarGridSpec(num...  9.18 us
    ppermute x6, starting transfers between devices, on_device(): lax.ppermute(projected, 'req', [(i, i ^ shift) for i in range(4)])  8.16 us
    dot_general x2, matrix products, project_merged(): jnp.dot(jnp.concatenate(blocks, axis=0), merge_weight, preferred_element_...  7.65 us
  transfers between devices with their start and end apart: 42, of which 14 were waited for; matrix products, arithmetic and copies ran while one was open for 7% of the time, Pallas kernels for 23%

profile of v5, /device:TPU:0, one launch (start us, length us, event | category | flops | bytes accessed | tf_op | source)
XLA Modules:
  0.0 184.2 jit_solution(18168920986677069581)
XLA Ops:
  0.0 9.2 %shard_map.118 = (bf16[1024,1408]{1,0:T(8,128)(2,1)}, bf16[176,1024]{1,0:T(8,128)(2,1)}, bf16[176,1024]{1,0:T(8,128)(2,1)}, bf16[176,1024]{1,0:T(8,128)(2,1)}) custom-call(s32[1]{0:T(128)} %bitcast.18.base_ref, s32[2,32]{1,0:T(2,128)} %bitcast.66, bf16[1024,1408]{1,0:T(8,128)(2,1)} %patches_ref.1, bf16[32,1408]{1,0:T(8,128)(2,1)} %row_ref.1, ...), custom_call_target="tpu_custom_call" | custom-call | flops 1522532352 | bytes 5767168 | tf_op jit(solution)/shard_map/pallas_call | solution.py:84
  9.2 2.9 %collective-permute-start = (bf16[176,1024]{1,0:T(8,128)(2,1)}, bf16[176,1024]{1,0:T(8,128)(2,1)S(1)}, u32[]{:S(2)}, u32[]{:S(2)}) collective-permute-start(bf16[176,1024]{1,0:T(8,128)(2,1)} %get-tuple-element.48.rest_0_), channel_id=1, source_target_pairs={{0,8},{8,0},{16,24},{24,16},{1,9},{9,1},{17,25},{25,17},{2,10},{10... | collective-permute-start | bytes 1081352 | tf_op jit(solution)/shard_map/ppermute | solution.py:366
  13.9 14.0 %shard_map.119 = (f32[1,1024]{1,0:T(1,128)}, f32[1,1024]{1,0:T(1,128)}, f32[88,1024]{1,0:T(8,128)}, f32[1,1024]{1,0:T(1,128)}, f32[1,1024]{1,0:T(1,128)}, /*index=5*/f32[88,1024]{1,0:T(8,128)}) custom-call(s32[4]{0:T(128)} %bitcast.76, s32[4]{0:T(128)} %bitcast.79, s32[1]{0:T(128)} %bitcast.18.base_ref, s32[1,1024]{1,0:T(1,128)} %bitcast.72, ...), custom_call_target="tpu_custom_call" | custom-call | flops 738197504 | bytes 1441792 | tf_op jit(solution)/shard_map/pallas_call | solution.py:186
  27.9 1.3 collective-permute-start.1
  29.2 3.0 %collective-permute-start.11 = (bf16[176,1024]{1,0:T(8,128)(2,1)S(1)}, bf16[176,1024]{1,0:T(8,128)(2,1)S(1)}, u32[]{:S(2)}, u32[]{:S(2)}) collective-permute-start(bf16[176,1024]{1,0:T(8,128)(2,1)S(1)} %collective-permute-done.10.rest_3_), channel_id=1, source_target_pairs={{0,16},{24,8},{1,17},{25,9},{2,18},{26,10},{3,19},{27,11},{4,20},{... | collective-permute-start | bytes 1081352 | tf_op jit(solution)/shard_map/ppermute | solution.py:372
  32.9 5.1 %collective-permute-done.1.rest_4_ = bf16[176,1024]{1,0:T(8,128)(2,1)S(1)} collective-permute-done((bf16[176,1024]{1,0:T(8,128)(2,1)S(1)}, bf16[176,1024]{1,0:T(8,128)(2,1)S(1)}, u32[]{:S(2)}, u32[]{:S(2)}) %collective-permute-start.1) | collective-permute-done | bytes 360480 | tf_op jit(solution)/shard_map/ppermute | solution.py:372
  38.7 3.9 %shard_map.120.refs_5_.refs_0_ = bf16[88,1024]{1,0:T(8,128)(2,1)} custom-call(s32[4]{0:T(128)} %bitcast.77, s32[4]{0:T(128)} %bitcast.80, s32[2]{0:T(128)} %and_select_fusion.base_ref, s32[1,1024]{1,0:T(1,128)} %bitcast.73, s32[1,1024]{1,0:T(1,128)} %bitcast.69, bf16[176,1024]{1,0:T(8,128)(2,1)} %get-tuple-element.47.q_ref, ...), custom_call_target="tpu_custom_call" | custom-call | flops 369098752 | bytes 720896 | tf_op jit(solution)/shard_map/pallas_call | solution.py:186
  42.6 3.1 %collective-permute-start.3 = (bf16[88,1024]{1,0:T(8,128)(2,1)}, bf16[88,1024]{1,0:T(8,128)(2,1)}, u32[]{:S(2)}, u32[]{:S(2)}) collective-permute-start(bf16[88,1024]{1,0:T(8,128)(2,1)} %shard_map.120.refs_5_.refs_0_), channel_id=1, source_target_pairs={{0,4},{1,5},{4,0},{5,1},{2,6},{3,7},{6,2},{7,3},{8,12},{9,13},{12,... | collective-permute-start | bytes 540680 | tf_op jit(solution)/shard_map/ppermute | solution.py:338
  46.4 3.9 %shard_map.123.refs_8_ = bf16[88,1024]{1,0:T(8,128)(2,1)} custom-call(s32[4]{0:T(128)} %bitcast.78, s32[4]{0:T(128)} %bitcast.81, s32[2]{0:T(128)} %and_select_fusion.base_ref, s32[1,1024]{1,0:T(1,128)} %bitcast.74, s32[1,1024]{1,0:T(1,128)} %bitcast.70, bf16[176,1024]{1,0:T(8,128)(2,1)} %get-tuple-element.47.q_ref, f32[1,1024]{1,0:T(1,128)} %get-tuple-element.58.rest_0_, ...), custom_call_target="tpu_custom_call" | custom-call | flops 369098752 | bytes 720896 | tf_op jit(solution)/shard_map/pallas_call | solution.py:186
  50.3 1.6 collective-permute-start.13
  52.0 1.6 collective-permute-start.2
  53.6 2.1 %copy-done.8 = bf16[1408,1408]{1,0:T(8,128)(2,1)S(1)} copy-done((bf16[1408,1408]{1,0:T(8,128)(2,1)S(1)}, bf16[1408,1408]{1,0:T(8,128)(2,1)}, u32[]{:S(2)}) %copy-start.8) | copy-done | bytes 3964952
  55.7 1.6 copy-done.34
  57.3 1.6 copy-done.35
  58.9 1.4 shard_map.121
  61.0 1.3 collective-permute-start.5
  63.1 1.5 collective-permute-start.15
  64.6 5.0 %collective-permute-start.12 = (bf16[88,1024]{1,0:T(8,128)(2,1)S(1)}, bf16[88,1024]{1,0:T(8,128)(2,1)S(1)}, u32[]{:S(2)}, u32[]{:S(2)}) collective-permute-start(bf16[88,1024]{1,0:T(8,128)(2,1)S(1)} %copy-done.9), channel_id=1, source_target_pairs={{0,2},{1,3},{2,0},{3,1},{4,6},{5,7},{6,4},{7,5},{8,10},{9,11},{10,... | collective-permute-start | bytes 540680 | tf_op jit(solution)/shard_map/ppermute | solution.py:338
  71.2 3.5 %collective-permute-done.15.refs_1_ = bf16[88,1024]{1,0:T(8,128)(2,1)S(1)} collective-permute-done((bf16[88,1024]{1,0:T(8,128)(2,1)S(1)}, bf16[88,1024]{1,0:T(8,128)(2,1)S(1)}, u32[]{:S(2)}, u32[]{:S(2)}) %collective-permute-start.15) | collective-permute-done | bytes 180256 | tf_op jit(solution)/shard_map/ppermute | solution.py:338
  75.4 1.4 collective-permute-done.12.refs_9_
  79.8 5.1 %shard_map.125 = (bf16[128,1408]{1,0:T(8,128)(2,1)S(1)}, bf16[128,1408]{1,0:T(8,128)(2,1)S(1)}) custom-call(s32[2]{0:T(128)S(1)} %pad_add_fusion.refs_3_.place_ref, bf16[88,1024]{1,0:T(8,128)(2,1)S(1)} %copy-done.7, bf16[88,1024]{1,0:T(8,128)(2,1)S(1)} %collective-permute-done.2.refs_1_, bf16[88,1024]{1,0:T(8,128)(2,1)} %collective-permute-done.3.refs_2_, ...), custom_call_target="tpu_custom_call" | custom-call | flops 2122317824 | bytes 11173888 | tf_op jit(solution)/shard_map/pallas_call | solution.py:285
  85.2 1.4 collective-permute-done.20.refs_1_
  87.5 2.4 %collective-permute-start.22 = (bf16[128,1408]{1,0:T(8,128)(2,1)}, bf16[128,1408]{1,0:T(8,128)(2,1)}, u32[]{:S(2)}, u32[]{:S(2)}) collective-permute-start(bf16[128,1408]{1,0:T(8,128)(2,1)} %shard_map.126), channel_id=1, source_target_pairs={{0,2},{1,3},{6,4},{7,5},{8,10},{9,11},{14,12},{15,13},{16,18},{17,... | collective-permute-start | bytes 1081352 | tf_op jit(solution)/shard_map/ppermute | solution.py:338
  89.9 5.8 %shard_map.127 = (bf16[128,1408]{1,0:T(8,128)(2,1)S(1)}, bf16[128,1408]{1,0:T(8,128)(2,1)}) custom-call(s32[2]{0:T(128)S(1)} %pad_add_fusion.refs_3_.place_ref, bf16[88,1024]{1,0:T(8,128)(2,1)S(1)} %copy-done.7, bf16[88,1024]{1,0:T(8,128)(2,1)S(1)} %collective-permute-done.2.refs_1_, bf16[88,1024]{1,0:T(8,128)(2,1)} %collective-permute-done.3.refs_2_, ...), custom_call_target="tpu_custom_call" | custom-call | flops 2122317824 | bytes 11173888 | tf_op jit(solution)/shard_map/pallas_call | solution.py:285
  96.5 5.9 %shard_map.128 = (bf16[128,1408]{1,0:T(8,128)(2,1)S(1)}, bf16[128,1408]{1,0:T(8,128)(2,1)}) custom-call(s32[2]{0:T(128)S(1)} %pad_add_fusion.refs_3_.place_ref, bf16[88,1024]{1,0:T(8,128)(2,1)S(1)} %copy-done.7, bf16[88,1024]{1,0:T(8,128)(2,1)S(1)} %collective-permute-done.2.refs_1_, bf16[88,1024]{1,0:T(8,128)(2,1)} %collective-permute-done.3.refs_2_, ...), custom_call_target="tpu_custom_call" | custom-call | flops 2122317824 | bytes 11173888 | tf_op jit(solution)/shard_map/pallas_call | solution.py:285
  103.9 1.0 collective-permute-start.24
  105.9 1.2 shard_map.129
  107.2 1.4 collective-permute-start.27
  109.5 1.1 shard_map.131
  110.6 1.6 collective-permute-start.26
  112.3 2.1 %copy-done.1 = bf16[1408,1408]{1,0:T(8,128)(2,1)S(1)} copy-done((bf16[1408,1408]{1,0:T(8,128)(2,1)S(1)}, bf16[1408,1408]{1,0:T(8,128)(2,1)}, u32[]{:S(2)}) %copy-start.1) | copy-done | bytes 3964952
  114.4 1.6 copy-done.6
  125.2 5.1 %shard_map.130 = (bf16[128,1408]{1,0:T(8,128)(2,1)S(1)}, bf16[128,1408]{1,0:T(8,128)(2,1)S(1)}, bf16[128,1408]{1,0:T(8,128)(2,1)S(1)}) custom-call(s32[2]{0:T(128)S(1)} %pad_add_fusion.refs_3_.place_ref, bf16[88,1024]{1,0:T(8,128)(2,1)S(1)} %copy-done.7, bf16[88,1024]{1,0:T(8,128)(2,1)S(1)} %copy-done.15, bf16[88,1024]{1,0:T(8,128)(2,1)} %collective-permute-done.3.refs_2_, ...), custom_call_target="tpu_custom_call" | custom-call | flops 2122317824 | bytes 11173888 | tf_op jit(solution)/shard_map/pallas_call | solution.py:285
  130.5 1.6 collective-permute-done.23
  132.6 1.4 collective-permute-start.29
  134.8 17.0 %collective-permute-done.29 = bf16[32,5632]{1,0:T(8,128)(2,1)S(1)} collective-permute-done((bf16[32,5632]{1,0:T(8,128)(2,1)S(1)}, bf16[32,5632]{1,0:T(8,128)(2,1)S(1)}, u32[]{:S(2)}, u32[]{:S(2)}) %collective-permute-start.29) | collective-permute-done | bytes 360480 | tf_op jit(solution)/shard_map/ppermute | solution.py:338
  152.4 1.3 collective-permute-start.35
  154.4 1.6 collective-permute-done.31
  156.1 3.9 %convolution_convert_fusion = bf16[192,512]{1,0:T(8,128)(2,1)S(1)} fusion(bf16[192,5632]{1,0:T(8,128)(2,1)S(1)} %constant_dynamic-update-slice_fusion, bf16[5632,512]{1,0:T(8,128)(2,1)} %param.24), kind=kOutput, calls=%fused_computation.8 | convolution fusion | flops 1107394560 | bytes 8126464 | tf_op jit(solution)/shard_map/dot_general | solution.py:489
  160.0 4.6 %collective-permute-done.35.refs_1_ = bf16[32,5632]{1,0:T(8,128)(2,1)S(1)} collective-permute-done((bf16[32,5632]{1,0:T(8,128)(2,1)S(1)}, bf16[32,5632]{1,0:T(8,128)(2,1)S(1)}, u32[]{:S(2)}, u32[]{:S(2)}) %collective-permute-start.35) | collective-permute-done | bytes 360480 | tf_op jit(solution)/shard_map/ppermute | solution.py:338
  165.7 1.5 collective-permute-start.38
  167.1 1.8 collective-permute-start.37
  168.9 1.4 collective-permute-start.33
  170.3 3.7 %convolution_convert_fusion.1 = bf16[64,512]{1,0:T(8,128)(2,1)S(1)} fusion(bf16[5632,512]{1,0:T(8,128)(2,1)} %param.24, bf16[32,5632]{1,0:T(8,128)(2,1)S(1)} %collective-permute-done.36, bf16[32,5632]{1,0:T(8,128)(2,1)S(1)} %shard_map.132), kind=kOutput, calls=%fused_computation.10 | convolution fusion | flops 370573312 | bytes 6553600 | tf_op jit(solution)/shard_map/dot_general | solution.py:489
  174.7 1.5 collective-permute-start.40
  176.2 1.4 collective-permute-start.39
  177.6 2.6 %collective-permute-done.33 = bf16[192,512]{1,0:T(8,128)(2,1)S(1)} collective-permute-done((bf16[192,512]{1,0:T(8,128)(2,1)S(1)}, bf16[192,512]{1,0:T(8,128)(2,1)S(1)}, u32[]{:S(2)}, u32[]{:S(2)}) %collective-permute-start.33) | collective-permute-done | bytes 196640 | tf_op jit(solution)/shard_map/ppermute | solution.py:506
  181.6 1.0 collective-permute-done.39
  (195 shorter events, 32.4 us)
Async XLA Ops:
  9.2 18.6 %collective-permute-start = (bf16[176,1024]{1,0:T(8,128)(2,1)}, bf16[176,1024]{1,0:T(8,128)(2,1)S(1)}, u32[]{:S(2)}, u32[]{:S(2)}) collective-permute-start(bf16[176,1024]{1,0:T(8,128)(2,1)} %get-tuple-element.48.rest_0_), channel_id=1, source_target_pairs={{0,8},{8,0},{16,24},{24,16},{1,9},{9,1},{17,25},{25,17},{2,10},{10... | collective-permute-start | bytes 1081352 | tf_op jit(solution)/shard_map/ppermute | solution.py:366
  12.1 17.0 %collective-permute-start.10 = (bf16[176,1024]{1,0:T(8,128)(2,1)}, bf16[176,1024]{1,0:T(8,128)(2,1)S(1)}, u32[]{:S(2)}, u32[]{:S(2)}) collective-permute-start(bf16[176,1024]{1,0:T(8,128)(2,1)} %get-tuple-element.49.rest_1_), channel_id=1, source_target_pairs={{0,8},{8,0},{16,24},{24,16},{1,9},{9,1},{17,25},{25,17},{2,10},{10... | collective-permute-start | bytes 1081352 | tf_op jit(solution)/shard_map/ppermute | solution.py:366
  27.8 24.1 %copy-start.40 = (f32[1408]{0:T(1024)S(1)}, f32[1408]{0:T(1024)}, u32[]{:S(2)}) copy-start(f32[1408]{0:T(1024)} %param.21) | copy-start | bytes 16900
  27.9 10.1 %collective-permute-start.1 = (bf16[176,1024]{1,0:T(8,128)(2,1)S(1)}, bf16[176,1024]{1,0:T(8,128)(2,1)S(1)}, u32[]{:S(2)}, u32[]{:S(2)}) collective-permute-start(bf16[176,1024]{1,0:T(8,128)(2,1)S(1)} %collective-permute-done.rest_3_), channel_id=1, source_target_pairs={{0,16},{24,8},{1,17},{25,9},{2,18},{26,10},{3,19},{27,11},{4,20},{... | collective-permute-start | bytes 1081352 | tf_op jit(solution)/shard_map/ppermute | solution.py:372
  29.2 16.5 %collective-permute-start.11 = (bf16[176,1024]{1,0:T(8,128)(2,1)S(1)}, bf16[176,1024]{1,0:T(8,128)(2,1)S(1)}, u32[]{:S(2)}, u32[]{:S(2)}) collective-permute-start(bf16[176,1024]{1,0:T(8,128)(2,1)S(1)} %collective-permute-done.10.rest_3_), channel_id=1, source_target_pairs={{0,16},{24,8},{1,17},{25,9},{2,18},{26,10},{3,19},{27,11},{4,20},{... | collective-permute-start | bytes 1081352 | tf_op jit(solution)/shard_map/ppermute | solution.py:372
  42.6 17.8 %collective-permute-start.3 = (bf16[88,1024]{1,0:T(8,128)(2,1)}, bf16[88,1024]{1,0:T(8,128)(2,1)}, u32[]{:S(2)}, u32[]{:S(2)}) collective-permute-start(bf16[88,1024]{1,0:T(8,128)(2,1)} %shard_map.120.refs_5_.refs_0_), channel_id=1, source_target_pairs={{0,4},{1,5},{4,0},{5,1},{2,6},{3,7},{6,2},{7,3},{8,12},{9,13},{12,... | collective-permute-start | bytes 540680 | tf_op jit(solution)/shard_map/ppermute | solution.py:338
  50.3 12.0 %collective-permute-start.13 = (bf16[88,1024]{1,0:T(8,128)(2,1)}, bf16[88,1024]{1,0:T(8,128)(2,1)S(1)}, u32[]{:S(2)}, u32[]{:S(2)}) collective-permute-start(bf16[88,1024]{1,0:T(8,128)(2,1)} %shard_map.123.refs_8_), channel_id=1, source_target_pairs={{0,4},{1,5},{4,0},{5,1},{2,6},{3,7},{6,2},{7,3},{8,12},{9,13},{12,... | collective-permute-start | bytes 540680 | tf_op jit(solution)/shard_map/ppermute | solution.py:338
  52.0 12.5 %collective-permute-start.2 = (bf16[88,1024]{1,0:T(8,128)(2,1)}, bf16[88,1024]{1,0:T(8,128)(2,1)S(1)}, u32[]{:S(2)}, u32[]{:S(2)}) collective-permute-start(bf16[88,1024]{1,0:T(8,128)(2,1)} %shard_map.120.refs_5_.refs_0_), channel_id=1, source_target_pairs={{0,2},{1,3},{2,0},{3,1},{4,6},{5,7},{6,4},{7,5},{8,10},{9,11},{10,... | collective-permute-start | bytes 540680 | tf_op jit(solution)/shard_map/ppermute | solution.py:338
  60.3 36.1 %copy-start = (bf16[1408,1408]{1,0:T(8,128)(2,1)}, bf16[1408,1408]{1,0:T(8,128)(2,1)S(1)}, u32[]{:S(2)}) copy-start(bf16[1408,1408]{1,0:T(8,128)(2,1)S(1)} %get-tuple-element.63.refs_18_) | copy-start | bytes 11894788
  60.3 36.1 %copy-start.3 = (bf16[1408,768]{1,0:T(8,128)(2,1)}, bf16[1408,768]{1,0:T(8,128)(2,1)S(1)}, u32[]{:S(2)}) copy-start(bf16[1408,768]{1,0:T(8,128)(2,1)S(1)} %get-tuple-element.64.refs_19_) | copy-start | bytes 6488068
  60.3 36.1 %copy-start.5 = (bf16[768,1408]{1,0:T(8,128)(2,1)}, bf16[768,1408]{1,0:T(8,128)(2,1)S(1)}, u32[]{:S(2)}) copy-start(bf16[768,1408]{1,0:T(8,128)(2,1)S(1)} %get-tuple-element.65.refs_20_) | copy-start | bytes 6488068
  60.4 4.3 %collective-permute-start.4 = (bf16[88,1024]{1,0:T(8,128)(2,1)S(1)}, bf16[88,1024]{1,0:T(8,128)(2,1)S(1)}, u32[]{:S(2)}, u32[]{:S(2)}) collective-permute-start(bf16[88,1024]{1,0:T(8,128)(2,1)S(1)} %copy-done.7), channel_id=1, source_target_pairs={{2,4},{3,5},{4,2},{5,3},{10,12},{11,13},{12,10},{13,11},{18,20},{1... | collective-permute-start | bytes 540680 | tf_op jit(solution)/shard_map/ppermute | solution.py:338
  61.0 9.6 %collective-permute-start.5 = (bf16[88,1024]{1,0:T(8,128)(2,1)}, bf16[88,1024]{1,0:T(8,128)(2,1)S(1)}, u32[]{:S(2)}, u32[]{:S(2)}) collective-permute-start(bf16[88,1024]{1,0:T(8,128)(2,1)} %collective-permute-done.3.refs_2_), channel_id=1, source_target_pairs={{2,0},{3,1},{4,6},{5,7},{10,8},{11,9},{12,14},{13,15},{18,16},{19,... | collective-permute-start | bytes 540680 | tf_op jit(solution)/shard_map/ppermute | solution.py:338
  62.4 8.3 %collective-permute-start.14 = (bf16[88,1024]{1,0:T(8,128)(2,1)S(1)}, bf16[88,1024]{1,0:T(8,128)(2,1)S(1)}, u32[]{:S(2)}, u32[]{:S(2)}) collective-permute-start(bf16[88,1024]{1,0:T(8,128)(2,1)S(1)} %copy-done.9), channel_id=1, source_target_pairs={{2,4},{3,5},{4,2},{5,3},{10,12},{11,13},{12,10},{13,11},{18,20},{1... | collective-permute-start | bytes 540680 | tf_op jit(solution)/shard_map/ppermute | solution.py:338
  63.1 11.7 %collective-permute-start.15 = (bf16[88,1024]{1,0:T(8,128)(2,1)S(1)}, bf16[88,1024]{1,0:T(8,128)(2,1)S(1)}, u32[]{:S(2)}, u32[]{:S(2)}) collective-permute-start(bf16[88,1024]{1,0:T(8,128)(2,1)S(1)} %collective-permute-done.13.refs_10_), channel_id=1, source_target_pairs={{2,0},{3,1},{4,6},{5,7},{10,8},{11,9},{12,14},{13,15},{18,16},{19,... | collective-permute-start | bytes 540680 | tf_op jit(solution)/shard_map/ppermute | solution.py:338
  64.5 31.9 %copy-start.14 = (bf16[88,1024]{1,0:T(8,128)(2,1)}, bf16[88,1024]{1,0:T(8,128)(2,1)S(1)}, u32[]{:S(2)}) copy-start(bf16[88,1024]{1,0:T(8,128)(2,1)S(1)} %collective-permute-done.2.refs_1_) | copy-start | bytes 540676
  64.6 10.3 %collective-permute-start.6 = (bf16[88,1024]{1,0:T(8,128)(2,1)S(1)}, bf16[88,1024]{1,0:T(8,128)(2,1)S(1)}, u32[]{:S(2)}, u32[]{:S(2)}) collective-permute-start(bf16[88,1024]{1,0:T(8,128)(2,1)S(1)} %copy-done.7), channel_id=1, source_target_pairs={{0,1},{1,0},{2,3},{3,2},{4,5},{5,4},{6,7},{7,6},{8,9},{9,8},{10,11... | collective-permute-start | bytes 540680 | tf_op jit(solution)/shard_map/ppermute | solution.py:344
  64.6 12.2 %collective-permute-start.12 = (bf16[88,1024]{1,0:T(8,128)(2,1)S(1)}, bf16[88,1024]{1,0:T(8,128)(2,1)S(1)}, u32[]{:S(2)}, u32[]{:S(2)}) collective-permute-start(bf16[88,1024]{1,0:T(8,128)(2,1)S(1)} %copy-done.9), channel_id=1, source_target_pairs={{0,2},{1,3},{2,0},{3,1},{4,6},{5,7},{6,4},{7,5},{8,10},{9,11},{10,... | collective-permute-start | bytes 540680 | tf_op jit(solution)/shard_map/ppermute | solution.py:338
  70.6 6.2 %collective-permute-start.16 = (bf16[88,1024]{1,0:T(8,128)(2,1)S(1)}, bf16[88,1024]{1,0:T(8,128)(2,1)S(1)}, u32[]{:S(2)}, u32[]{:S(2)}) collective-permute-start(bf16[88,1024]{1,0:T(8,128)(2,1)S(1)} %copy-done.9), channel_id=1, source_target_pairs={{0,1},{1,0},{2,3},{3,2},{4,5},{5,4},{6,7},{7,6},{8,9},{9,8},{10,11... | collective-permute-start | bytes 540680 | tf_op jit(solution)/shard_map/ppermute | solution.py:344
  70.7 6.7 %collective-permute-start.7 = (bf16[88,1024]{1,0:T(8,128)(2,1)S(1)}, bf16[88,1024]{1,0:T(8,128)(2,1)S(1)}, u32[]{:S(2)}, u32[]{:S(2)}) collective-permute-start(bf16[88,1024]{1,0:T(8,128)(2,1)S(1)} %collective-permute-done.2.refs_1_), channel_id=1, source_target_pairs={{0,1},{1,0},{2,3},{3,2},{4,5},{5,4},{6,7},{7,6},{8,9},{9,8},{10,11... | collective-permute-start | bytes 540680 | tf_op jit(solution)/shard_map/ppermute | solution.py:344
  74.8 2.7 %collective-permute-start.8 = (bf16[88,1024]{1,0:T(8,128)(2,1)}, bf16[88,1024]{1,0:T(8,128)(2,1)S(1)}, u32[]{:S(2)}, u32[]{:S(2)}) collective-permute-start(bf16[88,1024]{1,0:T(8,128)(2,1)} %collective-permute-done.3.refs_2_), channel_id=1, source_target_pairs={{0,1},{1,0},{2,3},{3,2},{4,5},{5,4},{6,7},{7,6},{8,9},{9,8},{10,11... | collective-permute-start | bytes 540680 | tf_op jit(solution)/shard_map/ppermute | solution.py:344
  74.8 21.6 %copy-start.16 = (bf16[88,1024]{1,0:T(8,128)(2,1)}, bf16[88,1024]{1,0:T(8,128)(2,1)S(1)}, u32[]{:S(2)}) copy-start(bf16[88,1024]{1,0:T(8,128)(2,1)S(1)} %collective-permute-done.6.refs_4_) | copy-start | bytes 540676
  74.8 3.4 %collective-permute-start.18 = (bf16[88,1024]{1,0:T(8,128)(2,1)}, bf16[88,1024]{1,0:T(8,128)(2,1)S(1)}, u32[]{:S(2)}, u32[]{:S(2)}) collective-permute-start(bf16[88,1024]{1,0:T(8,128)(2,1)} %copy-done.11), channel_id=1, source_target_pairs={{0,1},{1,0},{2,3},{3,2},{4,5},{5,4},{6,7},{7,6},{8,9},{9,8},{10,11... | collective-permute-start | bytes 540680 | tf_op jit(solution)/shard_map/ppermute | solution.py:344
  76.8 1.4 collective-permute-start.17
  76.9 1.7 collective-permute-start.9
  77.4 1.4 collective-permute-start.19
  84.9 1.7 collective-permute-start.20
  87.5 17.5 %collective-permute-start.22 = (bf16[128,1408]{1,0:T(8,128)(2,1)}, bf16[128,1408]{1,0:T(8,128)(2,1)}, u32[]{:S(2)}, u32[]{:S(2)}) collective-permute-start(bf16[128,1408]{1,0:T(8,128)(2,1)} %shard_map.126), channel_id=1, source_target_pairs={{0,2},{1,3},{6,4},{7,5},{8,10},{9,11},{14,12},{15,13},{16,18},{17,... | collective-permute-start | bytes 1081352 | tf_op jit(solution)/shard_map/ppermute | solution.py:338
  96.4 8.5 %collective-permute-start.21 = (bf16[128,1408]{1,0:T(8,128)(2,1)}, bf16[128,1408]{1,0:T(8,128)(2,1)}, u32[]{:S(2)}, u32[]{:S(2)}) collective-permute-start(bf16[128,1408]{1,0:T(8,128)(2,1)} %get-tuple-element.70), channel_id=1, source_target_pairs={{0,1},{1,0},{2,3},{3,2},{4,5},{5,4},{6,7},{7,6},{8,9},{9,8},{10,11... | collective-permute-start | bytes 1081352 | tf_op jit(solution)/shard_map/ppermute | solution.py:344
  103.2 5.4 %collective-permute-start.25 = (bf16[128,1408]{1,0:T(8,128)(2,1)}, bf16[128,1408]{1,0:T(8,128)(2,1)}, u32[]{:S(2)}, u32[]{:S(2)}) collective-permute-start(bf16[128,1408]{1,0:T(8,128)(2,1)} %get-tuple-element.78), channel_id=1, source_target_pairs={{0,1},{1,0},{2,3},{3,2},{4,5},{5,4},{6,7},{7,6},{8,9},{9,8},{10,11... | collective-permute-start | bytes 1081352 | tf_op jit(solution)/shard_map/ppermute | solution.py:344
  103.9 26.6 %collective-permute-start.24 = (bf16[128,1408]{1,0:T(8,128)(2,1)}, bf16[128,1408]{1,0:T(8,128)(2,1)S(1)}, u32[]{:S(2)}, u32[]{:S(2)}) collective-permute-start(bf16[128,1408]{1,0:T(8,128)(2,1)} %shard_map.126), channel_id=1, source_target_pairs={{2,4},{3,5},{4,2},{5,3},{10,12},{11,13},{12,10},{13,11},{18,20},{1... | collective-permute-start | bytes 1081352 | tf_op jit(solution)/shard_map/ppermute | solution.py:338
  107.2 23.4 %collective-permute-start.27 = (bf16[128,1408]{1,0:T(8,128)(2,1)S(1)}, bf16[128,1408]{1,0:T(8,128)(2,1)S(1)}, u32[]{:S(2)}, u32[]{:S(2)}) collective-permute-start(bf16[128,1408]{1,0:T(8,128)(2,1)S(1)} %shard_map.129), channel_id=1, source_target_pairs={{0,4},{1,5},{4,0},{5,1},{2,6},{3,7},{6,2},{7,3},{8,12},{9,13},{12,... | collective-permute-start | bytes 1081352 | tf_op jit(solution)/shard_map/ppermute | solution.py:338
  110.6 19.9 %collective-permute-start.26 = (bf16[128,1408]{1,0:T(8,128)(2,1)S(1)}, bf16[128,1408]{1,0:T(8,128)(2,1)S(1)}, u32[]{:S(2)}, u32[]{:S(2)}) collective-permute-start(bf16[128,1408]{1,0:T(8,128)(2,1)S(1)} %shard_map.131), channel_id=1, source_target_pairs={{0,2},{1,3},{2,0},{3,1},{4,6},{5,7},{6,4},{7,5},{8,10},{9,11},{10,... | collective-permute-start | bytes 1081352 | tf_op jit(solution)/shard_map/ppermute | solution.py:338
  130.4 1.7 collective-permute-start.23
  132.6 19.1 %collective-permute-start.29 = (bf16[32,5632]{1,0:T(8,128)(2,1)S(1)}, bf16[32,5632]{1,0:T(8,128)(2,1)S(1)}, u32[]{:S(2)}, u32[]{:S(2)}) collective-permute-start(bf16[32,5632]{1,0:T(8,128)(2,1)S(1)} %reshape.271), channel_id=1, source_target_pairs={{0,4},{1,5},{4,0},{5,1},{2,6},{3,7},{6,2},{7,3},{8,12},{9,13},{12,... | collective-permute-start | bytes 1081352 | tf_op jit(solution)/shard_map/ppermute | solution.py:338
  134.0 19.8 %collective-permute-start.28 = (bf16[32,5632]{1,0:T(8,128)(2,1)S(1)}, bf16[32,5632]{1,0:T(8,128)(2,1)S(1)}, u32[]{:S(2)}, u32[]{:S(2)}) collective-permute-start(bf16[32,5632]{1,0:T(8,128)(2,1)S(1)} %reshape.271), channel_id=1, source_target_pairs={{0,2},{1,3},{2,0},{3,1},{4,6},{5,7},{6,4},{7,5},{8,10},{9,11},{10,... | collective-permute-start | bytes 1081352 | tf_op jit(solution)/shard_map/ppermute | solution.py:338
  134.7 19.6 %collective-permute-start.30 = (bf16[32,5632]{1,0:T(8,128)(2,1)S(1)}, bf16[32,5632]{1,0:T(8,128)(2,1)S(1)}, u32[]{:S(2)}, u32[]{:S(2)}) collective-permute-start(bf16[32,5632]{1,0:T(8,128)(2,1)S(1)} %reshape.271), channel_id=1, source_target_pairs={{0,1},{1,0},{2,3},{3,2},{4,5},{5,4},{6,7},{7,6},{8,9},{9,8},{10,11... | collective-permute-start | bytes 1081352 | tf_op jit(solution)/shard_map/ppermute | solution.py:344
  151.8 8.2 %collective-permute-start.34 = (bf16[32,5632]{1,0:T(8,128)(2,1)S(1)}, bf16[32,5632]{1,0:T(8,128)(2,1)S(1)}, u32[]{:S(2)}, u32[]{:S(2)}) collective-permute-start(bf16[32,5632]{1,0:T(8,128)(2,1)S(1)} %reshape.271), channel_id=1, source_target_pairs={{2,4},{3,5},{4,2},{5,3},{10,12},{11,13},{12,10},{13,11},{18,20},{1... | collective-permute-start | bytes 1081352 | tf_op jit(solution)/shard_map/ppermute | solution.py:338
  152.4 12.2 %collective-permute-start.35 = (bf16[32,5632]{1,0:T(8,128)(2,1)S(1)}, bf16[32,5632]{1,0:T(8,128)(2,1)S(1)}, u32[]{:S(2)}, u32[]{:S(2)}) collective-permute-start(bf16[32,5632]{1,0:T(8,128)(2,1)S(1)} %collective-permute-done.29), channel_id=1, source_target_pairs={{2,0},{3,1},{4,6},{5,7},{10,8},{11,9},{12,14},{13,15},{18,16},{19,... | collective-permute-start | bytes 1081352 | tf_op jit(solution)/shard_map/ppermute | solution.py:338
  153.7 2.3 %collective-permute-start.32 = (bf16[32,5632]{1,0:T(8,128)(2,1)S(1)}, bf16[32,5632]{1,0:T(8,128)(2,1)S(1)}, u32[]{:S(2)}, u32[]{:S(2)}) collective-permute-start(bf16[32,5632]{1,0:T(8,128)(2,1)S(1)} %collective-permute-done.29), channel_id=1, source_target_pairs={{0,1},{1,0},{2,3},{3,2},{4,5},{5,4},{6,7},{7,6},{8,9},{9,8},{10,11... | collective-permute-start | bytes 1081352 | tf_op jit(solution)/shard_map/ppermute | solution.py:344
  153.8 2.2 %collective-permute-start.31 = (bf16[32,5632]{1,0:T(8,128)(2,1)S(1)}, bf16[32,5632]{1,0:T(8,128)(2,1)S(1)}, u32[]{:S(2)}, u32[]{:S(2)}) collective-permute-start(bf16[32,5632]{1,0:T(8,128)(2,1)S(1)} %collective-permute-done.28), channel_id=1, source_target_pairs={{0,1},{1,0},{2,3},{3,2},{4,5},{5,4},{6,7},{7,6},{8,9},{9,8},{10,11... | collective-permute-start | bytes 1081352 | tf_op jit(solution)/shard_map/ppermute | solution.py:344
  164.7 5.6 %collective-permute-start.36 = (bf16[32,5632]{1,0:T(8,128)(2,1)S(1)}, bf16[32,5632]{1,0:T(8,128)(2,1)S(1)}, u32[]{:S(2)}, u32[]{:S(2)}) collective-permute-start(bf16[32,5632]{1,0:T(8,128)(2,1)S(1)} %shard_map.132), channel_id=1, source_target_pairs={{0,1},{1,0},{2,3},{3,2},{4,5},{5,4},{6,7},{7,6},{8,9},{9,8},{10,11... | collective-permute-start | bytes 1081352 | tf_op jit(solution)/shard_map/ppermute | solution.py:344
  165.7 10.5 %collective-permute-start.38 = (bf16[192,512]{1,0:T(8,128)(2,1)S(1)}, bf16[192,512]{1,0:T(8,128)(2,1)S(1)}, u32[]{:S(2)}, u32[]{:S(2)}) collective-permute-start(bf16[192,512]{1,0:T(8,128)(2,1)S(1)} %convolution_convert_fusion), channel_id=1, source_target_pairs={{0,16},{8,24},{16,0},{24,8},{1,17},{9,25},{17,1},{25,9},{2,18},{10... | collective-permute-start | bytes 589832 | tf_op jit(solution)/shard_map/ppermute | solution.py:506
  167.1 10.5 %collective-permute-start.37 = (bf16[192,512]{1,0:T(8,128)(2,1)S(1)}, bf16[192,512]{1,0:T(8,128)(2,1)S(1)}, u32[]{:S(2)}, u32[]{:S(2)}) collective-permute-start(bf16[192,512]{1,0:T(8,128)(2,1)S(1)} %convolution_convert_fusion), channel_id=1, source_target_pairs={{0,8},{8,0},{16,24},{24,16},{1,9},{9,1},{17,25},{25,17},{2,10},{10... | collective-permute-start | bytes 589832 | tf_op jit(solution)/shard_map/ppermute | solution.py:506
  168.9 11.3 %collective-permute-start.33 = (bf16[192,512]{1,0:T(8,128)(2,1)S(1)}, bf16[192,512]{1,0:T(8,128)(2,1)S(1)}, u32[]{:S(2)}, u32[]{:S(2)}) collective-permute-start(bf16[192,512]{1,0:T(8,128)(2,1)S(1)} %convolution_convert_fusion), channel_id=1, source_target_pairs={{0,24},{8,16},{16,8},{24,0},{1,25},{9,17},{17,9},{25,1},{2,26},{10... | collective-permute-start | bytes 589832 | tf_op jit(solution)/shard_map/ppermute | solution.py:506
  174.0 7.6 %collective-permute-start.41 = (bf16[64,512]{1,0:T(8,128)(2,1)S(1)}, bf16[64,512]{1,0:T(8,128)(2,1)S(1)}, u32[]{:S(2)}, u32[]{:S(2)}) collective-permute-start(bf16[64,512]{1,0:T(8,128)(2,1)S(1)} %convolution_convert_fusion.1), channel_id=1, source_target_pairs={{0,16},{8,24},{16,0},{24,8},{1,17},{9,25},{17,1},{25,9},{2,18},{10... | collective-permute-start | bytes 196616 | tf_op jit(solution)/shard_map/ppermute | solution.py:506
  174.7 7.0 %collective-permute-start.40 = (bf16[64,512]{1,0:T(8,128)(2,1)S(1)}, bf16[64,512]{1,0:T(8,128)(2,1)S(1)}, u32[]{:S(2)}, u32[]{:S(2)}) collective-permute-start(bf16[64,512]{1,0:T(8,128)(2,1)S(1)} %convolution_convert_fusion.1), channel_id=1, source_target_pairs={{0,8},{8,0},{16,24},{24,16},{1,9},{9,1},{17,25},{25,17},{2,10},{10... | collective-permute-start | bytes 196616 | tf_op jit(solution)/shard_map/ppermute | solution.py:506
  176.2 6.4 %collective-permute-start.39 = (bf16[64,512]{1,0:T(8,128)(2,1)S(1)}, bf16[64,512]{1,0:T(8,128)(2,1)S(1)}, u32[]{:S(2)}, u32[]{:S(2)}) collective-permute-start(bf16[64,512]{1,0:T(8,128)(2,1)S(1)} %convolution_convert_fusion.1), channel_id=1, source_target_pairs={{0,24},{8,16},{16,8},{24,0},{1,25},{9,17},{17,9},{25,1},{2,26},{10... | collective-permute-start | bytes 196616 | tf_op jit(solution)/shard_map/ppermute | solution.py:506
  (43 other events, 299.7 us)
